TPU v7x, 32 devices: a whole 2x2x4 slice. The times are simulated.
32 devices in a mesh: dp: 8 (over z, y), seq: 4 (over x, core).
Axes of the slice: x: 2, y: 2, z: 4, core: 2. Of those that a mesh axis runs over, the one named last changes fastest.
Arguments:
- hidden_in: bfloat16 [32, 1024, 768], P('dp', 'seq'), may hold values from -6 to 6
- time_table: bfloat16 [1024, 128], replicated, may hold values from -6 to 6
- time_step: int32 [32], P('dp'), may hold values from 0 to 1023
- token_pos: int32 [32, 1024], P('dp', 'seq'), may hold values from 0 to 3071, as said below
- heads_weight: bfloat16 [768, 2304], P('seq'), may hold values from -0.15625 to 0.15625
- merge_weight: bfloat16 [768, 768], P('seq'), may hold values from -1.75 to 1.75
- lift_weight: bfloat16 [768, 3072], P('seq'), may hold values from -0.21875 to 0.21875
- lift_bias: bfloat16 [3072], P('seq'), may hold values from -3 to 3
- drop_weight: bfloat16 [3072, 768], P('seq'), may hold values from -0.109375 to 0.109375
- drop_bias: bfloat16 [768], P('seq'), may hold values from -3 to 3
- modulate_weight: bfloat16 [4608, 128], P('seq'), may hold values from -0.5 to 0.5
- modulate_bias: bfloat16 [4608], P('seq'), may hold values from -3 to 3
- first_gain: bfloat16 [768], P('seq'), may hold values from 0.099609375 to 1.8984375
- second_gain: bfloat16 [768], P('seq'), may hold values from 0.099609375 to 1.8984375
- out_grad: bfloat16 [32, 1024, 768], P('dp', 'seq'), may hold values from -6 to 6
Outputs:
- block_out: bfloat16 [32, 1024, 768], P('dp', 'seq')
- input_grad: bfloat16 [32, 1024, 768], P('dp', 'seq')
- heads_grad: float32 [768, 2304], P('seq')
- merge_grad: float32 [768, 768], P('seq')
- lift_grad: float32 [768, 3072], P('seq')
- liftbias_grad: float32 [3072], P('seq')
- drop_grad: float32 [3072, 768], P('seq')
- dropbias_grad: float32 [768], P('seq')
- modulate_grad: float32 [4608, 128], P('seq')
- modulatebias_grad: float32 [4608], P('seq')
- firstgain_grad: float32 [768], P('seq')
- secondgain_grad: float32 [768], P('seq')
- table_grad: float32 [1024, 128], P('seq')
Inputs may be any that keep to these rules, and one draw needn't show every extreme that they name: `token_pos`: positions count up by one along a row and start again at 0 at each separator token; in every aligned group of 4 rows one row holds no separator; such a row in the first group starts at 2048, such a row in the second group starts at 0.
All inputs are finite; a program needn't handle non-finite values.
Results may differ from a plain program's by a relative error of at most 0.017.
The roundings to bfloat16 on the way count: a program that leaves them out, or rounds other values in their place, can miss the bound.
Values may be sent and summed in bfloat16 or wider, within the bound.
No kernel may reach another device: no remote copies, remote signals or barrier semaphores. Data moves between devices by JAX's collectives and lax.ppermute only.
A program may use at most 320 MiB of HBM per device.

v0:
```python
from functools import partial
import math

import jax
import jax.numpy as jnp
from jax import lax
from jax.sharding import PartitionSpec as P

HEADS = 12


EPSILON = 1e-05


def rotate_half(values):
    middle = values.shape[-1] // 2
    return jnp.concatenate([-values[..., middle:], values[..., :middle]], axis=-1)


def rotate(values, cosine, sine):
    return values * cosine + rotate_half(values) * sine


def unrotate(values, cosine, sine):
    return values * cosine - rotate_half(values * sine)


def norm_forward(values, gain):
    center = values - jnp.mean(values, axis=-1, keepdims=True)
    inverse = lax.rsqrt(jnp.mean(center * center, axis=-1, keepdims=True) + EPSILON)
    unit = center * inverse
    return (unit, inverse, unit * gain)


def norm_backward(normed_grad, unit, inverse, gain):
    unit_grad = normed_grad * gain
    first = jnp.mean(unit_grad, axis=-1, keepdims=True)
    second = jnp.mean(unit_grad * unit, axis=-1, keepdims=True)
    return inverse * (unit_grad - first - unit * second)


def grouping(seqs, span):
    group = 1
    while group * span < 512 and seqs % (group * 2) == 0:
        group = group * 2
    return group


def shards(
    hidden_in,
    time_table,
    time_step,
    token_pos,
    heads_weight,
    merge_weight,
    lift_weight,
    lift_bias,
    drop_weight,
    drop_bias,
    modulate_weight,
    modulate_bias,
    first_gain,
    second_gain,
    out_grad,
):
    float_type = jnp.float32
    low_type = jnp.bfloat16
    position_count = lax.axis_size("seq")
    hidden_rows, upstream_rows, places_rows = (hidden_in, out_grad, token_pos)
    seqs, span, width = hidden_rows.shape
    length = span * position_count
    head_width = width // HEADS
    scale = 1.0 / math.sqrt(head_width)
    gathered = (
        lax.all_gather(heads_weight, "seq", axis=0, tiled=True),
        lax.all_gather(merge_weight, "seq", axis=0, tiled=True),
        lax.all_gather(lift_weight, "seq", axis=0, tiled=True),
        lax.all_gather(lift_bias, "seq", axis=0, tiled=True),
        lax.all_gather(drop_weight, "seq", axis=0, tiled=True),
        lax.all_gather(drop_bias, "seq", axis=0, tiled=True),
        lax.all_gather(modulate_weight, "seq", axis=0, tiled=True),
        lax.all_gather(modulate_bias, "seq", axis=0, tiled=True),
        lax.all_gather(first_gain, "seq", axis=0, tiled=True),
        lax.all_gather(second_gain, "seq", axis=0, tiled=True),
    )
    w_heads, w_merge, w_lift, b_lift, w_drop, b_drop, w_mod, b_mod, gain_one, gain_two = gathered
    gain_one = gain_one.astype(float_type)
    gain_two = gain_two.astype(float_type)
    table_rows = time_table.shape[0]
    choose = (time_step[:, None] == jnp.arange(table_rows, dtype=jnp.int32)[None, :]).astype(
        low_type
    )
    conds = jnp.dot(choose, time_table, preferred_element_type=float_type)
    modulation = lax.dot_general(
        conds.astype(low_type), w_mod, (((1,), (1,)), ((), ())), preferred_element_type=float_type
    ) + b_mod.astype(float_type)
    pieces = [piece[:, None, :] for piece in jnp.split(modulation, 6, axis=-1)]
    shift_a, scale_a, gate_a, shift_b, scale_b, gate_b = pieces
    positions = places_rows.astype(float_type)
    freqs = 10000.0 ** (-jnp.arange(0, head_width, 2, dtype=float_type) / head_width)
    angles = positions[..., None] * freqs
    angles = jnp.concatenate([angles, angles], axis=-1)
    cosine = jnp.cos(angles)[:, :, None, :]
    sine = jnp.sin(angles)[:, :, None, :]
    head_layout = (seqs, span, HEADS, head_width)
    inputs = hidden_rows.astype(float_type)
    unit_one, inverse_one, normed_one = norm_forward(inputs, gain_one)
    adapted_one = (normed_one * (1.0 + scale_a) + shift_a).astype(low_type)
    projected = jnp.einsum("scd,de->sce", adapted_one, w_heads, preferred_element_type=float_type)
    query_raw, key_raw, value_raw = jnp.split(projected, 3, axis=-1)
    query = rotate(query_raw.reshape(head_layout), cosine, sine).astype(low_type)
    keys_local = (
        rotate(key_raw.reshape(head_layout), cosine, sine)
        .astype(low_type)
        .reshape(seqs, span, width)
    )
    values_local = value_raw.astype(low_type)
    keys_all, values_all = (
        lax.all_gather(keys_local, "seq", axis=1, tiled=True),
        lax.all_gather(values_local, "seq", axis=1, tiled=True),
    )
    group = grouping(seqs, span)
    blocks = seqs // group

    def split_groups(array):
        return array.reshape((blocks, group) + array.shape[1:])

    def attend(block):
        query_b, keys_b, values_b = block
        keys_h = keys_b.reshape(group, length, HEADS, head_width)
        values_h = values_b.reshape(group, length, HEADS, head_width)
        scores = (
            jnp.einsum("gqhd,gkhd->ghqk", query_b, keys_h, preferred_element_type=float_type)
            * scale
        )
        peak = jnp.max(scores, axis=-1, keepdims=True)
        expos = jnp.exp(scores - peak)
        totals = jnp.sum(expos, axis=-1, keepdims=True)
        probs = (expos / totals).astype(low_type)
        mixed_b = jnp.einsum("ghqk,gkhd->gqhd", probs, values_h, preferred_element_type=float_type)
        return (mixed_b, peak[..., 0] + jnp.log(totals[..., 0]))

    mixed, logsum = lax.map(
        attend, (split_groups(query), split_groups(keys_all), split_groups(values_all))
    )
    mixed_low = mixed.reshape(seqs, span, width).astype(low_type)
    branch = jnp.einsum("scd,de->sce", mixed_low, w_merge, preferred_element_type=float_type)
    middle = inputs + gate_a * branch
    unit_two, inverse_two, normed_two = norm_forward(middle, gain_two)
    adapted_two = (normed_two * (1.0 + scale_b) + shift_b).astype(low_type)
    upper = jnp.einsum(
        "scd,df->scf", adapted_two, w_lift, preferred_element_type=float_type
    ) + b_lift.astype(float_type)
    active, gelu_back = jax.vjp(partial(jax.nn.gelu, approximate=True), upper)
    active_low = active.astype(low_type)
    lowered = jnp.einsum(
        "scf,fd->scd", active_low, w_drop, preferred_element_type=float_type
    ) + b_drop.astype(float_type)
    block_out = (middle + gate_b * lowered).astype(low_type)
    upstream = upstream_rows.astype(float_type)
    gate_b_grad = jnp.sum(upstream * lowered, axis=1)
    lowered_grad = (gate_b * upstream).astype(low_type)
    drop_grad = jnp.einsum(
        "scf,scd->fd", active_low, lowered_grad, preferred_element_type=float_type
    )
    dropbias_grad = jnp.sum(lowered_grad.astype(float_type), axis=(0, 1))
    active_grad = jnp.einsum("scd,fd->scf", lowered_grad, w_drop, preferred_element_type=float_type)
    (upper_grad,) = gelu_back(active_grad)
    upper_low = upper_grad.astype(low_type)
    lift_grad = jnp.einsum("scd,scf->df", adapted_two, upper_low, preferred_element_type=float_type)
    liftbias_grad = jnp.sum(upper_low.astype(float_type), axis=(0, 1))
    adapted_two_grad = jnp.einsum(
        "scf,df->scd", upper_low, w_lift, preferred_element_type=float_type
    )
    shift_b_grad = jnp.sum(adapted_two_grad, axis=1)
    scale_b_grad = jnp.sum(adapted_two_grad * normed_two, axis=1)
    normed_two_grad = adapted_two_grad * (1.0 + scale_b)
    secondgain_grad = jnp.sum(normed_two_grad * unit_two, axis=(0, 1))
    middle_grad = upstream + norm_backward(normed_two_grad, unit_two, inverse_two, gain_two)
    gate_a_grad = jnp.sum(middle_grad * branch, axis=1)
    branch_grad = (gate_a * middle_grad).astype(low_type)
    merge_grad = jnp.einsum(
        "scd,sce->de", mixed_low, branch_grad, preferred_element_type=float_type
    )
    mixed_grad = jnp.einsum(
        "sce,de->scd", branch_grad, w_merge, preferred_element_type=float_type
    ).astype(low_type)
    keys_back, values_back = (
        lax.all_gather(keys_local, "seq", axis=1, tiled=True),
        lax.all_gather(values_local, "seq", axis=1, tiled=True),
    )

    def attend_back(block):
        query_b, keys_b, values_b, logsum_b, mixed_grad_b = block
        keys_h = keys_b.reshape(group, length, HEADS, head_width)
        values_h = values_b.reshape(group, length, HEADS, head_width)
        scores = (
            jnp.einsum("gqhd,gkhd->ghqk", query_b, keys_h, preferred_element_type=float_type)
            * scale
        )
        probs = jnp.exp(scores - logsum_b[..., None])
        probs_low = probs.astype(low_type)
        values_term = jnp.einsum(
            "ghqk,gqhd->gkhd", probs_low, mixed_grad_b, preferred_element_type=float_type
        )
        probs_grad = jnp.einsum(
            "gqhd,gkhd->ghqk", mixed_grad_b, values_h, preferred_element_type=float_type
        )
        center = jnp.sum(probs * probs_grad, axis=-1, keepdims=True)
        scores_grad = (probs * (probs_grad - center)).astype(low_type)
        query_term = (
            jnp.einsum("ghqk,gkhd->gqhd", scores_grad, keys_h, preferred_element_type=float_type)
            * scale
        )
        keys_term = (
            jnp.einsum("ghqk,gqhd->gkhd", scores_grad, query_b, preferred_element_type=float_type)
            * scale
        )
        return (
            query_term,
            keys_term.reshape(group, length, width),
            values_term.reshape(group, length, width),
        )

    mixed_grad_h = mixed_grad.reshape(head_layout)
    query_term, keys_term, values_term = lax.map(
        attend_back,
        (
            split_groups(query),
            split_groups(keys_back),
            split_groups(values_back),
            logsum,
            split_groups(mixed_grad_h),
        ),
    )
    keys_grad, values_grad = (
        lax.psum_scatter(
            keys_term.reshape(seqs, length, width).astype(jnp.bfloat16),
            "seq",
            scatter_dimension=1,
            tiled=True,
        ).astype(jnp.float32),
        lax.psum_scatter(
            values_term.reshape(seqs, length, width).astype(jnp.bfloat16),
            "seq",
            scatter_dimension=1,
            tiled=True,
        ).astype(jnp.float32),
    )
    query_grad = unrotate(query_term.reshape(head_layout), cosine, sine).reshape(seqs, span, width)
    key_grad = unrotate(keys_grad.reshape(head_layout), cosine, sine).reshape(seqs, span, width)
    projected_grad = jnp.concatenate([query_grad, key_grad, values_grad], axis=-1).astype(low_type)
    heads_grad = jnp.einsum(
        "scd,sce->de", adapted_one, projected_grad, preferred_element_type=float_type
    )
    adapted_one_grad = jnp.einsum(
        "sce,de->scd", projected_grad, w_heads, preferred_element_type=float_type
    )
    shift_a_grad = jnp.sum(adapted_one_grad, axis=1)
    scale_a_grad = jnp.sum(adapted_one_grad * normed_one, axis=1)
    normed_one_grad = adapted_one_grad * (1.0 + scale_a)
    firstgain_grad = jnp.sum(normed_one_grad * unit_one, axis=(0, 1))
    input_grad = (
        middle_grad + norm_backward(normed_one_grad, unit_one, inverse_one, gain_one)
    ).astype(low_type)
    modulation_grad = jnp.concatenate(
        [shift_a_grad, scale_a_grad, gate_a_grad, shift_b_grad, scale_b_grad, gate_b_grad], axis=-1
    )
    modulate_grad = jnp.einsum("sm,sc->mc", modulation_grad, conds, precision=lax.Precision.HIGHEST)
    modulatebias_grad = jnp.sum(modulation_grad, axis=0)
    conds_grad = jnp.einsum(
        "sm,mc->sc", modulation_grad, w_mod.astype(float_type), precision=lax.Precision.HIGHEST
    )
    table_grad = jnp.einsum(
        "sn,sc->nc", choose.astype(float_type), conds_grad, precision=lax.Precision.HIGHEST
    )
    terms = (
        heads_grad,
        merge_grad,
        lift_grad,
        liftbias_grad,
        drop_grad,
        dropbias_grad,
        modulate_grad,
        modulatebias_grad,
        firstgain_grad,
        secondgain_grad,
        table_grad,
    )
    shares = (
        lax.psum_scatter(
            terms[0].astype(jnp.bfloat16), "seq", scatter_dimension=0, tiled=True
        ).astype(jnp.float32),
        lax.psum_scatter(
            terms[1].astype(jnp.bfloat16), "seq", scatter_dimension=0, tiled=True
        ).astype(jnp.float32),
        lax.psum_scatter(
            terms[2].astype(jnp.bfloat16), "seq", scatter_dimension=0, tiled=True
        ).astype(jnp.float32),
        lax.psum_scatter(
            terms[3].astype(jnp.bfloat16), "seq", scatter_dimension=0, tiled=True
        ).astype(jnp.float32),
        lax.psum_scatter(
            terms[4].astype(jnp.bfloat16), "seq", scatter_dimension=0, tiled=True
        ).astype(jnp.float32),
        lax.psum_scatter(
            terms[5].astype(jnp.bfloat16), "seq", scatter_dimension=0, tiled=True
        ).astype(jnp.float32),
        lax.psum_scatter(
            terms[6].astype(jnp.bfloat16), "seq", scatter_dimension=0, tiled=True
        ).astype(jnp.float32),
        lax.psum_scatter(
            terms[7].astype(jnp.bfloat16), "seq", scatter_dimension=0, tiled=True
        ).astype(jnp.float32),
        lax.psum_scatter(
            terms[8].astype(jnp.bfloat16), "seq", scatter_dimension=0, tiled=True
        ).astype(jnp.float32),
        lax.psum_scatter(
            terms[9].astype(jnp.bfloat16), "seq", scatter_dimension=0, tiled=True
        ).astype(jnp.float32),
        lax.psum_scatter(
            terms[10].astype(jnp.bfloat16), "seq", scatter_dimension=0, tiled=True
        ).astype(jnp.float32),
    )
    summed = lax.psum(
        (
            shares[0],
            shares[1],
            shares[2],
            shares[3],
            shares[4],
            shares[5],
            shares[6],
            shares[7],
            shares[8],
            shares[9],
            shares[10],
        ),
        "dp",
    )
    return (
        block_out,
        input_grad,
        summed[0],
        summed[1],
        summed[2],
        summed[3],
        summed[4],
        summed[5],
        summed[6],
        summed[7],
        summed[8],
        summed[9],
        summed[10],
    )


def solution(mesh):
    return jax.shard_map(
        shards,
        mesh=mesh,
        in_specs=(
            P("dp", "seq", None),
            P(),
            P("dp"),
            P("dp", "seq"),
            P("seq", None),
            P("seq", None),
            P("seq", None),
            P("seq"),
            P("seq", None),
            P("seq"),
            P("seq", None),
            P("seq"),
            P("seq"),
            P("seq"),
            P("dp", "seq", None),
        ),
        out_specs=(
            P("dp", "seq", None),
            P("dp", "seq", None),
            P("seq", None),
            P("seq", None),
            P("seq", None),
            P("seq"),
            P("seq", None),
            P("seq"),
            P("seq", None),
            P("seq"),
            P("seq"),
            P("seq"),
            P("seq", None),
        ),
        check_vma=False,
    )
```

profile of v0, /device:TPU:8, one launch (start us, length us, event | category | flops | bytes accessed | tf_op | source)
XLA Modules:
  0.0 1158.8 jit_solution(14610913163980127939)
XLA Ops:
  13.3 7.0 all-reduce.10
  31.7 29.0 %all-gather.12.cloned.1.call-done = bf16[768,2304]{1,0:T(8,128)(2,1)} async-done(((bf16[192,2304]{1,0:T(8,128)(2,1)}), bf16[768,2304]{1,0:T(8,128)(2,1)}) %all-gather.12.cloned.1.call-update) | async-done | bytes 3538960 | tf_op jit(solution)/shard_map/all_gather | solution.py:75
  60.7 6.2 fusion.52
  77.7 5.6 split.42
  94.6 6.6 add_convert_fusion.2
  120.3 8.7 copy.93
  129.0 37.9 %all-gather.16.cloned.1.call-done = bf16[4,1024,768]{2,1,0:T(8,128)(2,1)} async-done(((bf16[4,256,768]{2,1,0:T(8,128)(2,1)}), bf16[4,1024,768]{2,1,0:T(8,128)(2,1)}) %all-gather.16.cloned.1.call-update) | async-done | bytes 6291472 | tf_op jit(solution)/shard_map/all_gather | solution.py:119
  167.0 8.7 copy.94
  175.7 75.2 %while.28 = (s32[]{:T(128)}, bf16[2,2,256,12,64]{2,4,3,1,0:T(8,128)(2,1)}, f32[2,2,12,256]{3,2,1,0:T(8,128)S(1)}, bf16[2,2,1024,768]{2,3,1,0:T(8,128)(2,1)}, bf1...) while((s32[]{:T(128)}, bf16[2,2,256,12,64]{2,4,3,1,0:T(8,128)(2,1)}, ...), condition=%wide.region_5.6_spmd.clone, body=%wide.region_2.5_spmd.sunk.clone | while | flops 1667229696 | bytes 96952408 | solution.py:143
  179.5 10.2 multiply_reduce_fusion.11
  189.7 11.7 %fusion.143 = f32[2,12,256]{2,1,0:T(8,128)S(1)} fusion(f32[2,12,256,1024]{3,2,1,0:T(8,128)} %get-tuple-element.385, f32[2,12,256]{2,1,0:T(8,128)S(1)} %get-tuple-element.386), kind=kLoop, calls=%fused_computation.3.clone.1.clone | loop fusion | flops 18868224 | bytes 25214976 | tf_op jit(solution)/shard_map/while/body/eval_jaxpr/reduce_sum | solution.py:138
  201.4 11.8 %bitcast_dynamic-update-slice_fusion.9 = bf16[2,2,256,12,64]{2,4,3,1,0:T(8,128)(2,1)} fusion(bf16[2,2,256,12,64]{2,4,3,1,0:T(8,128)(2,1)} %get-tuple-element.425, s32[]{:T(128)S(6)} %copy.125, bf16[2,1024,12,64]{1,3,2,0:T(8,128)(2,1)S(1)} %bitcast.191, f32[2,12,256,1024]{3,2,1,0:T(8,128)} %get-tuple-element.385, ...), kind=kOutput, calls=%fused_computation.5.clone.1.clone | convolution fusion | flops 830472192 | bytes 29933572 | tf_op jit(solution)/shard_map/while/body/eval_jaxpr/ghqk,gkhd->gqhd/dot_general | solution.py:140
  216.8 10.3 multiply_reduce_fusion.11
  227.1 12.0 %fusion.143 = f32[2,12,256]{2,1,0:T(8,128)S(1)} fusion(f32[2,12,256,1024]{3,2,1,0:T(8,128)} %get-tuple-element.385, f32[2,12,256]{2,1,0:T(8,128)S(1)} %get-tuple-element.386), kind=kLoop, calls=%fused_computation.3.clone.1.clone | loop fusion | flops 18868224 | bytes 25214976 | tf_op jit(solution)/shard_map/while/body/eval_jaxpr/reduce_sum | solution.py:138
  239.1 11.8 %bitcast_dynamic-update-slice_fusion.9 = bf16[2,2,256,12,64]{2,4,3,1,0:T(8,128)(2,1)} fusion(bf16[2,2,256,12,64]{2,4,3,1,0:T(8,128)(2,1)} %get-tuple-element.425, s32[]{:T(128)S(6)} %copy.125, bf16[2,1024,12,64]{1,3,2,0:T(8,128)(2,1)S(1)} %bitcast.191, f32[2,12,256,1024]{3,2,1,0:T(8,128)} %get-tuple-element.385, ...), kind=kOutput, calls=%fused_computation.5.clone.1.clone | convolution fusion | flops 830472192 | bytes 29933572 | tf_op jit(solution)/shard_map/while/body/eval_jaxpr/ghqk,gkhd->gqhd/dot_general | solution.py:140
  258.2 11.4 fusion.40
  269.7 16.6 %fusion.93 = (bf16[3072]{0:T(1024)(128)(2,1)}, bf16[4,256,3072]{2,1,0:T(8,128)(2,1)}) fusion(f32[4,256,3072]{2,1,0:T(8,128)} %fusion.40, f32[3072]{0:T(1024)S(1)} %bitcast.210, bf16[3072,768]{1,0:T(8,128)(2,1)} %all-gather.22.cloned.1.call-done, bf16[4,256,768]{2,1,0:T(8,128)(2,1)S(1)} %copy-done.27, f32[4,768]{1,0:T(4,128)S(1)} %copy-done.36), kind=kOutput, calls=%fused_computation.174 | convolution fusion | flops 4903400448 | bytes 25196544 | tf_op jit(solution)/shard_map/scd,fd->scf/dot_general | solution.py:167
  286.3 10.2 multiply_reduce_fusion.2
  296.5 15.1 %fusion.67 = (f32[4,768]{1,0:T(4,128)}, bf16[4,256,768]{2,1,0:T(8,128)(2,1)}, f32[4,768]{1,0:T(4,128)}, f32[4,256,768]{2,1,0:T(8,128)S(1)}) fusion(bf16[4,256,768]{2,1,0:T(8,128)(2,1)S(1)} %copy-done.27, f32[768]{0:T(1024)S(1)} %copy-done.65, f32[4,256,768]{2,1,0:T(8,128)S(1)} %copy-done.18, f32[4,768]{1,0:T(4,128)S(1)} %copy-done.36, ...), kind=kOutput, calls=%fused_computation.96 | convolution fusion | flops 4877445120 | bytes 33114112 | tf_op jit(solution)/shard_map/scf,fd->scd/dot_general | solution.py:156
  316.3 178.3 %while.29 = (s32[]{:T(128)}, f32[2,2,256,12,64]{2,4,3,1,0:T(8,128)}, bf16[2,2,1024,768]{2,3,1,0:T(8,128)(2,1)}, bf16[2,2,1024,768]{2,3,1,0:T(8,128)(2,1)}, bf16[...) while((s32[]{:T(128)}, ...), condition=%wide.region_12.13_spmd.clone, body=%wide.region_10.12_spmd.sunk.clone | while | flops 4105562112 | bytes 316326176 | solution.py:226
  322.2 11.5 fusion.153
  333.7 12.2 %fusion.154 = bf16[2,12,64,1024]{3,2,1,0:T(8,128)(2,1)} fusion(f32[2,12,256,1024]{3,2,1,0:T(8,128)} %fusion.153, f32[2,12,256]{2,1,0:T(8,128)S(1)} %dynamic-slice_bitcast_fusion.3, bf16[2,2,256,12,64]{2,4,3,1,0:T(8,128)(2,1)S(1)} %copy-done.6, s32[]{:T(128)S(6)} %copy.135), kind=kOutput, calls=%fused_computation.18.clone.1.clone | convolution fusion | flops 824180736 | bytes 29130756 | tf_op jit(solution)/shard_map/while/body/eval_jaxpr/ghqk,gqhd->gkhd/dot_general | solution.py:203
  345.9 17.6 %multiply_reduce_fusion.12 = (f32[2,12,256]{2,1,0:T(8,128)S(1)}, f32[2,12,256,1024]{3,2,1,0:T(8,128)}) fusion(f32[2,12,256,1024]{3,2,1,0:T(8,128)} %fusion.153, f32[2,12,256]{2,1,0:T(8,128)S(1)} %dynamic-slice_bitcast_fusion.3, bf16[2,1024,12,64]{1,3,2,0:T(8,128)(2,1)} %bitcast.188, bf16[2,2,256,12,64]{2,4,3,1,0:T(8,128)(2,1)} %get-tuple-element.461, ...), kind=kOutput, calls=%fused_computation.15.clone.1.clone | convolution fusion | flops 830466048 | bytes 54312964 | tf_op jit(solution)/shard_map/while/body/eval_jaxpr/gqhd,gkhd->ghqk/dot_general | solution.py:206
  363.5 21.7 %multiply_convert_fusion.9 = bf16[2,12,256,1024]{3,2,1,0:T(8,128)(2,1)} fusion(f32[2,12,256,1024]{3,2,1,0:T(8,128)} %get-tuple-element.404, f32[2,12,256,1024]{3,2,1,0:T(8,128)} %fusion.153, f32[2,12,256]{2,1,0:T(8,128)S(1)} %get-tuple-element.405, f32[2,12,256]{2,1,0:T(8,128)S(1)} %dynamic-slice_bitcast_fusion.3), kind=kLoop, calls=%fused_computation.14.clone.1.clone | loop fusion | flops 31457280 | bytes 62963712 | tf_op jit(solution)/shard_map/while/body/eval_jaxpr/convert_element_type | solution.py:210
  385.2 8.5 bitcast_dynamic-update-slice_fusion.11
  393.7 8.3 broadcast_multiply_fusion.12
  411.2 11.5 fusion.153
  422.7 12.2 %fusion.154 = bf16[2,12,64,1024]{3,2,1,0:T(8,128)(2,1)} fusion(f32[2,12,256,1024]{3,2,1,0:T(8,128)} %fusion.153, f32[2,12,256]{2,1,0:T(8,128)S(1)} %dynamic-slice_bitcast_fusion.3, bf16[2,2,256,12,64]{2,4,3,1,0:T(8,128)(2,1)S(1)} %copy-done.6, s32[]{:T(128)S(6)} %copy.135), kind=kOutput, calls=%fused_computation.18.clone.1.clone | convolution fusion | flops 824180736 | bytes 29130756 | tf_op jit(solution)/shard_map/while/body/eval_jaxpr/ghqk,gqhd->gkhd/dot_general | solution.py:203
  434.9 17.6 %multiply_reduce_fusion.12 = (f32[2,12,256]{2,1,0:T(8,128)S(1)}, f32[2,12,256,1024]{3,2,1,0:T(8,128)}) fusion(f32[2,12,256,1024]{3,2,1,0:T(8,128)} %fusion.153, f32[2,12,256]{2,1,0:T(8,128)S(1)} %dynamic-slice_bitcast_fusion.3, bf16[2,1024,12,64]{1,3,2,0:T(8,128)(2,1)} %bitcast.188, bf16[2,2,256,12,64]{2,4,3,1,0:T(8,128)(2,1)} %get-tuple-element.461, ...), kind=kOutput, calls=%fused_computation.15.clone.1.clone | convolution fusion | flops 830466048 | bytes 54312964 | tf_op jit(solution)/shard_map/while/body/eval_jaxpr/gqhd,gkhd->ghqk/dot_general | solution.py:206
  452.5 21.7 %multiply_convert_fusion.9 = bf16[2,12,256,1024]{3,2,1,0:T(8,128)(2,1)} fusion(f32[2,12,256,1024]{3,2,1,0:T(8,128)} %get-tuple-element.404, f32[2,12,256,1024]{3,2,1,0:T(8,128)} %fusion.153, f32[2,12,256]{2,1,0:T(8,128)S(1)} %get-tuple-element.405, f32[2,12,256]{2,1,0:T(8,128)S(1)} %dynamic-slice_bitcast_fusion.3), kind=kLoop, calls=%fused_computation.14.clone.1.clone | loop fusion | flops 31457280 | bytes 62963712 | tf_op jit(solution)/shard_map/while/body/eval_jaxpr/convert_element_type | solution.py:210
  474.2 8.5 bitcast_dynamic-update-slice_fusion.11
  482.7 8.3 broadcast_multiply_fusion.12
  494.6 8.7 copy.102
  503.4 8.7 copy.106
  518.7 12.4 %bitcast_convert_fusion = bf16[3072,768]{1,0:T(8,128)(2,1)} fusion(bf16[4,256,768]{2,1,0:T(8,128)(2,1)S(1)} %copy-done.28, f32[4,768]{1,0:T(4,128)S(1)} %copy-done.37, f32[4,256,3072]{2,1,0:T(8,128)} %fusion.40, f32[3072]{0:T(1024)S(1)} %bitcast.212), kind=kOutput, calls=%fused_computation.53 | convolution fusion | flops 4868014080 | bytes 18898944 | tf_op jit(solution)/shard_map/scf,scd->fd/dot_general | solution.py:163
  533.0 10.0 bitcast_convert_fusion.1
  547.6 14.2 %reduce-scatter.9.cloned.1.call-done = bf16[4,256,768]{2,1,0:T(8,128)(2,1)} async-done(((bf16[4,1024,768]{2,1,0:T(8,128)(2,1)}), bf16[4,256,768]{2,1,0:T(8,128)(2,1)}) %reduce-scatter.9.cloned.1.call-update) | async-done | bytes 1572880 | tf_op jit(solution)/shard_map/reduce_scatter | solution.py:237
  581.4 6.9 subtract_convert_fusion.1
  588.3 34.6 %reduce-scatter.11.cloned.1.call-done = bf16[4,256,768]{2,1,0:T(8,128)(2,1)} async-done(((bf16[4,1024,768]{2,1,0:T(8,128)(2,1)}), bf16[4,256,768]{2,1,0:T(8,128)(2,1)}) %reduce-scatter.11.cloned.1.call-update) | async-done | bytes 1572880 | tf_op jit(solution)/shard_map/reduce_scatter | solution.py:243
  623.0 9.1 fusion.64
  639.5 7.9 bitcast_convert_fusion.2
  651.7 50.6 %reduce-scatter.19.cloned.1.call-done = bf16[768,768]{1,0:T(8,128)(2,1)} async-done(((bf16[3072,768]{1,0:T(8,128)(2,1)}), bf16[768,768]{1,0:T(8,128)(2,1)}) %reduce-scatter.19.cloned.1.call-update) | async-done | bytes 1179664 | tf_op jit(solution)/shard_map/reduce_scatter | solution.py:303
  702.2 50.2 %reduce-scatter.17.cloned.1.call-done = bf16[192,3072]{1,0:T(8,128)(2,1)} async-done(((bf16[768,3072]{1,0:T(8,128)(2,1)}), bf16[192,3072]{1,0:T(8,128)(2,1)}) %reduce-scatter.17.cloned.1.call-update) | async-done | bytes 1179664 | tf_op jit(solution)/shard_map/reduce_scatter | solution.py:297
  752.6 10.4 all-reduce.9
  767.9 7.9 reduce-scatter.23.cloned.1.call-done
  775.8 28.7 %reduce-scatter.21.cloned.1.call-done = bf16[1152,128]{1,0:T(8,128)(2,1)} async-done(((bf16[4608,128]{1,0:T(8,128)(2,1)}), bf16[1152,128]{1,0:T(8,128)(2,1)}) %reduce-scatter.21.cloned.1.call-update) | async-done | bytes 294928 | tf_op jit(solution)/shard_map/reduce_scatter | solution.py:309
  804.5 43.1 %reduce-scatter.13.cloned.1.call-done = bf16[192,2304]{1,0:T(8,128)(2,1)} async-done(((bf16[768,2304]{1,0:T(8,128)(2,1)}), bf16[192,2304]{1,0:T(8,128)(2,1)}) %reduce-scatter.13.cloned.1.call-update) | async-done | bytes 884752 | tf_op jit(solution)/shard_map/reduce_scatter | solution.py:291
  847.6 304.5 %all-reduce.12 = (f32[192,2304]{1,0:T(8,128)}, f32[192,768]{1,0:T(8,128)}, f32[192,3072]{1,0:T(8,128)}, f32[768]{0:T(1024)}, f32[768,768]{1,0:T(8,128)}, /*index...) all-reduce(bf16[192,2304]{1,0:T(8,128)(2,1)} %reduce-scatter.13.clo, ...), channel_id=1, replica_groups=mesh['dp'=8,'seq'=4] {'dp'}, use_global_device_ids=true, to_apply=%region_18.19 | all-reduce | flops 1952192 | bytes 11718144 | tf_op jit(solution)/shard_map/psum | solution.py:325
  (292 shorter events, 142.2 us)
Async XLA Ops:
  7.2 21.4 %copy-start = (bf16[1024,128]{1,0:T(8,128)(2,1)S(1)}, bf16[1024,128]{1,0:T(8,128)(2,1)}, u32[]{:S(2)}) copy-start(bf16[1024,128]{1,0:T(8,128)(2,1)} %param.20) | copy-start | bytes 786436
  7.2 20.8 %copy-start.10 = (bf16[4,256,768]{2,1,0:T(8,128)(2,1)S(1)}, bf16[4,256,768]{2,1,0:T(8,128)(2,1)}, u32[]{:S(2)}) copy-start(bf16[4,256,768]{2,1,0:T(8,128)(2,1)} %param.19) | copy-start | bytes 4718596
  7.2 21.4 %copy-start.71 = (s32[4]{0:T(128)S(1)}, s32[4]{0:T(128)}, u32[]{:S(2)}) copy-start(s32[4]{0:T(128)} %param.21) | copy-start | bytes 52
  7.2 21.6 %all-gather.10.cloned.1.call-start = ((), (), s32[]{:S(2)}) async-start(), calls=%async_computation.8 | async-start | bytes 1474560 | tf_op jit(solution)/shard_map/all_gather | solution.py:81
  8.0 52.8 %all-gather.12.cloned.1.call-start = ((), (), s32[]{:S(2)}) async-start(), calls=%async_computation.9 | async-start | bytes 4423680 | tf_op jit(solution)/shard_map/all_gather | solution.py:75
  8.7 111.6 %all-gather.14.cloned.1.call-start = ((), (), s32[]{:S(2)}) async-start(), calls=%async_computation.10 | async-start | bytes 7864320 | tf_op jit(solution)/shard_map/all_gather | solution.py:120
  20.3 46.7 %copy-start.42 = (f32[768]{0:T(1024)}, f32[768]{0:T(1024)S(1)}, u32[]{:S(2)}) copy-start(f32[768]{0:T(1024)S(1)} %convert_element_type.165) | copy-start | bytes 9220
  28.0 38.9 %copy-start.40 = (f32[4,256]{1,0:T(4,128)}, f32[4,256]{1,0:T(4,128)S(1)}, u32[]{:S(2)}) copy-start(f32[4,256]{1,0:T(4,128)S(1)} %broadcast_multiply_fusion.9) | copy-start | bytes 12292
  28.6 38.3 %copy-start.44 = (f32[4,256]{1,0:T(4,128)}, f32[4,256]{1,0:T(4,128)S(1)}, u32[]{:S(2)}) copy-start(f32[4,256]{1,0:T(4,128)S(1)} %add_rsqrt_fusion.1) | copy-start | bytes 12292
  31.7 35.2 %copy-start.34 = (f32[4,768]{1,0:T(4,128)}, f32[4,768]{1,0:T(4,128)S(1)}, u32[]{:S(2)}) copy-start(f32[4,768]{1,0:T(4,128)S(1)} %get-tuple-element.257) | copy-start | bytes 36868
  31.7 35.2 %copy-start.48 = (f32[4,768]{1,0:T(4,128)}, f32[4,768]{1,0:T(4,128)S(1)}, u32[]{:S(2)}) copy-start(f32[4,768]{1,0:T(4,128)S(1)} %get-tuple-element.256) | copy-start | bytes 36868
  71.9 95.0 %all-gather.16.cloned.1.call-start = ((), (), s32[]{:S(2)}) async-start(), calls=%async_computation.11 | async-start | bytes 7864320 | tf_op jit(solution)/shard_map/all_gather | solution.py:119
  73.1 16.0 %copy-start.24 = (f32[4,256,64]{1,2,0:T(8,128)}, f32[4,256,64]{1,2,0:T(8,128)S(1)}, u32[]{:S(2)}) copy-start(f32[4,256,64]{1,2,0:T(8,128)S(1)} %get-tuple-element.250) | copy-start | bytes 786436
  77.7 17.0 %copy-start.8 = (f32[4,256,768]{2,1,0:T(8,128)}, f32[4,256,768]{2,1,0:T(8,128)S(1)}, u32[]{:S(2)}) copy-start(f32[4,256,768]{2,1,0:T(8,128)S(1)} %copy.90) | copy-start | bytes 9437188
  101.3 149.7 %all-gather.18.cloned.1.call-start = ((), (), s32[]{:S(2)}) async-start(), calls=%async_computation.12 | async-start | bytes 1474560 | tf_op jit(solution)/shard_map/all_gather | solution.py:76
  101.9 156.3 %all-gather.20.cloned.1.call-start = ((), (), s32[]{:S(2)}) async-start(), calls=%async_computation.13 | async-start | bytes 5898240 | tf_op jit(solution)/shard_map/all_gather | solution.py:77
  102.5 167.2 %all-gather.22.cloned.1.call-start = ((), (), s32[]{:S(2)}) async-start(), calls=%async_computation.14 | async-start | bytes 5898240 | tf_op jit(solution)/shard_map/all_gather | solution.py:79
  103.2 458.6 %reduce-scatter.9.cloned.1.call-start = ((), (), s32[]{:S(2)}) async-start(), calls=%async_computation.15 | async-start | bytes 7864320 | tf_op jit(solution)/shard_map/reduce_scatter | solution.py:237
  175.7 75.3 %copy-start.11 = (bf16[4,256,768]{2,1,0:T(8,128)(2,1)S(1)}, bf16[4,256,768]{2,1,0:T(8,128)(2,1)}, u32[]{:S(2)}) copy-start(bf16[4,256,768]{2,1,0:T(8,128)(2,1)} %param.19) | copy-start | bytes 4718596
  175.7 75.3 %copy-start.38 = (f32[4,768]{1,0:T(4,128)S(1)}, f32[4,768]{1,0:T(4,128)}, u32[]{:S(2)}) copy-start(f32[4,768]{1,0:T(4,128)} %get-tuple-element.258) | copy-start | bytes 36868
  256.0 40.5 %copy-start.46 = (f32[4,256]{1,0:T(4,128)}, f32[4,256]{1,0:T(4,128)S(1)}, u32[]{:S(2)}) copy-start(f32[4,256]{1,0:T(4,128)S(1)} %broadcast_multiply_fusion.8) | copy-start | bytes 12292
  258.1 38.3 %copy-start.67 = (f32[4,256]{1,0:T(4,128)}, f32[4,256]{1,0:T(4,128)S(1)}, u32[]{:S(2)}) copy-start(f32[4,256]{1,0:T(4,128)S(1)} %add_rsqrt_fusion) | copy-start | bytes 12292
  258.2 11.5 copy-start.27
  258.2 11.5 copy-start.36
  269.7 16.6 %copy-start.18 = (f32[4,256,768]{2,1,0:T(8,128)S(1)}, f32[4,256,768]{2,1,0:T(8,128)}, u32[]{:S(2)}) copy-start(f32[4,256,768]{2,1,0:T(8,128)} %copy-done.17) | copy-start | bytes 9437188
  269.7 16.6 %copy-start.73 = (bf16[768,3072]{1,0:T(8,128)(2,1)S(1)}, bf16[768,3072]{1,0:T(8,128)(2,1)}, u32[]{:S(2)}) copy-start(bf16[768,3072]{1,0:T(8,128)(2,1)} %all-gather.20.cloned.1.call-done) | copy-start | bytes 14155780
  296.5 16.7 %copy-start.31 = (bf16[768,768]{1,0:T(8,128)(2,1)S(1)}, bf16[768,768]{1,0:T(8,128)(2,1)}, u32[]{:S(2)}) copy-start(bf16[768,768]{1,0:T(8,128)(2,1)} %all-gather.18.cloned.1.call-done) | copy-start | bytes 3538948
  322.2 11.5 copy-start.6
  363.5 21.7 %copy-start.14 = (f32[2,2,256,12,64]{2,4,3,1,0:T(8,128)S(1)}, f32[2,2,256,12,64]{2,4,3,1,0:T(8,128)}, u32[]{:S(2)}) copy-start(f32[2,2,256,12,64]{2,4,3,1,0:T(8,128)} %get-tuple-element.446) | copy-start | bytes 9437188 | tf_op jit(solution)/shard_map/while
  411.2 11.5 copy-start.6
  452.5 21.7 %copy-start.14 = (f32[2,2,256,12,64]{2,4,3,1,0:T(8,128)S(1)}, f32[2,2,256,12,64]{2,4,3,1,0:T(8,128)}, u32[]{:S(2)}) copy-start(f32[2,2,256,12,64]{2,4,3,1,0:T(8,128)} %get-tuple-element.446) | copy-start | bytes 9437188 | tf_op jit(solution)/shard_map/while
  503.3 119.6 %reduce-scatter.11.cloned.1.call-start = ((), (), s32[]{:S(2)}) async-start(), calls=%async_computation.16 | async-start | bytes 7864320 | tf_op jit(solution)/shard_map/reduce_scatter | solution.py:243
  512.1 139.6 %reduce-scatter.15.cloned.1.call-start = ((), (), s32[]{:S(2)}) async-start(), calls=%async_computation.18 | async-start | bytes 1474560 | tf_op jit(solution)/shard_map/reduce_scatter | solution.py:294
  518.6 183.7 %reduce-scatter.19.cloned.1.call-start = ((), (), s32[]{:S(2)}) async-start(), calls=%async_computation.20 | async-start | bytes 5898240 | tf_op jit(solution)/shard_map/reduce_scatter | solution.py:303
  531.2 221.3 %reduce-scatter.17.cloned.1.call-start = ((), (), s32[]{:S(2)}) async-start(), calls=%async_computation.19 | async-start | bytes 5898240 | tf_op jit(solution)/shard_map/reduce_scatter | solution.py:297
  543.0 232.8 %reduce-scatter.23.cloned.1.call-start = ((), (), s32[]{:S(2)}) async-start(), calls=%async_computation.22 | async-start | bytes 327680 | tf_op jit(solution)/shard_map/reduce_scatter | solution.py:321
  547.6 17.3 %copy-start.25 = (f32[4,256,64]{1,2,0:T(8,128)S(1)}, f32[4,256,64]{1,2,0:T(8,128)}, u32[]{:S(2)}) copy-start(f32[4,256,64]{1,2,0:T(8,128)} %copy-done.24) | copy-start | bytes 786436
  581.3 41.6 %copy-start.35 = (f32[4,768]{1,0:T(4,128)S(1)}, f32[4,768]{1,0:T(4,128)}, u32[]{:S(2)}) copy-start(f32[4,768]{1,0:T(4,128)} %copy-done.34) | copy-start | bytes 36868
  581.3 41.6 %copy-start.41 = (f32[4,256]{1,0:T(4,128)S(1)}, f32[4,256]{1,0:T(4,128)}, u32[]{:S(2)}) copy-start(f32[4,256]{1,0:T(4,128)} %copy-done.40) | copy-start | bytes 12292
  581.3 41.6 %copy-start.43 = (f32[768]{0:T(1024)S(1)}, f32[768]{0:T(1024)}, u32[]{:S(2)}) copy-start(f32[768]{0:T(1024)} %copy-done.42) | copy-start | bytes 9220
  581.4 41.6 %copy-start.45 = (f32[4,256]{1,0:T(4,128)S(1)}, f32[4,256]{1,0:T(4,128)}, u32[]{:S(2)}) copy-start(f32[4,256]{1,0:T(4,128)} %copy-done.44) | copy-start | bytes 12292
  634.3 170.3 %reduce-scatter.21.cloned.1.call-start = ((), (), s32[]{:S(2)}) async-start(), calls=%async_computation.21 | async-start | bytes 1474560 | tf_op jit(solution)/shard_map/reduce_scatter | solution.py:309
  639.2 208.4 %reduce-scatter.13.cloned.1.call-start = ((), (), s32[]{:S(2)}) async-start(), calls=%async_computation.17 | async-start | bytes 4423680 | tf_op jit(solution)/shard_map/reduce_scatter | solution.py:291
  647.4 105.2 %copy-start.62 = (bf16[3072]{0:T(1024)(128)(2,1)S(1)}, bf16[3072]{0:T(1024)(128)(2,1)}, u32[]{:S(2)}) copy-start(bf16[3072]{0:T(1024)(128)(2,1)} %get-tuple-element.264) | copy-start | bytes 18436
  647.4 105.2 %copy-start.70 = (bf16[768]{0:T(1024)(128)(2,1)S(1)}, bf16[768]{0:T(1024)(128)(2,1)}, u32[]{:S(2)}) copy-start(bf16[768]{0:T(1024)(128)(2,1)} %get-tuple-element.160) | copy-start | bytes 4612
  763.4 84.3 %copy-start.30 = (bf16[768,768]{1,0:T(8,128)(2,1)S(1)}, bf16[768,768]{1,0:T(8,128)(2,1)}, u32[]{:S(2)}) copy-start(bf16[768,768]{1,0:T(8,128)(2,1)} %reduce-scatter.19.cloned.1.call-done) | copy-start | bytes 3538948
  763.4 84.3 %copy-start.33 = (bf16[192,768]{1,0:T(8,128)(2,1)S(1)}, bf16[192,768]{1,0:T(8,128)(2,1)}, u32[]{:S(2)}) copy-start(bf16[192,768]{1,0:T(8,128)(2,1)} %reduce-scatter.15.cloned.1.call-done) | copy-start | bytes 884740
  763.4 388.7 %copy-start.1 = (bf16[1024,128]{1,0:T(8,128)(2,1)S(1)}, bf16[1024,128]{1,0:T(8,128)(2,1)}, u32[]{:S(2)}) copy-start(bf16[1024,128]{1,0:T(8,128)(2,1)} %param.20) | copy-start | bytes 786436
  (48 other events, 246.0 us)
Sparse Core Ops, SparseCore 0:
  9.6 18.7 all-gather.9
  29.9 30.7 all-gather.11
  72.1 46.4 all-gather.13
  120.5 46.3 all-gather.15
  168.4 17.4 all-gather.17
  187.3 37.4 all-gather.19
  226.3 37.4 all-gather.21
  503.4 58.3 reduce-scatter.8
  564.5 58.3 reduce-scatter.10
  625.9 25.7 reduce-scatter.14
  654.4 47.8 reduce-scatter.18
  704.6 47.8 reduce-scatter.16
  755.7 20.0 reduce-scatter.22
  778.8 25.7 reduce-scatter.20
  807.1 40.4 reduce-scatter.12
where the time goes:
time: 1170 us; the launch traced here: 1160 us
  blocking collectives  333 us (28%)
  waiting for transfers between devices  301 us (26%)
  matrix products  279 us (24%)
  local copies, waits for them, and re-layouts  114 us (10%)
  other arithmetic  113 us (10%)
  between operations  17.7 us (2%)
    psum x1, blocking collectives, shards(): lax.psum((shares[0], shares[1], shares[2], shares[3], shares[4], shares[5...  304 us
    reduce_scatter x1, waiting for transfers between devices, shards(): lax.psum_scatter(terms[4].astype(jnp.bfloat16), 'seq', scatter_dimension=...  50.6 us
    reduce_scatter x1, waiting for transfers between devices, shards(): lax.psum_scatter(terms[2].astype(jnp.bfloat16), 'seq', scatter_dimension=...  50.2 us
    convert_element_type x2, other arithmetic, attend_back(): scores_grad = (probs * (probs_grad - center)).astype(low_type)  43.4 us
    reduce_scatter x1, waiting for transfers between devices, shards(): lax.psum_scatter(terms[0].astype(jnp.bfloat16), 'seq', scatter_dimension=...  43.1 us
    all_gather x1, waiting for transfers between devices, shards(): lax.all_gather(keys_local, 'seq', axis=1, tiled=True)  37.9 us
    dot_general x2, matrix products, attend_back(): jnp.einsum('gqhd,gkhd->ghqk', mixed_grad_b, values_h, preferred_element_t...  35.2 us
    reduce_scatter x1, waiting for transfers between devices, shards(): lax.psum_scatter(values_term.reshape(seqs, length, width).astype(jnp.bflo...  34.6 us
  transfers between devices with their start and end apart: 15, of which 10 were waited for; matrix products, arithmetic and copies ran while one was open for 22% of the time, Pallas kernels for 0%

commit v1 on v0

v1 whole, which is shorter than its diff:
```python
from functools import partial
import math

import jax
import jax.numpy as jnp
from jax import lax
from jax.experimental import pallas as pl
from jax.experimental.pallas import tpu as pltpu
from jax.sharding import PartitionSpec as P

HEADS = 12
EPSILON = 1e-05
LANES = 128
VMEM = 60 * 1024 * 1024
LOW = jnp.bfloat16
FULL = jnp.float32


def matmul(left, right, left_dim=1, right_dim=0):
    dims = (((left_dim,), (right_dim,)), ((), ()))
    return lax.dot_general(left, right, dims, preferred_element_type=FULL)


def call(body, name, grid, in_specs, out_specs, out_shape, scratch, flops, args, moved):
    return pl.pallas_call(
        body,
        name=name,
        grid_spec=pltpu.PrefetchScalarGridSpec(
            num_scalar_prefetch=1,
            grid=grid,
            in_specs=in_specs,
            out_specs=out_specs,
            scratch_shapes=scratch,
        ),
        out_shape=out_shape,
        compiler_params=pltpu.CompilerParams(
            dimension_semantics=("arbitrary",) * len(grid), vmem_limit_bytes=VMEM
        ),
        cost_estimate=pl.CostEstimate(flops=flops, bytes_accessed=moved, transcendentals=0),
    )(*args)


def whole(shape):
    zeros = (0,) * len(shape)
    return pl.BlockSpec(shape, lambda *_: zeros, pipeline_mode=pl.Buffered(1))


def kept(shape):
    zeros = (0,) * len(shape)
    return pl.BlockSpec(shape, lambda *_: zeros)


def assemble(me, target, pieces):
    rows = pieces[0].shape[0]
    for d, piece in enumerate(pieces):
        at = pl.multiple_of((me ^ d) * rows, 16)
        target[pl.ds(at, rows), :] = piece[...]


def split_rows(me, value, keep, send):
    rows = value.shape[0] // 4
    mine_x, mine_c = me >> 1, me & 1
    for j in range(4):
        part = value[j * rows : (j + 1) * rows].astype(LOW)[None]
        at = (j >> 1) ^ mine_x

        @pl.when(mine_c == (j & 1))
        def _(part=part, at=at):
            keep[pl.ds(at, 1)] = part

        @pl.when(mine_c != (j & 1))
        def _(part=part, at=at):
            send[pl.ds(at, 1)] = part


def normalize(values):
    center = values - jnp.mean(values, axis=-1, keepdims=True)
    inverse = lax.rsqrt(jnp.mean(center * center, axis=-1, keepdims=True) + EPSILON)
    return center * inverse, inverse


def unnormalize(weighted, unit, inverse):
    first = jnp.mean(weighted, axis=-1, keepdims=True)
    second = jnp.mean(weighted * unit, axis=-1, keepdims=True)
    return inverse * (weighted - first - unit * second)


def lower_half(head):
    lane = lax.broadcasted_iota(jnp.int32, (1, LANES), 1)
    return (lane & (head - 1)) < head // 2


def column_sum(values):
    return jnp.sum(values, axis=0, keepdims=True)


def project_kernel(head, me_ref, hidden, vectors, p0, p1, p2, p3, cosine, sine, adapted, query, key, value, weight):
    @pl.when(pl.program_id(0) == 0)
    def _():
        assemble(me_ref[0], weight, (p0, p1, p2, p3))

    unit, _ = normalize(hidden[...].astype(FULL))
    low = (unit * vectors[0:1, :] * vectors[1:2, :] + vectors[2:3, :]).astype(LOW)
    adapted[...] = low
    width = low.shape[1]
    cos, sin = cosine[...], sine[...]
    under = lower_half(head)
    signed = jnp.where(under, -sin, sin)
    scale = 1.0 / math.sqrt(head)
    for which, target in enumerate((query, key)):
        part = matmul(low, weight[:, which * width : (which + 1) * width])
        for j in range(width // LANES):
            block = part[:, j * LANES : (j + 1) * LANES]
            turned = jnp.where(
                under,
                pltpu.roll(block, LANES - head // 2, 1),
                pltpu.roll(block, head // 2, 1),
            )
            turned = (block * cos + turned * signed).astype(LOW)
            if which == 0:
                turned = turned * jnp.asarray(scale, LOW)
            target[:, j * LANES : (j + 1) * LANES] = turned
    value[...] = matmul(low, weight[:, 2 * width :]).astype(LOW)


def project(me, hidden, vectors, pieces, cosine, sine, head):
    length, width = hidden.shape
    step = 256
    rows = pl.BlockSpec((step, width), lambda i, _: (i, 0))
    angle = pl.BlockSpec((step, LANES), lambda i, _: (i, 0))
    out = jax.ShapeDtypeStruct((length, width), LOW)
    return call(
        partial(project_kernel, head),
        "project",
        (length // step,),
        [rows, whole(vectors.shape)] + [whole(p.shape) for p in pieces] + [angle, angle],
        [rows] * 4,
        [out] * 4,
        [pltpu.VMEM((width, 3 * width), LOW)],
        2 * length * width * 3 * width,
        (me, hidden, vectors, *pieces, cosine, sine),
        2 * length * width * 8,
    )


def attend_kernel(step, head, me_ref, query, key, value, mixed, logsum):
    lane = lax.broadcasted_iota(jnp.int32, (1, LANES), 1)
    first = lane < head
    keys, values = key[...], value[...]
    zero = jnp.zeros_like(keys)
    split = (jnp.where(first, keys, zero), jnp.where(first, zero, keys))
    for i in range(query.shape[0] // step):
        at = slice(i * step, (i + 1) * step)
        block = query[at, :]
        outs, sums = [], []
        for h in range(2):
            scores = matmul(block, split[h], 1, 1)
            peak = jnp.max(scores, axis=1, keepdims=True)
            expos = jnp.exp(scores - peak)
            total = jnp.sum(expos, axis=1, keepdims=True)
            outs.append(matmul(expos.astype(LOW), values) * (1.0 / total))
            sums.append(peak + jnp.log(total))
        mixed[at, :] = jnp.where(first, outs[0], outs[1]).astype(LOW)
        turned = jnp.where(first, sums[0], sums[1]).T
        logsum[0, 0:1, at] = turned[0:1, :]
        logsum[0, 1:2, at] = turned[head : head + 1, :]


def attend(me, query, key, value, head):
    length, width = query.shape
    pairs = width // LANES
    block = pl.BlockSpec((length, LANES), lambda i, _: (0, i))
    return call(
        partial(attend_kernel, 512, head),
        "attend",
        (pairs,),
        [block] * 3,
        [block, pl.BlockSpec((1, 2, length), lambda i, _: (i, 0, 0))],
        [
            jax.ShapeDtypeStruct((length, width), LOW),
            jax.ShapeDtypeStruct((pairs, 2, length), FULL),
        ],
        [],
        16 * length * length * width,
        (me, query, key, value),
        2 * length * width * 4,
    )


def merge_kernel(me_ref, mixed, hidden, vectors, p0, p1, p2, p3, middle, adapted, weight):
    @pl.when(pl.program_id(0) == 0)
    def _():
        assemble(me_ref[0], weight, (p0, p1, p2, p3))

    branch = matmul(mixed[...], weight[...])
    mid = hidden[...].astype(FULL) + vectors[0:1, :] * branch
    middle[...] = mid
    unit, _ = normalize(mid)
    adapted[...] = (unit * vectors[1:2, :] * vectors[2:3, :] + vectors[3:4, :]).astype(LOW)


def merge(me, mixed, hidden, vectors, pieces):
    length, width = hidden.shape
    step = 256
    rows = pl.BlockSpec((step, width), lambda i, _: (i, 0))
    return call(
        merge_kernel,
        "merge",
        (length // step,),
        [rows, rows, whole(vectors.shape)] + [whole(p.shape) for p in pieces],
        [rows, rows],
        [jax.ShapeDtypeStruct((length, width), FULL), jax.ShapeDtypeStruct((length, width), LOW)],
        [pltpu.VMEM((width, width), LOW)],
        2 * length * width * width,
        (me, mixed, hidden, vectors, *pieces),
        2 * length * width * 6,
    )


ORDER = (1, 3, 0, 2)


def feed_kernel(
    subs, me_ref, adapted, upstream, middle, vectors, lift_bias, l0, l1, l2, l3, d0, d1, d2, d3,
    block_out, adapted_grad, sums, liftbias_grad, lift_keep, lift_send, drop_keep, drop_send,
    lift, drop, turned, lowered_grad, lowered,
):
    i = pl.program_id(0)
    me = me_ref[0]
    gate = vectors[0:1, :]

    @pl.when(i == 0)
    def _():
        turned[...] = adapted[...].T
        lowered_grad[...] = (gate * upstream[...].astype(FULL)).astype(LOW)
        lowered[...] = jnp.zeros_like(lowered)
        adapted_grad[...] = jnp.zeros_like(adapted_grad)

    assemble(me, lift, (l0, l1, l2, l3))
    for at, d in enumerate(ORDER):

        @pl.when(i // subs == at)
        def _(d=d):
            drop[...] = (d0, d1, d2, d3)[d][...]

    weight_up, weight_down = lift[...], drop[...]
    upper = matmul(adapted[...], weight_up) + lift_bias[...]
    square = upper * upper
    root = math.sqrt(2.0 / math.pi)
    bent = jnp.tanh(upper * (root + root * 0.044715 * square))
    half = 0.5 + 0.5 * bent
    slope = half + upper * (0.5 - 0.5 * bent * bent) * (root + 3.0 * root * 0.044715 * square)
    active = (upper * half).astype(LOW)
    lowered[...] += matmul(active, weight_down)
    down = lowered_grad[...]
    upper_grad = (matmul(down, weight_down, 1, 1) * slope).astype(LOW)
    adapted_grad[...] += matmul(upper_grad, weight_up, 1, 1)
    liftbias_grad[...] = column_sum(upper_grad.astype(FULL))
    drop_grad = matmul(active, down, 0, 0).astype(LOW)[None]

    @pl.when(i < 2 * subs)
    def _():
        drop_send[...] = drop_grad

    @pl.when(i >= 2 * subs)
    def _():
        drop_keep[...] = drop_grad

    split_rows(me, matmul(turned[...], upper_grad), lift_keep, lift_send)

    @pl.when(i == 4 * subs - 1)
    def _():
        total = lowered[...] + vectors[1:2, :]
        block_out[...] = (middle[...] + gate * total).astype(LOW)
        sums[0:1, :] = column_sum(upstream[...].astype(FULL) * total)
        sums[1:2, :] = column_sum(lowered_grad[...].astype(FULL))


def feed(me, adapted, upstream, middle, vectors, lift_bias, lifts, drops):
    length, width = adapted.shape
    piece = drops[0].shape[0]
    units = 4 * piece
    step = 384
    subs = piece // step

    def order(i):
        k = i // subs
        return jnp.where(k == 0, 1, jnp.where(k == 1, 3, jnp.where(k == 2, 0, 2)))

    def column(i, me_ref):
        return (me_ref[0] ^ order(i)) * subs + i % subs

    def own(d):
        at = ORDER.index(d)
        return pl.BlockSpec((step, width), lambda i, _: (jnp.clip(i - at * subs, 0, subs - 1), 0))

    strip = pl.BlockSpec((1, step), lambda i, m: (0, column(i, m)))
    lift_spec = pl.BlockSpec((width // 4, step), lambda i, m: (0, column(i, m)))
    quarter = pl.BlockSpec((2, width // 4, step), lambda i, m: (0, 0, column(i, m)))

    def send_at(i, _):
        j = jnp.minimum(i, 2 * subs - 1)
        return (j // subs, j % subs, 0)

    def keep_at(i, _):
        j = jnp.maximum(i - 2 * subs, 0)
        return (j // subs, j % subs, 0)

    low = jax.ShapeDtypeStruct((length, width), LOW)
    return call(
        partial(feed_kernel, subs),
        "feed",
        (4 * subs,),
        [whole(adapted.shape), whole(adapted.shape), whole(adapted.shape), whole(vectors.shape), strip]
        + [lift_spec] * 4
        + [own(d) for d in range(4)],
        [
            kept((length, width)),
            kept((length, width)),
            kept((8, width)),
            strip,
            quarter,
            quarter,
            pl.BlockSpec((1, step, width), keep_at),
            pl.BlockSpec((1, step, width), send_at),
        ],
        [
            low,
            jax.ShapeDtypeStruct((length, width), FULL),
            jax.ShapeDtypeStruct((8, width), FULL),
            jax.ShapeDtypeStruct((1, units), FULL),
            jax.ShapeDtypeStruct((2, width // 4, units), LOW),
            jax.ShapeDtypeStruct((2, width // 4, units), LOW),
            jax.ShapeDtypeStruct((2, piece, width), LOW),
            jax.ShapeDtypeStruct((2, piece, width), LOW),
        ],
        [
            pltpu.VMEM((width, step), LOW),
            pltpu.VMEM((step, width), LOW),
            pltpu.VMEM((width, length), LOW),
            pltpu.VMEM((length, width), LOW),
            pltpu.VMEM((length, width), FULL),
        ],
        12 * length * width * units,
        (me, adapted, upstream, middle, vectors, lift_bias, *lifts, *drops),
        8 * width * units + 24 * length * width,
    )


def unmerge_kernel(
    me_ref, adapted_grad, middle, upstream, mixed, vectors, p0, p1, p2, p3,
    middle_grad, mixed_grad, sums, keep, send, weight, total,
):
    i = pl.program_id(0)

    @pl.when(i == 0)
    def _():
        assemble(me_ref[0], weight, (p0, p1, p2, p3))
        total[...] = jnp.zeros_like(total)
        sums[...] = jnp.zeros_like(sums)

    gate, gain, grow = vectors[0:1, :], vectors[1:2, :], vectors[2:3, :]
    unit, inverse = normalize(middle[...])
    grad = adapted_grad[...]
    sums[0:1, :] += column_sum(grad)
    sums[1:2, :] += column_sum(grad * (unit * gain))
    normed_grad = grad * grow
    sums[2:3, :] += column_sum(normed_grad * unit)
    mid_grad = upstream[...].astype(FULL) + unnormalize(normed_grad * gain, unit, inverse)
    middle_grad[...] = mid_grad
    low = mixed[...]
    sums[3:4, :] += column_sum(mid_grad * matmul(low, weight[...]))
    branch_grad = (gate * mid_grad).astype(LOW)
    total[...] += matmul(low, branch_grad, 0, 0)
    mixed_grad[...] = matmul(branch_grad, weight[...], 1, 1).astype(LOW)

    @pl.when(i == pl.num_programs(0) - 1)
    def _():
        split_rows(me_ref[0], total[...], keep, send)


def unmerge(me, adapted_grad, middle, upstream, mixed, vectors, pieces):
    length, width = mixed.shape
    step = 256
    rows = pl.BlockSpec((step, width), lambda i, _: (i, 0))
    part = (2, width // 4, width)
    return call(
        unmerge_kernel,
        "unmerge",
        (length // step,),
        [rows] * 4 + [whole(vectors.shape)] + [whole(p.shape) for p in pieces],
        [rows, rows, kept((8, width)), kept(part), kept(part)],
        [
            jax.ShapeDtypeStruct((length, width), FULL),
            jax.ShapeDtypeStruct((length, width), LOW),
            jax.ShapeDtypeStruct((8, width), FULL),
            jax.ShapeDtypeStruct(part, LOW),
            jax.ShapeDtypeStruct(part, LOW),
        ],
        [pltpu.VMEM((width, width), LOW), pltpu.VMEM((width, width), FULL)],
        6 * length * width * width,
        (me, adapted_grad, middle, upstream, mixed, vectors, *pieces),
        2 * length * width * 12,
    )


def unattend_kernel(step, head, me_ref, query, key, value, mixed, mixed_grad, logsum, cosine, sine, grads, query_sum, key_sum, value_sum):
    lane = lax.broadcasted_iota(jnp.int32, (1, LANES), 1)
    first = lane < head
    keys, values = key[...], value[...]
    zero = jnp.zeros_like(keys)
    keys_h = (jnp.where(first, keys, zero), jnp.where(first, zero, keys))
    values_h = (jnp.where(first, values, zero), jnp.where(first, zero, values))
    turned = keys.T
    scale = 1.0 / math.sqrt(head)
    for i in range(query.shape[0] // step):
        at = slice(i * step, (i + 1) * step)
        block, grad = query[at, :], mixed_grad[at, :]
        product = (grad.astype(FULL) * mixed[at, :].astype(FULL)).T
        queries, values_new, keys_new = [], [], []
        for h in range(2):
            center = jnp.sum(product[h * head : (h + 1) * head], axis=0, keepdims=True)
            probs = jnp.exp(matmul(keys_h[h], block, 1, 1) - logsum[0, h : h + 1, at])
            probs_grad = matmul(values_h[h], grad, 1, 1)
            scores_grad = (probs * (probs_grad - center)).astype(LOW)
            values_new.append(matmul(probs.astype(LOW), grad))
            keys_new.append(matmul(scores_grad, block))
            queries.append(matmul(turned[h * head : (h + 1) * head], scores_grad))
        query_sum[at, :] = jnp.concatenate(queries, axis=0).T * scale
        key_part = jnp.where(first, keys_new[0], keys_new[1])
        value_part = jnp.where(first, values_new[0], values_new[1])
        if i == 0:
            key_sum[...] = key_part
            value_sum[...] = value_part
        else:
            key_sum[...] += key_part
            value_sum[...] += value_part
    under = lower_half(head)
    cos, sin = cosine[...], sine[...]
    for which, total in enumerate((query_sum, key_sum)):
        rotated = total[...]
        swept = rotated * sin
        back = jnp.where(
            under, pltpu.roll(swept, LANES - head // 2, 1), -pltpu.roll(swept, head // 2, 1)
        )
        grads[which] = (rotated * cos + back).astype(LOW)
    grads[2] = value_sum[...].astype(LOW)


def unattend(me, query, key, value, mixed, mixed_grad, logsum, cosine, sine, head):
    length, width = query.shape
    pairs = width // LANES
    block = pl.BlockSpec((length, LANES), lambda i, _: (0, i))
    return call(
        partial(unattend_kernel, 256, head),
        "unattend",
        (pairs,),
        [block] * 5
        + [pl.BlockSpec((1, 2, length), lambda i, _: (i, 0, 0))]
        + [whole((length, LANES))] * 2,
        [pl.BlockSpec((3, length, LANES), lambda i, _: (0, 0, i))],
        [jax.ShapeDtypeStruct((3, length, width), LOW)],
        [pltpu.VMEM((length, LANES), FULL)] * 3,
        40 * length * length * width,
        (me, query, key, value, mixed, mixed_grad, logsum, cosine, sine),
        2 * length * width * 8,
    )[0]


def weigh_kernel(me_ref, adapted, grads, keep, send, turned):
    @pl.when(pl.program_id(0) == 0)
    def _():
        turned[...] = adapted[...].T

    split_rows(me_ref[0], matmul(turned[...], grads[0]), keep, send)


def weigh(me, adapted, grads):
    length, width = adapted.shape
    step = 384
    subs = width // step
    part = pl.BlockSpec((2, width // 4, step), lambda i, _: (0, 0, i))
    shape = jax.ShapeDtypeStruct((2, width // 4, 3 * width), LOW)
    return call(
        weigh_kernel,
        "weigh",
        (3 * subs,),
        [whole(adapted.shape), pl.BlockSpec((1, length, step), lambda i, _: (i // subs, 0, i % subs))],
        [part, part],
        [shape, shape],
        [pltpu.VMEM((width, length), LOW)],
        6 * length * width * width,
        (me, adapted, grads),
        2 * length * width * 7,
    )


def unproject_kernel(me_ref, grads, hidden, middle_grad, vectors, p0, p1, p2, p3, input_grad, sums, weight):
    i = pl.program_id(0)

    @pl.when(i == 0)
    def _():
        assemble(me_ref[0], weight, (p0, p1, p2, p3))
        sums[...] = jnp.zeros_like(sums)

    gain, grow = vectors[0:1, :], vectors[1:2, :]
    width = hidden.shape[1]
    grad = matmul(grads[0], weight[:, :width], 1, 1)
    grad += matmul(grads[1], weight[:, width : 2 * width], 1, 1)
    grad += matmul(grads[2], weight[:, 2 * width :], 1, 1)
    unit, inverse = normalize(hidden[...].astype(FULL))
    sums[0:1, :] += column_sum(grad)
    sums[1:2, :] += column_sum(grad * (unit * gain))
    normed_grad = grad * grow
    sums[2:3, :] += column_sum(normed_grad * unit)
    input_grad[...] = (middle_grad[...] + unnormalize(normed_grad * gain, unit, inverse)).astype(LOW)


def unproject(me, grads, hidden, middle_grad, vectors, pieces):
    length, width = hidden.shape
    step = 256
    rows = pl.BlockSpec((step, width), lambda i, _: (i, 0))
    return call(
        unproject_kernel,
        "unproject",
        (length // step,),
        [pl.BlockSpec((3, step, width), lambda i, _: (0, i, 0)), rows, rows, whole(vectors.shape)]
        + [whole(p.shape) for p in pieces],
        [rows, kept((8, width))],
        [jax.ShapeDtypeStruct((length, width), LOW), jax.ShapeDtypeStruct((8, width), FULL)],
        [pltpu.VMEM((width, 3 * width), LOW)],
        6 * length * width * width,
        (me, grads, hidden, middle_grad, vectors, *pieces),
        2 * length * width * 10,
    )


def swap(array, axis, distance):
    size = lax.axis_size(axis)
    return lax.ppermute(array, axis, [(i, i ^ distance) for i in range(size)])


def gather_pieces(weight):
    across = swap(weight, "seq", 2)
    return (weight, swap(weight, "seq", 1), across, swap(across, "seq", 1))


def stages(size):
    out = [2] if size > 1 else []
    size //= 2
    while size > 1:
        factor = 4 if size % 4 == 0 else 2
        out.append(factor)
        size //= factor
    return out


def reduce_over_rows(keep, send):
    term = keep.astype(FULL) + swap(send, "seq", 1).astype(FULL)
    term = term[0] + swap(term[1].astype(LOW), "seq", 2).astype(FULL)
    size = lax.axis_size("dp")
    place = lax.axis_index("dp")
    stride = 1
    plan = []
    for factor in stages(size):
        plan.append((factor, stride))
        columns = term.shape[-1]
        parts = term.reshape(factor, -1, columns)
        at = (place // stride) % factor
        if factor == 2:
            mine = lax.dynamic_index_in_dim(parts, at, 0, keepdims=False)
            other = lax.dynamic_index_in_dim(parts, 1 - at, 0, keepdims=False)
            term = mine + swap(other.astype(LOW), "dp", stride).astype(FULL)
        else:
            groups = [
                [base + stride * k for k in range(factor)]
                for base in range(size)
                if (base // stride) % factor == 0
            ]
            parts = lax.all_to_all(
                parts.astype(LOW), "dp", 0, 0, axis_index_groups=groups, tiled=True
            )
            term = jnp.sum(parts.astype(FULL), axis=0)
        stride *= factor
    term = term.astype(LOW)
    for factor, stride in reversed(plan):
        at = (place // stride) % factor
        rows, columns = term.shape
        target = jnp.zeros((factor, rows, columns), LOW)
        for d in range(factor):
            part = swap(term, "dp", d * stride) if d else term
            target = lax.dynamic_update_index_in_dim(target, part, at ^ d, 0)
        term = target.reshape(factor * rows, columns)
    return term.astype(FULL)


def shards(
    hidden_in,
    time_table,
    time_step,
    token_pos,
    heads_weight,
    merge_weight,
    lift_weight,
    lift_bias,
    drop_weight,
    drop_bias,
    modulate_weight,
    modulate_bias,
    first_gain,
    second_gain,
    out_grad,
):
    count = lax.axis_size("seq")
    place = lax.axis_index("seq")
    seqs, span, width = hidden_in.shape
    assert count == 4 and seqs == count
    length = span * count
    head = width // HEADS
    me = place.astype(jnp.int32).reshape(1)

    hidden = lax.all_to_all(hidden_in, "seq", 0, 0, tiled=True).reshape(length, width)
    heads = gather_pieces(heads_weight)
    positions = lax.all_to_all(token_pos, "seq", 0, 0, tiled=True).reshape(length)
    merges = gather_pieces(merge_weight)
    lifts = gather_pieces(lift_weight)
    drops = gather_pieces(drop_weight)
    upstream = lax.all_to_all(out_grad, "seq", 0, 0, tiled=True).reshape(length, width)

    table_rows, depth = time_table.shape
    choose = (time_step[:, None] == jnp.arange(table_rows, dtype=jnp.int32)[None, :]).astype(LOW)
    conds = jnp.dot(choose, time_table, preferred_element_type=FULL)
    modulation = matmul(conds.astype(LOW), modulate_weight, 1, 1) + modulate_bias.astype(FULL)
    columns = modulation.shape[1]
    small = jnp.concatenate(
        [modulation.reshape(-1)]
        + [v.astype(FULL) for v in (lift_bias, drop_bias, first_gain, second_gain)]
    )
    small = lax.all_gather(small, "seq", axis=0)
    chosen = small[:, : seqs * columns].reshape(count, seqs, columns)
    chosen = lax.dynamic_index_in_dim(chosen, place, 1, keepdims=False).reshape(6, width)
    rest = small[:, seqs * columns :]
    sizes = (lift_bias.shape[0], drop_bias.shape[0], first_gain.shape[0], second_gain.shape[0])
    vectors, at = [], 0
    for size in sizes:
        vectors.append(rest[:, at : at + size].reshape(1, -1))
        at += size
    up_bias, down_bias, gain_one, gain_two = vectors
    shift_a, scale_a, gate_a, shift_b, scale_b, gate_b = [chosen[k : k + 1] for k in range(6)]
    grow_a, grow_b = 1.0 + scale_a, 1.0 + scale_b

    def rows(*items):
        blank = jnp.zeros((8 - len(items), width), FULL)
        return jnp.concatenate(items + (blank,), axis=0)

    freqs = 10000.0 ** (-jnp.arange(0, head, 2, dtype=FULL) / head)
    freqs = jnp.tile(freqs, 2 * LANES // head)
    angles = positions.astype(FULL)[:, None] * freqs
    cosine, sine = jnp.cos(angles), jnp.sin(angles)

    adapted_a, query, key, value = project(
        me, hidden, rows(gain_one, grow_a, shift_a), heads, cosine, sine, head
    )
    mixed, logsum = attend(me, query, key, value, head)
    middle, adapted_b = merge(me, mixed, hidden, rows(gate_a, gain_two, grow_b, shift_b), merges)
    block_out, adapted_b_grad, feed_sums, liftbias_grad, lift_keep, lift_send, drop_keep, drop_send = feed(
        me, adapted_b, upstream, middle, rows(gate_b, down_bias), up_bias, lifts, drops
    )
    block_out = lax.all_to_all(block_out.reshape(count, span, width), "seq", 0, 0, tiled=True)
    drop_grad = reduce_over_rows(drop_keep, drop_send)
    lift_grad = reduce_over_rows(lift_keep, lift_send)
    middle_grad, mixed_grad, merge_sums, merge_keep, merge_send = unmerge(
        me, adapted_b_grad, middle, upstream, mixed, rows(gate_a, gain_two, grow_b), merges
    )
    merge_grad = reduce_over_rows(merge_keep, merge_send)
    grads = unattend(me, query, key, value, mixed, mixed_grad, logsum, cosine, sine, head)
    heads_keep, heads_send = weigh(me, adapted_a, grads)
    heads_grad = reduce_over_rows(heads_keep, heads_send)
    input_grad, project_sums = unproject(
        me, grads, hidden, middle_grad, rows(gain_one, grow_a), heads
    )
    input_grad = lax.all_to_all(input_grad.reshape(count, span, width), "seq", 0, 0, tiled=True)

    modulation_grad = jnp.concatenate(
        [project_sums[0:2], merge_sums[3:4], merge_sums[0:2], feed_sums[0:1]], axis=0
    ).reshape(count, columns)
    pack = jnp.concatenate(
        [
            modulation_grad,
            liftbias_grad.reshape(count, -1),
            feed_sums[1].reshape(count, -1),
            project_sums[2].reshape(count, -1),
            merge_sums[2].reshape(count, -1),
        ],
        axis=1,
    )
    pack = lax.all_to_all(pack, "seq", 0, 0, tiled=True)
    pack = jnp.concatenate([pack[:, :columns].reshape(-1), jnp.sum(pack[:, columns:], axis=0)])
    pack = lax.all_gather(pack, "dp", axis=0)
    row_grads = pack[:, : seqs * columns].reshape(-1, columns)
    totals = jnp.sum(pack[:, seqs * columns :], axis=0)
    ends, at = [], 0
    for size in sizes:
        ends.append(totals[at : at + size])
        at += size
    liftbias_out, dropbias_out, firstgain_out, secondgain_out = ends
    steps = lax.all_gather(time_step, "dp", axis=0, tiled=True)
    picks = (steps[:, None] == jnp.arange(table_rows, dtype=jnp.int32)[None, :]).astype(LOW)
    all_conds = jnp.dot(picks, time_table, preferred_element_type=FULL)
    exact = lax.Precision.HIGHEST
    modulate_grad = jnp.einsum("sm,sc->mc", row_grads, all_conds, precision=exact)
    modulatebias_grad = jnp.sum(row_grads, axis=0)
    conds_grad = jnp.einsum(
        "sm,mc->sc", row_grads, modulate_weight.astype(FULL), precision=exact
    )
    conds_grad = lax.psum(conds_grad, "seq")
    share = table_rows // count
    own = (steps[None, :] == (place * share + jnp.arange(share, dtype=jnp.int32))[:, None])
    table_grad = jnp.dot(own.astype(FULL), conds_grad, precision=exact)
    return (
        block_out,
        input_grad,
        heads_grad,
        merge_grad,
        lift_grad,
        liftbias_out,
        drop_grad,
        dropbias_out,
        modulate_grad,
        modulatebias_grad,
        firstgain_out,
        secondgain_out,
        table_grad,
    )


def solution(mesh):
    return jax.shard_map(
        shards,
        mesh=mesh,
        in_specs=(
            P("dp", "seq", None),
            P(),
            P("dp"),
            P("dp", "seq"),
            P("seq", None),
            P("seq", None),
            P("seq", None),
            P("seq"),
            P("seq", None),
            P("seq"),
            P("seq", None),
            P("seq"),
            P("seq"),
            P("seq"),
            P("dp", "seq", None),
        ),
        out_specs=(
            P("dp", "seq", None),
            P("dp", "seq", None),
            P("seq", None),
            P("seq", None),
            P("seq", None),
            P("seq"),
            P("seq", None),
            P("seq"),
            P("seq", None),
            P("seq"),
            P("seq"),
            P("seq"),
            P("seq", None),
        ),
        check_vma=False,
    )
```

time: 1170 us -> 604 us (0.52)
  blocking collectives: 333 us -> 20.6 us
  matrix products: 279 us -> 5.57 us
  Pallas kernels: 0 us -> 159 us
  other arithmetic: 113 us -> 34.7 us
  starting transfers between devices: 0.78 us -> 77.2 us
  local copies, waits for them, and re-layouts: 114 us -> 39.4 us
  waiting for transfers between devices: 301 us -> 241 us
    psum x1, blocking collectives: 304 us -> 10.1 us  [shards(): conds_grad = lax.psum(conds_grad, 'seq')]
    dot_general x31 -> x5, matrix products: 279 us -> 5.57 us  [the longest x1 1.91 us: shards(): jnp.einsum('sm,sc->mc', row_grads, all_conds, precision=exact)]
    reduce_scatter x8 -> x0, waiting for transfers between devices: 231 us -> none  [the longest x1 50.6 us: shards(): lax.psum_scatter(terms[4].astype(jnp.bfloat16), 'seq', scatter_dimension=...]
    pallas_call x0 -> x8, Pallas kernels: none -> 159 us  [call(): pl.pallas_call(body, name=name, grid_spec=pltpu.PrefetchScalarGridSpec(nu...]
    ppermute x0 -> x40, waiting for transfers between devices: none -> 93.3 us  [swap(): return lax.ppermute(array, axis, [(i, i ^ distance) for i in range(size)])]
    all_to_all x0 -> x10, waiting for transfers between devices: none -> 84.8 us  [the longest x1 50.9 us: shards(): lax.all_to_all(hidden_in, 'seq', 0, 0, tiled=True).reshape(length, width)]
    all_gather x7 -> x0, waiting for transfers between devices: 67 us -> none  [the longest x1 37.9 us: shards(): lax.all_gather(keys_local, 'seq', axis=1, tiled=True)]
    unnamed x15 -> x4, waiting for transfers between devices: 3.29 us -> 62.6 us
  transfers between devices with their start and end apart: 15 -> 52, of which waited for: 10 -> 24; matrix products, arithmetic and copies ran while one was open for 22% -> 11% of each run, Pallas kernels for 0% -> 16%
where the time goes in v1:
time: 604 us; the launch traced here: 594 us
  waiting for transfers between devices  241 us (40%)
  Pallas kernels  159 us (26%)
  starting transfers between devices  77.2 us (13%)
  local copies, waits for them, and re-layouts  39.4 us (7%)
  other arithmetic  34.7 us (6%)
  blocking collectives  20.6 us (3%)
  between operations  17.3 us (3%)
    pallas_call x8, Pallas kernels, call(): pl.pallas_call(body, name=name, grid_spec=pltpu.PrefetchScalarGridSpec(nu...  159 us
    ppermute x40, waiting for transfers between devices, swap(): return lax.ppermute(array, axis, [(i, i ^ distance) for i in range(size)])  93.3 us
    unnamed x4, waiting for transfers between devices  62.6 us
    all_to_all x1, waiting for transfers between devices, shards(): lax.all_to_all(hidden_in, 'seq', 0, 0, tiled=True).reshape(length, width)  50.9 us
    ppermute x40, starting transfers between devices, swap(): return lax.ppermute(array, axis, [(i, i ^ distance) for i in range(size)])  36 us
    all_to_all x4, waiting for transfers between devices, reduce_over_rows(): lax.all_to_all(parts.astype(LOW), 'dp', 0, 0, axis_index_groups=groups, t...  24.7 us
    all_to_all x4, starting transfers between devices, reduce_over_rows(): lax.all_to_all(parts.astype(LOW), 'dp', 0, 0, axis_index_groups=groups, t...  20.1 us
    unnamed x60, local copies, waits for them, and re-layouts  16.2 us
  transfers between devices with their start and end apart: 52, of which 24 were waited for; matrix products, arithmetic and copies ran while one was open for 11% of the time, Pallas kernels for 16%

profile of v1, /device:TPU:8, one launch (start us, length us, event | category | flops | bytes accessed | tf_op | source)
XLA Modules:
  0.0 594.3 jit_solution(7553604596992013921)
XLA Ops:
  12.8 2.8 concatenate.27
  18.0 3.2 all-to-all-start.1
  28.0 10.5 %all-reduce.2 = s32[32]{0:T(128)S(1)} all-reduce(s32[32]{0:T(128)S(1)} %dynamic-update-slice.2), channel_id=1, replica_groups=mesh['dp'=8,'seq'=4] {'dp'}, use_global_device_ids=true, to_apply=%add.2 | all-reduce | flops 32 | bytes 256
  39.9 3.6 all-to-all-start
  43.5 3.1 multiply_sine_fusion
  46.6 2.6 all-reduce.6.cloned.1.call-done
  53.3 50.9 %all-to-all-done = bf16[4,256,768]{2,1,0:T(8,128)(2,1)S(1)} async-done(((bf16[4,256,768]{2,1,0:T(8,128)(2,1)}), bf16[4,256,768]{2,1,0:T(8,128)(2,1)S(1)}, u32[]{:S(2)}, u32[]{:S(2)}) %all-to-all-start) | async-done | bytes 1572896 | tf_op jit(solution)/shard_map/all_to_all | solution.py:622
  104.3 3.6 all-to-all-start.2
  107.8 9.0 %project.1 = (bf16[1024,768]{1,0:T(8,128)(2,1)}, bf16[1024,768]{1,0:T(8,128)(2,1)}, bf16[1024,768]{1,0:T(8,128)(2,1)}, bf16[1024,768]{1,0:T(8,128)(2,1)}) custom-call(s32[1]{0:T(128)} %bitcast.me_ref, bf16[1024,768]{1,0:T(8,128)(2,1)} %bitcast.166, f32[8,768]{1,0:T(8,128)} %get-tuple-element.80.vectors, bf16[192,2304]{1,0:T(8,128)(2,1)} %p0.7, ...), custom_call_target="tpu_custom_call" | custom-call | flops 3623878656 | bytes 12582912 | tf_op jit(solution)/shard_map/project/pallas_call | solution.py:25
  118.0 21.6 %attend.1 = (bf16[1024,768]{1,0:T(8,128)(2,1)}, f32[6,2,1024]{2,1,0:T(2,128)}) custom-call(s32[1]{0:T(128)} %bitcast.me_ref, bf16[1024,768]{1,0:T(8,128)(2,1)} %get-tuple-element.38.query, bf16[1024,768]{1,0:T(8,128)(2,1)} %get-tuple-element.39.key, bf16[1024,768]{1,0:T(8,128)(2,1)} %get-tuple-element.40.value), custom_call_target="tpu_custom_call" | custom-call | flops 12884901888 | bytes 6291456 | tf_op jit(solution)/shard_map/attend/pallas_call | solution.py:25
  140.3 6.1 %merge.1 = (f32[1024,768]{1,0:T(8,128)}, bf16[1024,768]{1,0:T(8,128)(2,1)}) custom-call(s32[1]{0:T(128)} %bitcast.me_ref, bf16[1024,768]{1,0:T(8,128)(2,1)} %get-tuple-element.41.mixed, bf16[1024,768]{1,0:T(8,128)(2,1)} %bitcast.167, f32[8,768]{1,0:T(8,128)} %concatenate.29.vectors, bf16[192,768]{1,0:T(8,128)(2,1)} %p0.6, ...), custom_call_target="tpu_custom_call" | custom-call | flops 1207959552 | bytes 9437184 | tf_op jit(solution)/shard_map/merge/pallas_call | solution.py:25
  148.1 54.7 %feed.1 = (bf16[1024,768]{1,0:T(8,128)(2,1)}, f32[1024,768]{1,0:T(8,128)}, f32[8,768]{1,0:T(8,128)}, f32[1,3072]{1,0:T(1,128)}, bf16[2,192,3072]{2,1,0:T(8,128)(...) custom-call(s32[1]{0:T(128)} %bitcast.me_ref, ...), custom_call_target="tpu_custom_call" | custom-call | flops 28991029248 | bytes 37748736 | tf_op jit(solution)/shard_map/feed/pallas_call | solution.py:25
  202.9 11.0 %unmerge.1 = (f32[1024,768]{1,0:T(8,128)}, bf16[1024,768]{1,0:T(8,128)(2,1)}, f32[8,768]{1,0:T(8,128)}, bf16[2,192,768]{2,1,0:T(8,128)(2,1)}, bf16[2,192,768]{2,1,0:T(8,128)(2,1)}) custom-call(s32[1]{0:T(128)} %bitcast.me_ref, f32[1024,768]{1,0:T(8,128)} %get-tuple-element.45.adapted_grad, f32[1024,768]{1,0:T(8,128)} %get-tuple-element.43.middle, ...), custom_call_target="tpu_custom_call" | custom-call | flops 3623878656 | bytes 18874368 | tf_op jit(solution)/shard_map/unmerge/pallas_call | solution.py:25
  215.2 36.1 %unattend.1.grads = bf16[3,1024,768]{2,1,0:T(8,128)(2,1)} custom-call(s32[1]{0:T(128)} %bitcast.me_ref, bf16[1024,768]{1,0:T(8,128)(2,1)} %get-tuple-element.38.query, bf16[1024,768]{1,0:T(8,128)(2,1)} %get-tuple-element.39.key, bf16[1024,768]{1,0:T(8,128)(2,1)} %get-tuple-element.40.value, bf16[1024,768]{1,0:T(8,128)(2,1)} %get-tuple-element.41.mixed, ...), custom_call_target="tpu_custom_call" | custom-call | flops 32212254720 | bytes 12582912 | tf_op jit(solution)/shard_map/unattend/pallas_call | solution.py:25
  251.4 9.9 %unproject.1 = (bf16[1024,768]{1,0:T(8,128)(2,1)}, f32[8,768]{1,0:T(8,128)}) custom-call(s32[1]{0:T(128)} %bitcast.me_ref, bf16[3,1024,768]{2,1,0:T(8,128)(2,1)} %unattend.1.grads, bf16[1024,768]{1,0:T(8,128)(2,1)} %bitcast.168, f32[1024,768]{1,0:T(8,128)} %get-tuple-element.48.middle_grad, f32[8,768]{1,0:T(8,128)} %get-tuple-element.79.vectors, ...), custom_call_target="tpu_custom_call" | custom-call | flops 3623878656 | bytes 15728640 | tf_op jit(solution)/shard_map/unproject/pallas_call | solution.py:25
  266.6 3.3 all-to-all-start.8
  271.2 2.6 all-to-all-done.8
  273.8 3.6 all-to-all-start.4
  283.3 10.2 %weigh.1 = (bf16[2,192,2304]{2,1,0:T(8,128)(2,1)}, bf16[2,192,2304]{2,1,0:T(8,128)(2,1)}) custom-call(s32[1]{0:T(128)} %bitcast.me_ref, bf16[1024,768]{1,0:T(8,128)(2,1)} %get-tuple-element.50.adapted, bf16[3,1024,768]{2,1,0:T(8,128)(2,1)} %unattend.1.grads), custom_call_target="tpu_custom_call" | custom-call | flops 3623878656 | bytes 11010048 | tf_op jit(solution)/shard_map/weigh/pallas_call | solution.py:25
  293.5 59.9 %all-reduce.8.cloned.1.call-done = f32[47616]{0:T(1024)} async-done(((f32[47616]{0:T(1024)}), f32[47616]{0:T(1024)}) %all-reduce.8.cloned.1.call-update) | async-done | bytes 190480
  355.5 10.1 %psum.7 = f32[32,128]{1,0:T(8,128)S(1)} all-reduce(f32[32,128]{1,0:T(8,128)S(1)} %fusion.29), channel_id=1, replica_groups=mesh['dp'=8,'seq'=4] {'seq'}, use_global_device_ids=true, to_apply=%region_7.8 | all-reduce | flops 4096 | bytes 32768 | tf_op jit(solution)/shard_map/psum | solution.py:716
  372.6 4.9 all-to-all-start.6
  378.4 4.4 all-to-all-done.6
  383.5 3.8 all-to-all-start.3
  390.8 2.7 collective-permute-done.22
  394.7 2.8 collective-permute-done.24
  400.8 6.5 %all-to-all-done.3 = bf16[4,256,768]{2,1,0:T(8,128)(2,1)S(1)} async-done(((bf16[4,256,768]{2,1,0:T(8,128)(2,1)}), bf16[4,256,768]{2,1,0:T(8,128)(2,1)S(1)}, u32[]{:S(2)}, u32[]{:S(2)}) %all-to-all-start.3) | async-done | bytes 1572896 | tf_op jit(solution)/shard_map/all_to_all | solution.py:669
  412.1 2.2 convert_add_fusion
  417.7 2.5 convert_add_fusion.1
  420.2 14.1 %collective-permute-done.13 = bf16[192,2304]{1,0:T(8,128)(2,1)S(1)} collective-permute-done((bf16[192,2304]{1,0:T(8,128)(2,1)S(1)}, bf16[192,2304]{1,0:T(8,128)(2,1)S(1)}, u32[]{:S(2)}, u32[]{:S(2)}) %collective-permute-start.13) | collective-permute-done | bytes 884768 | tf_op jit(solution)/shard_map/ppermute | solution.py:540
  435.8 8.2 %collective-permute-done.14 = bf16[96,2304]{1,0:T(8,128)(2,1)S(1)} collective-permute-done((bf16[96,2304]{1,0:T(8,128)(2,1)S(1)}, bf16[96,2304]{1,0:T(8,128)(2,1)S(1)}, u32[]{:S(2)}, u32[]{:S(2)}) %collective-permute-start.14) | collective-permute-done | bytes 442400 | tf_op jit(solution)/shard_map/ppermute | solution.py:540
  444.8 4.1 all-to-all-start.5
  448.9 10.7 %collective-permute-done.34 = bf16[768,768]{1,0:T(8,128)(2,1)} collective-permute-done((bf16[768,768]{1,0:T(8,128)(2,1)S(1)}, bf16[768,768]{1,0:T(8,128)(2,1)}, u32[]{:S(2)}, u32[]{:S(2)}) %collective-permute-start.34) | collective-permute-done | bytes 1179680 | tf_op jit(solution)/shard_map/ppermute | solution.py:540
  459.7 2.4 fusion
  463.6 20.0 %collective-permute-done.27 = bf16[192,3072]{1,0:T(8,128)(2,1)} collective-permute-done((bf16[192,3072]{1,0:T(8,128)(2,1)S(1)}, bf16[192,3072]{1,0:T(8,128)(2,1)}, u32[]{:S(2)}, u32[]{:S(2)}) %collective-permute-start.27) | collective-permute-done | bytes 1179680 | tf_op jit(solution)/shard_map/ppermute | solution.py:540
  495.8 2.8 collective-permute-done.17
  500.6 2.4 fusion.5
  503.0 4.9 all-to-all-start.9
  511.1 8.3 %all-to-all-done.9 = bf16[4,96,768]{2,1,0:T(8,128)(2,1)} async-done(((bf16[4,96,768]{2,1,0:T(8,128)(2,1)}), bf16[4,96,768]{2,1,0:T(8,128)(2,1)}, u32[]{:S(2)}, u32[]{:S(2)}) %all-to-all-start.9) | async-done | bytes 589856 | tf_op jit(solution)/shard_map/all_to_all | solution.py:580
  519.4 6.2 %all-to-all-start.7 = ((bf16[4,24,3072]{2,1,0:T(8,128)(2,1)}), bf16[4,24,3072]{2,1,0:T(8,128)(2,1)S(1)}, u32[]{:S(2)}, u32[]{:S(2)}) async-start(bf16[4,24,3072]{2,1,0:T(8,128)(2,1)} %bitcast.157), calls=%async_computation.7 | async-start | bytes 1179648 | tf_op jit(solution)/shard_map/all_to_all | solution.py:580
  529.2 2.9 collective-permute-start.37
  532.7 12.0 %all-to-all-done.7 = bf16[4,24,3072]{2,1,0:T(8,128)(2,1)S(1)} async-done(((bf16[4,24,3072]{2,1,0:T(8,128)(2,1)}), bf16[4,24,3072]{2,1,0:T(8,128)(2,1)S(1)}, u32[]{:S(2)}, u32[]{:S(2)}) %all-to-all-start.7) | async-done | bytes 589856 | tf_op jit(solution)/shard_map/all_to_all | solution.py:580
  546.1 5.6 collective-permute-start.30
  552.4 5.3 collective-permute-done.38
  558.4 2.5 collective-permute-done.30
  561.0 3.6 collective-permute-done.31
  565.6 7.0 %collective-permute-done.39 = bf16[384,768]{1,0:T(8,128)(2,1)S(1)} collective-permute-done((bf16[384,768]{1,0:T(8,128)(2,1)S(1)}, bf16[384,768]{1,0:T(8,128)(2,1)S(1)}, u32[]{:S(2)}, u32[]{:S(2)}) %collective-permute-start.39) | collective-permute-done | bytes 589856 | tf_op jit(solution)/shard_map/ppermute | solution.py:540
  574.2 7.9 %collective-permute-done.32 = bf16[96,3072]{1,0:T(8,128)(2,1)S(1)} collective-permute-done((bf16[96,3072]{1,0:T(8,128)(2,1)S(1)}, bf16[96,3072]{1,0:T(8,128)(2,1)S(1)}, u32[]{:S(2)}, u32[]{:S(2)}) %collective-permute-start.32) | collective-permute-done | bytes 589856 | tf_op jit(solution)/shard_map/ppermute | solution.py:540
  (245 shorter events, 97.8 us)
Async XLA Ops:
  7.2 42.1 %all-reduce.6.cloned.1.call-start = ((), (), s32[]{:S(2)}) async-start(), calls=%async_computation.10 | async-start | bytes 196608
  7.2 43.1 %collective-permute-start.1 = (bf16[192,2304]{1,0:T(8,128)(2,1)}, bf16[192,2304]{1,0:T(8,128)(2,1)S(1)}, u32[]{:S(2)}, u32[]{:S(2)}) collective-permute-start(bf16[192,2304]{1,0:T(8,128)(2,1)} %p0.7), channel_id=1, source_target_pairs={{0,2},{1,3},{2,0},{3,1},{4,6},{5,7},{6,4},{7,5},{8,10},{9,11},{10,... | collective-permute-start | bytes 2654216 | tf_op jit(solution)/shard_map/ppermute | solution.py:540
  8.8 44.0 %collective-permute-start = (bf16[192,2304]{1,0:T(8,128)(2,1)}, bf16[192,2304]{1,0:T(8,128)(2,1)}, u32[]{:S(2)}, u32[]{:S(2)}) collective-permute-start(bf16[192,2304]{1,0:T(8,128)(2,1)} %p0.7), channel_id=1, source_target_pairs={{0,1},{1,0},{2,3},{3,2},{4,5},{5,4},{6,7},{7,6},{8,9},{9,8},{10,11... | collective-permute-start | bytes 2654216 | tf_op jit(solution)/shard_map/ppermute | solution.py:540
  18.0 22.0 %all-to-all-start.1 = ((s32[4,1,256]{2,1,0:T(1,128)}), s32[4,1,256]{2,1,0:T(1,128)S(1)}, u32[]{:S(2)}, u32[]{:S(2)}) async-start(s32[4,1,256]{2,1,0:T(1,128)} %all_to_all.39), calls=%async_computation.1 | async-start | bytes 8192 | tf_op jit(solution)/shard_map/all_to_all | solution.py:624
  21.2 95.6 %collective-permute-start.4 = (bf16[192,768]{1,0:T(8,128)(2,1)}, bf16[192,768]{1,0:T(8,128)(2,1)}, u32[]{:S(2)}, u32[]{:S(2)}) collective-permute-start(bf16[192,768]{1,0:T(8,128)(2,1)} %p0.6), channel_id=1, source_target_pairs={{0,2},{1,3},{2,0},{3,1},{4,6},{5,7},{6,4},{7,5},{8,10},{9,11},{10,... | collective-permute-start | bytes 884744 | tf_op jit(solution)/shard_map/ppermute | solution.py:540
  23.2 94.3 %collective-permute-start.10 = (bf16[768,768]{1,0:T(8,128)(2,1)}, bf16[768,768]{1,0:T(8,128)(2,1)}, u32[]{:S(2)}, u32[]{:S(2)}) collective-permute-start(bf16[768,768]{1,0:T(8,128)(2,1)} %d0.1), channel_id=1, source_target_pairs={{0,2},{1,3},{2,0},{3,1},{4,6},{5,7},{6,4},{7,5},{8,10},{9,11},{10,... | collective-permute-start | bytes 3538952 | tf_op jit(solution)/shard_map/ppermute | solution.py:540
  23.3 94.6 %collective-permute-start.7 = (bf16[192,3072]{1,0:T(8,128)(2,1)}, bf16[192,3072]{1,0:T(8,128)(2,1)}, u32[]{:S(2)}, u32[]{:S(2)}) collective-permute-start(bf16[192,3072]{1,0:T(8,128)(2,1)} %l0.1), channel_id=1, source_target_pairs={{0,2},{1,3},{2,0},{3,1},{4,6},{5,7},{6,4},{7,5},{8,10},{9,11},{10,... | collective-permute-start | bytes 3538952 | tf_op jit(solution)/shard_map/ppermute | solution.py:540
  39.9 64.3 %all-to-all-start = ((bf16[4,256,768]{2,1,0:T(8,128)(2,1)}), bf16[4,256,768]{2,1,0:T(8,128)(2,1)S(1)}, u32[]{:S(2)}, u32[]{:S(2)}) async-start(bf16[4,256,768]{2,1,0:T(8,128)(2,1)} %param.15), calls=%async_computation | async-start | bytes 3145728 | tf_op jit(solution)/shard_map/all_to_all | solution.py:622
  52.8 64.7 %collective-permute-start.3 = (bf16[192,768]{1,0:T(8,128)(2,1)}, bf16[192,768]{1,0:T(8,128)(2,1)}, u32[]{:S(2)}, u32[]{:S(2)}) collective-permute-start(bf16[192,768]{1,0:T(8,128)(2,1)} %p0.6), channel_id=1, source_target_pairs={{0,1},{1,0},{2,3},{3,2},{4,5},{5,4},{6,7},{7,6},{8,9},{9,8},{10,11... | collective-permute-start | bytes 884744 | tf_op jit(solution)/shard_map/ppermute | solution.py:540
  53.3 93.2 %collective-permute-start.6 = (bf16[192,3072]{1,0:T(8,128)(2,1)}, bf16[192,3072]{1,0:T(8,128)(2,1)}, u32[]{:S(2)}, u32[]{:S(2)}) collective-permute-start(bf16[192,3072]{1,0:T(8,128)(2,1)} %l0.1), channel_id=1, source_target_pairs={{0,1},{1,0},{2,3},{3,2},{4,5},{5,4},{6,7},{7,6},{8,9},{9,8},{10,11... | collective-permute-start | bytes 3538952 | tf_op jit(solution)/shard_map/ppermute | solution.py:540
  104.3 42.2 %all-to-all-start.2 = ((bf16[4,256,768]{2,1,0:T(8,128)(2,1)}), bf16[4,256,768]{2,1,0:T(8,128)(2,1)S(1)}, u32[]{:S(2)}, u32[]{:S(2)}) async-start(bf16[4,256,768]{2,1,0:T(8,128)(2,1)} %param.29), calls=%async_computation.2 | async-start | bytes 3145728 | tf_op jit(solution)/shard_map/all_to_all | solution.py:628
  116.9 29.6 %collective-permute-start.9 = (bf16[768,768]{1,0:T(8,128)(2,1)}, bf16[768,768]{1,0:T(8,128)(2,1)S(1)}, u32[]{:S(2)}, u32[]{:S(2)}) collective-permute-start(bf16[768,768]{1,0:T(8,128)(2,1)} %d0.1), channel_id=1, source_target_pairs={{0,1},{1,0},{2,3},{3,2},{4,5},{5,4},{6,7},{7,6},{8,9},{9,8},{10,11... | collective-permute-start | bytes 3538952 | tf_op jit(solution)/shard_map/ppermute | solution.py:540
  117.4 22.2 %collective-permute-start.5 = (bf16[192,768]{1,0:T(8,128)(2,1)}, bf16[192,768]{1,0:T(8,128)(2,1)S(1)}, u32[]{:S(2)}, u32[]{:S(2)}) collective-permute-start(bf16[192,768]{1,0:T(8,128)(2,1)} %collective-permute-done.4.p2), channel_id=1, source_target_pairs={{0,1},{1,0},{2,3},{3,2},{4,5},{5,4},{6,7},{7,6},{8,9},{9,8},{10,11... | collective-permute-start | bytes 884744 | tf_op jit(solution)/shard_map/ppermute | solution.py:540
  117.5 29.0 %collective-permute-start.11 = (bf16[768,768]{1,0:T(8,128)(2,1)}, bf16[768,768]{1,0:T(8,128)(2,1)}, u32[]{:S(2)}, u32[]{:S(2)}) collective-permute-start(bf16[768,768]{1,0:T(8,128)(2,1)} %collective-permute-done.10.d2), channel_id=1, source_target_pairs={{0,1},{1,0},{2,3},{3,2},{4,5},{5,4},{6,7},{7,6},{8,9},{9,8},{10,11... | collective-permute-start | bytes 3538952 | tf_op jit(solution)/shard_map/ppermute | solution.py:540
  117.9 28.6 %collective-permute-start.8 = (bf16[192,3072]{1,0:T(8,128)(2,1)}, bf16[192,3072]{1,0:T(8,128)(2,1)}, u32[]{:S(2)}, u32[]{:S(2)}) collective-permute-start(bf16[192,3072]{1,0:T(8,128)(2,1)} %collective-permute-done.7.l2), channel_id=1, source_target_pairs={{0,1},{1,0},{2,3},{3,2},{4,5},{5,4},{6,7},{7,6},{8,9},{9,8},{10,11... | collective-permute-start | bytes 3538952 | tf_op jit(solution)/shard_map/ppermute | solution.py:540
  214.7 63.7 %collective-permute-start.19 = (bf16[2,192,768]{2,1,0:T(8,128)(2,1)}, bf16[2,192,768]{2,1,0:T(8,128)(2,1)S(1)}, u32[]{:S(2)}, u32[]{:S(2)}) collective-permute-start(bf16[2,192,768]{2,1,0:T(8,128)(2,1)} %get-tuple-element.54), channel_id=1, source_target_pairs={{0,1},{1,0},{2,3},{3,2},{4,5},{5,4},{6,7},{7,6},{8,9},{9,8},{10,11... | collective-permute-start | bytes 1769480 | tf_op jit(solution)/shard_map/ppermute | solution.py:540
  266.6 7.2 %all-to-all-start.8 = ((f32[4,1,2496]{2,1,0:T(1,128)}), f32[4,1,2496]{2,1,0:T(1,128)S(1)}, u32[]{:S(2)}, u32[]{:S(2)}) async-start(f32[4,1,2496]{2,1,0:T(1,128)} %all_to_all.47), calls=%async_computation.8 | async-start | bytes 81920 | tf_op jit(solution)/shard_map/all_to_all | solution.py:697
  270.6 141.5 %collective-permute-start.33 = (bf16[2,768,768]{2,1,0:T(8,128)(2,1)}, bf16[2,768,768]{2,1,0:T(8,128)(2,1)}, u32[]{:S(2)}, u32[]{:S(2)}) collective-permute-start(bf16[2,768,768]{2,1,0:T(8,128)(2,1)} %get-tuple-element.62), channel_id=1, source_target_pairs={{0,1},{1,0},{2,3},{3,2},{4,5},{5,4},{6,7},{7,6},{8,9},{9,8},{10,11... | collective-permute-start | bytes 7077896 | tf_op jit(solution)/shard_map/ppermute | solution.py:540
  271.1 145.1 %collective-permute-start.26 = (bf16[2,192,3072]{2,1,0:T(8,128)(2,1)}, bf16[2,192,3072]{2,1,0:T(8,128)(2,1)}, u32[]{:S(2)}, u32[]{:S(2)}) collective-permute-start(bf16[2,192,3072]{2,1,0:T(8,128)(2,1)} %get-tuple-element.56), channel_id=1, source_target_pairs={{0,1},{1,0},{2,3},{3,2},{4,5},{5,4},{6,7},{7,6},{8,9},{9,8},{10,11... | collective-permute-start | bytes 7077896 | tf_op jit(solution)/shard_map/ppermute | solution.py:540
  273.8 98.8 %all-to-all-start.4 = ((bf16[4,256,768]{2,1,0:T(8,128)(2,1)}), bf16[4,256,768]{2,1,0:T(8,128)(2,1)S(1)}, u32[]{:S(2)}, u32[]{:S(2)}) async-start(bf16[4,256,768]{2,1,0:T(8,128)(2,1)} %bitcast.165), calls=%async_computation.4 | async-start | bytes 3145728 | tf_op jit(solution)/shard_map/all_to_all | solution.py:682
  277.4 76.1 %all-reduce.8.cloned.1.call-start = ((), (), s32[]{:S(2)}) async-start(), calls=%async_computation.11 | async-start | bytes 385024
  281.4 84.2 %collective-permute-start.20 = (bf16[192,768]{1,0:T(8,128)(2,1)}, bf16[192,768]{1,0:T(8,128)(2,1)}, u32[]{:S(2)}, u32[]{:S(2)}) collective-permute-start(bf16[192,768]{1,0:T(8,128)(2,1)} %fusion.13), channel_id=1, source_target_pairs={{0,2},{1,3},{2,0},{3,1},{4,6},{5,7},{6,4},{7,5},{8,10},{9,11},{10,... | collective-permute-start | bytes 884744 | tf_op jit(solution)/shard_map/ppermute | solution.py:540
  293.5 114.8 %collective-permute-start.12 = (bf16[2,192,2304]{2,1,0:T(8,128)(2,1)}, bf16[2,192,2304]{2,1,0:T(8,128)(2,1)}, u32[]{:S(2)}, u32[]{:S(2)}) collective-permute-start(bf16[2,192,2304]{2,1,0:T(8,128)(2,1)} %get-tuple-element.52), channel_id=1, source_target_pairs={{0,1},{1,0},{2,3},{3,2},{4,5},{5,4},{6,7},{7,6},{8,9},{9,8},{10,11... | collective-permute-start | bytes 5308424 | tf_op jit(solution)/shard_map/ppermute | solution.py:540
  366.7 5.3 collective-permute-start.21
  372.6 10.2 %all-to-all-start.6 = ((bf16[4,24,768]{2,1,0:T(8,128)(2,1)}), bf16[4,24,768]{2,1,0:T(8,128)(2,1)S(1)}, u32[]{:S(2)}, u32[]{:S(2)}) async-start(bf16[4,24,768]{2,1,0:T(8,128)(2,1)} %bitcast.27), calls=%async_computation.6 | async-start | bytes 294912 | tf_op jit(solution)/shard_map/all_to_all | solution.py:580
  383.5 23.9 %all-to-all-start.3 = ((bf16[4,256,768]{2,1,0:T(8,128)(2,1)}), bf16[4,256,768]{2,1,0:T(8,128)(2,1)S(1)}, u32[]{:S(2)}, u32[]{:S(2)}) async-start(bf16[4,256,768]{2,1,0:T(8,128)(2,1)} %bitcast.164), calls=%async_computation.3 | async-start | bytes 3145728 | tf_op jit(solution)/shard_map/all_to_all | solution.py:669
  397.4 10.0 %collective-permute-start.25 = (bf16[96,768]{1,0:T(8,128)(2,1)S(1)}, bf16[96,768]{1,0:T(8,128)(2,1)S(1)}, u32[]{:S(2)}, u32[]{:S(2)}) collective-permute-start(bf16[96,768]{1,0:T(8,128)(2,1)S(1)} %bitcast.171), channel_id=1, source_target_pairs={{0,4},{4,0},{8,12},{12,8},{16,20},{20,16},{24,28},{28,24},{1,5},{5... | collective-permute-start | bytes 442376 | tf_op jit(solution)/shard_map/ppermute | solution.py:540
  411.7 22.6 %collective-permute-start.13 = (bf16[192,2304]{1,0:T(8,128)(2,1)S(1)}, bf16[192,2304]{1,0:T(8,128)(2,1)S(1)}, u32[]{:S(2)}, u32[]{:S(2)}) collective-permute-start(bf16[192,2304]{1,0:T(8,128)(2,1)S(1)} %fusion.7), channel_id=1, source_target_pairs={{0,2},{1,3},{2,0},{3,1},{4,6},{5,7},{6,4},{7,5},{8,10},{9,11},{10,... | collective-permute-start | bytes 2654216 | tf_op jit(solution)/shard_map/ppermute | solution.py:540
  414.4 45.3 %collective-permute-start.34 = (bf16[768,768]{1,0:T(8,128)(2,1)S(1)}, bf16[768,768]{1,0:T(8,128)(2,1)}, u32[]{:S(2)}, u32[]{:S(2)}) collective-permute-start(bf16[768,768]{1,0:T(8,128)(2,1)S(1)} %fusion.4), channel_id=1, source_target_pairs={{0,2},{1,3},{2,0},{3,1},{4,6},{5,7},{6,4},{7,5},{8,10},{9,11},{10,... | collective-permute-start | bytes 3538952 | tf_op jit(solution)/shard_map/ppermute | solution.py:540
  434.5 9.5 %collective-permute-start.14 = (bf16[96,2304]{1,0:T(8,128)(2,1)S(1)}, bf16[96,2304]{1,0:T(8,128)(2,1)S(1)}, u32[]{:S(2)}, u32[]{:S(2)}) collective-permute-start(bf16[96,2304]{1,0:T(8,128)(2,1)S(1)} %fusion.12), channel_id=1, source_target_pairs={{0,4},{4,0},{8,12},{12,8},{16,20},{20,16},{24,28},{28,24},{1,5},{5... | collective-permute-start | bytes 1327112 | tf_op jit(solution)/shard_map/ppermute | solution.py:540
  435.4 48.2 %collective-permute-start.27 = (bf16[192,3072]{1,0:T(8,128)(2,1)S(1)}, bf16[192,3072]{1,0:T(8,128)(2,1)}, u32[]{:S(2)}, u32[]{:S(2)}) collective-permute-start(bf16[192,3072]{1,0:T(8,128)(2,1)S(1)} %fusion.3), channel_id=1, source_target_pairs={{0,2},{1,3},{2,0},{3,1},{4,6},{5,7},{6,4},{7,5},{8,10},{9,11},{10,... | collective-permute-start | bytes 3538952 | tf_op jit(solution)/shard_map/ppermute | solution.py:540
  444.8 41.8 %all-to-all-start.5 = ((bf16[4,24,2304]{2,1,0:T(8,128)(2,1)}), bf16[4,24,2304]{2,1,0:T(8,128)(2,1)S(1)}, u32[]{:S(2)}, u32[]{:S(2)}) async-start(bf16[4,24,2304]{2,1,0:T(8,128)(2,1)} %bitcast.13), calls=%async_computation.5 | async-start | bytes 884736 | tf_op jit(solution)/shard_map/all_to_all | solution.py:580
  463.0 37.7 %collective-permute-start.35 = (bf16[384,768]{1,0:T(8,128)(2,1)}, bf16[384,768]{1,0:T(8,128)(2,1)}, u32[]{:S(2)}, u32[]{:S(2)}) collective-permute-start(bf16[384,768]{1,0:T(8,128)(2,1)} %fusion.10), channel_id=1, source_target_pairs={{0,4},{4,0},{8,12},{12,8},{16,20},{20,16},{24,28},{28,24},{1,5},{5... | collective-permute-start | bytes 1769480 | tf_op jit(solution)/shard_map/ppermute | solution.py:540
  486.1 23.0 %collective-permute-start.28 = (bf16[96,3072]{1,0:T(8,128)(2,1)}, bf16[96,3072]{1,0:T(8,128)(2,1)}, u32[]{:S(2)}, u32[]{:S(2)}) collective-permute-start(bf16[96,3072]{1,0:T(8,128)(2,1)} %fusion.9), channel_id=1, source_target_pairs={{0,4},{4,0},{8,12},{12,8},{16,20},{20,16},{24,28},{28,24},{1,5},{5... | collective-permute-start | bytes 1769480 | tf_op jit(solution)/shard_map/ppermute | solution.py:540
  486.8 5.9 %collective-permute-start.15 = (bf16[24,2304]{1,0:T(8,128)(2,1)S(1)}, bf16[24,2304]{1,0:T(8,128)(2,1)S(1)}, u32[]{:S(2)}, u32[]{:S(2)}) collective-permute-start(bf16[24,2304]{1,0:T(8,128)(2,1)S(1)} %reduce_sum.75), channel_id=1, source_target_pairs={{0,8},{4,12},{8,0},{12,4},{16,24},{20,28},{24,16},{28,20},{1,9},{5... | collective-permute-start | bytes 331784 | tf_op jit(solution)/shard_map/ppermute | solution.py:540
  487.5 7.6 %collective-permute-start.16 = (bf16[24,2304]{1,0:T(8,128)(2,1)S(1)}, bf16[24,2304]{1,0:T(8,128)(2,1)S(1)}, u32[]{:S(2)}, u32[]{:S(2)}) collective-permute-start(bf16[24,2304]{1,0:T(8,128)(2,1)S(1)} %reduce_sum.75), channel_id=1, source_target_pairs={{0,16},{4,20},{8,24},{12,28},{16,0},{20,4},{24,8},{28,12},{1,17},{... | collective-permute-start | bytes 331784 | tf_op jit(solution)/shard_map/ppermute | solution.py:540
  488.5 10.1 %collective-permute-start.17 = (bf16[24,2304]{1,0:T(8,128)(2,1)S(1)}, bf16[24,2304]{1,0:T(8,128)(2,1)S(1)}, u32[]{:S(2)}, u32[]{:S(2)}) collective-permute-start(bf16[24,2304]{1,0:T(8,128)(2,1)S(1)} %reduce_sum.75), channel_id=1, source_target_pairs={{0,24},{4,28},{8,16},{12,20},{16,8},{20,12},{24,0},{28,4},{1,25},{... | collective-permute-start | bytes 331784 | tf_op jit(solution)/shard_map/ppermute | solution.py:540
  499.2 26.3 %collective-permute-start.18 = (bf16[96,2304]{1,0:T(8,128)(2,1)}, bf16[96,2304]{1,0:T(8,128)(2,1)}, u32[]{:S(2)}, u32[]{:S(2)}) collective-permute-start(bf16[96,2304]{1,0:T(8,128)(2,1)} %bitcast.19), channel_id=1, source_target_pairs={{0,4},{4,0},{8,12},{12,8},{16,20},{20,16},{24,28},{28,24},{1,5},{5... | collective-permute-start | bytes 1327112 | tf_op jit(solution)/shard_map/ppermute | solution.py:540
  503.0 16.3 %all-to-all-start.9 = ((bf16[4,96,768]{2,1,0:T(8,128)(2,1)}), bf16[4,96,768]{2,1,0:T(8,128)(2,1)}, u32[]{:S(2)}, u32[]{:S(2)}) async-start(bf16[4,96,768]{2,1,0:T(8,128)(2,1)} %bitcast.56), calls=%async_computation.9 | async-start | bytes 1179648 | tf_op jit(solution)/shard_map/all_to_all | solution.py:580
  519.4 25.3 %all-to-all-start.7 = ((bf16[4,24,3072]{2,1,0:T(8,128)(2,1)}), bf16[4,24,3072]{2,1,0:T(8,128)(2,1)S(1)}, u32[]{:S(2)}, u32[]{:S(2)}) async-start(bf16[4,24,3072]{2,1,0:T(8,128)(2,1)} %bitcast.157), calls=%async_computation.7 | async-start | bytes 1179648 | tf_op jit(solution)/shard_map/all_to_all | solution.py:580
  529.1 22.7 %collective-permute-start.36 = (bf16[96,768]{1,0:T(8,128)(2,1)S(1)}, bf16[96,768]{1,0:T(8,128)(2,1)S(1)}, u32[]{:S(2)}, u32[]{:S(2)}) collective-permute-start(bf16[96,768]{1,0:T(8,128)(2,1)S(1)} %reduce_sum.80), channel_id=1, source_target_pairs={{0,8},{4,12},{8,0},{12,4},{16,24},{20,28},{24,16},{28,20},{1,9},{5... | collective-permute-start | bytes 442376 | tf_op jit(solution)/shard_map/ppermute | solution.py:540
  529.2 23.2 %collective-permute-start.37 = (bf16[96,768]{1,0:T(8,128)(2,1)S(1)}, bf16[96,768]{1,0:T(8,128)(2,1)S(1)}, u32[]{:S(2)}, u32[]{:S(2)}) collective-permute-start(bf16[96,768]{1,0:T(8,128)(2,1)S(1)} %reduce_sum.80), channel_id=1, source_target_pairs={{0,16},{4,20},{8,24},{12,28},{16,0},{20,4},{24,8},{28,12},{1,17},{... | collective-permute-start | bytes 442376 | tf_op jit(solution)/shard_map/ppermute | solution.py:540
  532.1 25.6 %collective-permute-start.38 = (bf16[96,768]{1,0:T(8,128)(2,1)S(1)}, bf16[96,768]{1,0:T(8,128)(2,1)S(1)}, u32[]{:S(2)}, u32[]{:S(2)}) collective-permute-start(bf16[96,768]{1,0:T(8,128)(2,1)S(1)} %reduce_sum.80), channel_id=1, source_target_pairs={{0,24},{4,28},{8,16},{12,20},{16,8},{20,12},{24,0},{28,4},{1,25},{... | collective-permute-start | bytes 442376 | tf_op jit(solution)/shard_map/ppermute | solution.py:540
  544.8 13.7 %collective-permute-start.29 = (bf16[24,3072]{1,0:T(8,128)(2,1)S(1)}, bf16[24,3072]{1,0:T(8,128)(2,1)S(1)}, u32[]{:S(2)}, u32[]{:S(2)}) collective-permute-start(bf16[24,3072]{1,0:T(8,128)(2,1)S(1)} %reduce_sum.77), channel_id=1, source_target_pairs={{0,8},{4,12},{8,0},{12,4},{16,24},{20,28},{24,16},{28,20},{1,9},{5... | collective-permute-start | bytes 442376 | tf_op jit(solution)/shard_map/ppermute | solution.py:540
  546.1 14.9 %collective-permute-start.30 = (bf16[24,3072]{1,0:T(8,128)(2,1)S(1)}, bf16[24,3072]{1,0:T(8,128)(2,1)S(1)}, u32[]{:S(2)}, u32[]{:S(2)}) collective-permute-start(bf16[24,3072]{1,0:T(8,128)(2,1)S(1)} %reduce_sum.77), channel_id=1, source_target_pairs={{0,16},{4,20},{8,24},{12,28},{16,0},{20,4},{24,8},{28,12},{1,17},{... | collective-permute-start | bytes 442376 | tf_op jit(solution)/shard_map/ppermute | solution.py:540
  551.8 12.7 %collective-permute-start.31 = (bf16[24,3072]{1,0:T(8,128)(2,1)S(1)}, bf16[24,3072]{1,0:T(8,128)(2,1)S(1)}, u32[]{:S(2)}, u32[]{:S(2)}) collective-permute-start(bf16[24,3072]{1,0:T(8,128)(2,1)S(1)} %reduce_sum.77), channel_id=1, source_target_pairs={{0,24},{4,28},{8,16},{12,20},{16,8},{20,12},{24,0},{28,4},{1,25},{... | collective-permute-start | bytes 442376 | tf_op jit(solution)/shard_map/ppermute | solution.py:540
  557.7 14.8 %collective-permute-start.39 = (bf16[384,768]{1,0:T(8,128)(2,1)S(1)}, bf16[384,768]{1,0:T(8,128)(2,1)S(1)}, u32[]{:S(2)}, u32[]{:S(2)}) collective-permute-start(bf16[384,768]{1,0:T(8,128)(2,1)S(1)} %bitcast.158), channel_id=1, source_target_pairs={{0,4},{4,0},{8,12},{12,8},{16,20},{20,16},{24,28},{28,24},{1,5},{5... | collective-permute-start | bytes 1769480 | tf_op jit(solution)/shard_map/ppermute | solution.py:540
  564.6 17.5 %collective-permute-start.32 = (bf16[96,3072]{1,0:T(8,128)(2,1)S(1)}, bf16[96,3072]{1,0:T(8,128)(2,1)S(1)}, u32[]{:S(2)}, u32[]{:S(2)}) collective-permute-start(bf16[96,3072]{1,0:T(8,128)(2,1)S(1)} %bitcast.160), channel_id=1, source_target_pairs={{0,4},{4,0},{8,12},{12,8},{16,20},{20,16},{24,28},{28,24},{1,5},{5... | collective-permute-start | bytes 1769480 | tf_op jit(solution)/shard_map/ppermute | solution.py:540
  (28 other events, 208.9 us)
Sparse Core Ops, SparseCore 0:
  16.8 32.3 all-reduce.5
  282.5 70.9 all-reduce.7

commit v2 on v1

v2 whole, which is shorter than its diff:
```python
from functools import partial
import math

import jax
import jax.numpy as jnp
from jax import lax
from jax.experimental import pallas as pl
from jax.experimental.pallas import tpu as pltpu
from jax.sharding import PartitionSpec as P

HEADS = 12
EPSILON = 1e-05
LANES = 128
VMEM = 60 * 1024 * 1024
LOW = jnp.bfloat16
FULL = jnp.float32


def matmul(left, right, left_dim=1, right_dim=0):
    dims = (((left_dim,), (right_dim,)), ((), ()))
    return lax.dot_general(left, right, dims, preferred_element_type=FULL)


def call(body, name, grid, in_specs, out_specs, out_shape, scratch, flops, args, moved):
    return pl.pallas_call(
        body,
        name=name,
        grid_spec=pltpu.PrefetchScalarGridSpec(
            num_scalar_prefetch=1,
            grid=grid,
            in_specs=in_specs,
            out_specs=out_specs,
            scratch_shapes=scratch,
        ),
        out_shape=out_shape,
        compiler_params=pltpu.CompilerParams(
            dimension_semantics=("arbitrary",) * len(grid), vmem_limit_bytes=VMEM
        ),
        cost_estimate=pl.CostEstimate(flops=1024, bytes_accessed=1024, transcendentals=0),
    )(*args)


def whole(shape):
    zeros = (0,) * len(shape)
    return pl.BlockSpec(shape, lambda *_: zeros, pipeline_mode=pl.Buffered(1))


def kept(shape):
    zeros = (0,) * len(shape)
    return pl.BlockSpec(shape, lambda *_: zeros)


def assemble(at, target, pieces):
    me, b = at[0], at[1]
    own, core, across, handed, core_across, core_handed = pieces
    rows = target.shape[0] // 8
    width = across.shape[-1]
    halves = (
        (me, 0, lambda cut: own[0, cut, :]),
        (me, 1, lambda cut: own[1, cut, :]),
        (me ^ 1, 0, lambda cut: core[0, cut, :]),
        (me ^ 1, 1, lambda cut: core[1, cut, :]),
        (me ^ 2, b, lambda cut: across[cut, :]),
        (me ^ 2, 1 - b, lambda cut: handed[cut, :]),
        (me ^ 3, b, lambda cut: core_across[cut, :]),
        (me ^ 3, 1 - b, lambda cut: core_handed[cut, :]),
    )
    for shard, half, read in halves:
        place = pl.ds(pl.multiple_of((2 * shard + half) * rows, 16), rows)
        for k in range(target.shape[1] // width):
            cut = slice(k * rows, (k + 1) * rows)
            target[place, k * width : (k + 1) * width] = read(cut)


def stack_halves(target, pack):
    rows = target.shape[0] // 8
    for j in range(4):
        for k in range(2):
            low = (2 * j + k) * rows
            target[low : low + rows, :] = pack[4 * k + j]


def merge_spec(pack, width):
    rows = width // 8
    at = pack.shape[1] // rows - 1
    return pl.BlockSpec((8, rows, width), lambda *_: (0, at, 0), pipeline_mode=pl.Buffered(1))


def split_rows(me, value, keep, send):
    rows = value.shape[0] // 4
    mine_x, mine_c = me >> 1, me & 1
    for j in range(4):
        part = value[j * rows : (j + 1) * rows].astype(LOW)[None]
        at = (j >> 1) ^ mine_x

        @pl.when(mine_c == (j & 1))
        def _(part=part, at=at):
            keep[pl.ds(at, 1)] = part

        @pl.when(mine_c != (j & 1))
        def _(part=part, at=at):
            send[pl.ds(at, 1)] = part


def normalize(values):
    center = values - jnp.mean(values, axis=-1, keepdims=True)
    inverse = lax.rsqrt(jnp.mean(center * center, axis=-1, keepdims=True) + EPSILON)
    return center * inverse, inverse


def unnormalize(weighted, unit, inverse):
    first = jnp.mean(weighted, axis=-1, keepdims=True)
    second = jnp.mean(weighted * unit, axis=-1, keepdims=True)
    return inverse * (weighted - first - unit * second)


def lower_half(head):
    lane = lax.broadcasted_iota(jnp.int32, (1, LANES), 1)
    return (lane & (head - 1)) < head // 2


def column_sum(values):
    return jnp.sum(values, axis=0, keepdims=True)


def project_kernel(head, me_ref, hidden, vectors, p0, p1, p2, p3, p4, p5, cosine, sine, adapted, query, key, value, weight):
    @pl.when(pl.program_id(0) == 0)
    def _():
        assemble(me_ref, weight, (p0, p1, p2, p3, p4, p5))

    unit, _ = normalize(hidden[...].astype(FULL))
    low = (unit * vectors[0:1, :] * vectors[1:2, :] + vectors[2:3, :]).astype(LOW)
    adapted[...] = low
    width = low.shape[1]
    cos, sin = cosine[...], sine[...]
    under = lower_half(head)
    signed = jnp.where(under, -sin, sin)
    scale = 1.0 / math.sqrt(head)
    for which, target in enumerate((query, key)):
        part = matmul(low, weight[:, which * width : (which + 1) * width])
        for j in range(width // LANES):
            block = part[:, j * LANES : (j + 1) * LANES]
            turned = jnp.where(
                under,
                pltpu.roll(block, LANES - head // 2, 1),
                pltpu.roll(block, head // 2, 1),
            )
            turned = (block * cos + turned * signed).astype(LOW)
            if which == 0:
                turned = turned * jnp.asarray(scale, LOW)
            target[:, j * LANES : (j + 1) * LANES] = turned
    value[...] = matmul(low, weight[:, 2 * width :]).astype(LOW)


def project(me, hidden, vectors, pieces, cosine, sine, head):
    length, width = hidden.shape
    step = 256
    rows = pl.BlockSpec((step, width), lambda i, _: (i, 0))
    angle = pl.BlockSpec((step, LANES), lambda i, _: (i, 0))
    out = jax.ShapeDtypeStruct((length, width), LOW)
    return call(
        partial(project_kernel, head),
        "project",
        (length // step,),
        [rows, whole(vectors.shape)] + [whole(p.shape) for p in pieces] + [angle, angle],
        [rows] * 4,
        [out] * 4,
        [pltpu.VMEM((width, 3 * width), LOW)],
        2 * length * width * 3 * width,
        (me, hidden, vectors, *pieces, cosine, sine),
        2 * length * width * 8,
    )


def attend_kernel(step, head, me_ref, query, key, value, mixed, logsum):
    lane = lax.broadcasted_iota(jnp.int32, (1, LANES), 1)
    first = lane < head
    keys, values = key[...], value[...]
    zero = jnp.zeros_like(keys)
    split = (jnp.where(first, keys, zero), jnp.where(first, zero, keys))
    for i in range(query.shape[0] // step):
        at = slice(i * step, (i + 1) * step)
        block = query[at, :]
        outs, sums = [], []
        for h in range(2):
            scores = matmul(block, split[h], 1, 1)
            peak = jnp.max(scores, axis=1, keepdims=True)
            expos = jnp.exp(scores - peak)
            total = jnp.sum(expos, axis=1, keepdims=True)
            outs.append(matmul(expos.astype(LOW), values) * (1.0 / total))
            sums.append(peak + jnp.log(total))
        mixed[at, :] = jnp.where(first, outs[0], outs[1]).astype(LOW)
        turned = jnp.where(first, sums[0], sums[1]).T
        logsum[0, 0:1, at] = turned[0:1, :]
        logsum[0, 1:2, at] = turned[head : head + 1, :]


def attend(me, query, key, value, head, start, pairs):
    length = query.shape[0]
    width = pairs * LANES
    block = pl.BlockSpec((length, LANES), lambda i, _: (0, i + start))
    own = pl.BlockSpec((length, LANES), lambda i, _: (0, i))
    return call(
        partial(attend_kernel, 512, head),
        "attend",
        (pairs,),
        [block] * 3,
        [own, pl.BlockSpec((1, 2, length), lambda i, _: (i, 0, 0))],
        [
            jax.ShapeDtypeStruct((length, width), LOW),
            jax.ShapeDtypeStruct((pairs, 2, length), FULL),
        ],
        [],
        16 * length * length * width,
        (me, query, key, value),
        2 * length * width * 4,
    )


def blend(parts, weight):
    total, at = None, 0
    for part in parts:
        size = part.shape[1]
        term = matmul(part[...], weight[at : at + size, :])
        total = term if total is None else total + term
        at += size
    return total


def merge_kernel(me_ref, m0, m1, hidden, vectors, pack, middle, adapted, weight):
    @pl.when(pl.program_id(0) == 0)
    def _():
        stack_halves(weight, pack)

    branch = blend((m0, m1), weight)
    mid = hidden[...].astype(FULL) + vectors[0:1, :] * branch
    middle[...] = mid
    unit, _ = normalize(mid)
    adapted[...] = (unit * vectors[1:2, :] * vectors[2:3, :] + vectors[3:4, :]).astype(LOW)


def merge(me, mixed, hidden, vectors, pack):
    length, width = hidden.shape
    step = 256
    rows = pl.BlockSpec((step, width), lambda i, _: (i, 0))
    some = [pl.BlockSpec((step, m.shape[1]), lambda i, _: (i, 0)) for m in mixed]
    return call(
        merge_kernel,
        "merge",
        (length // step,),
        some + [rows, whole(vectors.shape), merge_spec(pack, width)],
        [rows, rows],
        [jax.ShapeDtypeStruct((length, width), FULL), jax.ShapeDtypeStruct((length, width), LOW)],
        [pltpu.VMEM((width, width), LOW)],
        2 * length * width * width,
        (me, *mixed, hidden, vectors, pack),
        2 * length * width * 6,
    )


def feed_kernel(last, at_ref, adapted, upstream, vectors, lift_bias, pack, *refs):
    if last:
        low_in, grad_in, middle, block_out, adapted_grad, sums, liftbias_grad, grads = refs[:8]
        lift, turned, lowered_grad, lowered, low_got, grad_got, middle_got, sem = refs[8:]
        copies = [
            pltpu.make_async_copy(source, target, sem.at[k])
            for k, (source, target) in enumerate(
                ((low_in, low_got), (grad_in, grad_got), (middle, middle_got))
            )
        ]
        for copy in copies:
            copy.start()
    else:
        lowered, adapted_grad, liftbias_grad, grads = refs[:4]
        lift, turned, lowered_grad = refs[4:]
    gate = vectors[0:1, :]
    rows = lift.shape[0] // 4
    step = lift.shape[1] // 2
    turned[...] = adapted[...].T
    lowered_grad[...] = (gate * upstream[...].astype(FULL)).astype(LOW)
    for i in range(2):
        deep = slice(step + i * rows, step + (i + 1) * rows)
        half_rows, half_step = rows // 2, step // 2
        for j in range(4):
            for k in range(2):
                low = (2 * j + k) * half_rows
                at = half_step + i * half_rows
                lift[low : low + half_rows, :] = pack[4 * k + j, at : at + half_rows, :]
        weight_up = lift[...]
        weight_down = jnp.concatenate(
            [pack[4 * k + j, :half_step, :] for j in (2 * i, 2 * i + 1) for k in range(2)], axis=0
        )
        across = slice(2 * i * step, 2 * (i + 1) * step)
        upper = matmul(adapted[...], weight_up) + lift_bias[:, across]
        square = upper * upper
        root = math.sqrt(2.0 / math.pi)
        bent = jnp.tanh(upper * (root + root * 0.044715 * square))
        half = 0.5 + 0.5 * bent
        slope = half + upper * (0.5 - 0.5 * bent * bent) * (root + 3.0 * root * 0.044715 * square)
        active = (upper * half).astype(LOW)
        low_part = matmul(active, weight_down)
        down = lowered_grad[...]
        upper_grad = (matmul(down, weight_down, 1, 1) * slope).astype(LOW)
        grad_part = matmul(upper_grad, weight_up, 1, 1)
        if i == 0:
            lowered[...] = low_part
            adapted_grad[...] = grad_part
        else:
            lowered[...] += low_part
            adapted_grad[...] += grad_part
        liftbias_grad[:, across] = column_sum(upper_grad.astype(FULL))
        drop_part = matmul(active, down, 0, 0).astype(LOW)
        for k in range(2):
            grads[2 * i + k, :step, :] = drop_part[k * step : (k + 1) * step]
        lift_part = matmul(turned[...], upper_grad).astype(LOW)
        for j in range(4):
            grads[j, deep, :] = lift_part[j * rows : (j + 1) * rows]

    if last:
        for copy in copies:
            copy.wait()
        adapted_grad[...] += grad_got[...]
        total = lowered[...] + low_got[...] + vectors[1:2, :]
        block_out[...] = (middle_got[...] + gate * total).astype(LOW)
        sums[0:1, :] = column_sum(upstream[...].astype(FULL) * total)
        sums[1:2, :] = column_sum(lowered_grad[...].astype(FULL))


def feed(me, adapted, upstream, vectors, lift_bias, pack, which, before=()):
    length, width = adapted.shape
    last = len(before) > 0
    units = lift_bias.shape[1]
    wide = jax.ShapeDtypeStruct((length, width), FULL)
    low = jax.ShapeDtypeStruct((length, width), LOW)
    more = jax.ShapeDtypeStruct((4, units // 2, width), LOW)
    sums = jax.ShapeDtypeStruct((8, width), FULL)
    bias = jax.ShapeDtypeStruct((1, units), FULL)
    outs = [low, wide, sums, bias, more] if last else [wide, wide, bias, more]
    scratch = [
        pltpu.VMEM((width, units // 2), LOW),
        pltpu.VMEM((width, length), LOW),
        pltpu.VMEM((length, width), LOW),
    ]
    if last:
        scratch += [pltpu.VMEM((length, width), FULL)] * 4 + [pltpu.SemaphoreType.DMA((3,))]
    return call(
        partial(feed_kernel, last),
        "feed",
        (1,),
        [whole(a.shape) for a in (adapted, upstream, vectors, lift_bias)]
        + [
            pl.BlockSpec(
                (8, units // 4, width), lambda *_: (0, which, 0), pipeline_mode=pl.Buffered(1)
            )
        ]
        + [pl.BlockSpec(memory_space=pl.ANY) for _ in before],
        [whole(o.shape) for o in outs],
        outs,
        scratch,
        12 * length * width * units,
        (me, adapted, upstream, vectors, lift_bias, pack, *before),
        8 * width * units + 24 * length * width,
    )


def unmerge_kernel(
    me_ref, adapted_grad, middle, upstream, m0, m1, vectors, pack,
    middle_grad, mixed_grad, sums, keep, send, weight, total,
):
    i = pl.program_id(0)

    @pl.when(i == 0)
    def _():
        stack_halves(weight, pack)
        total[...] = jnp.zeros_like(total)
        sums[...] = jnp.zeros_like(sums)

    gate, gain, grow = vectors[0:1, :], vectors[1:2, :], vectors[2:3, :]
    unit, inverse = normalize(middle[...])
    grad = adapted_grad[...]
    sums[0:1, :] += column_sum(grad)
    sums[1:2, :] += column_sum(grad * (unit * gain))
    normed_grad = grad * grow
    sums[2:3, :] += column_sum(normed_grad * unit)
    mid_grad = upstream[...].astype(FULL) + unnormalize(normed_grad * gain, unit, inverse)
    middle_grad[...] = mid_grad
    sums[3:4, :] += column_sum(mid_grad * blend((m0, m1), weight))
    branch_grad = (gate * mid_grad).astype(LOW)
    at = 0
    for part in (m0, m1):
        size = part.shape[1]
        total[at : at + size, :] += matmul(part[...], branch_grad, 0, 0)
        at += size
    mixed_grad[...] = matmul(branch_grad, weight[...], 1, 1).astype(LOW)

    @pl.when(i == pl.num_programs(0) - 1)
    def _():
        split_rows(me_ref[0], total[...], keep, send)


def unmerge(me, adapted_grad, middle, upstream, mixed, vectors, pack):
    length, width = middle.shape
    step = 256
    rows = pl.BlockSpec((step, width), lambda i, _: (i, 0))
    some = [pl.BlockSpec((step, m.shape[1]), lambda i, _: (i, 0)) for m in mixed]
    part = (2, width // 4, width)
    return call(
        unmerge_kernel,
        "unmerge",
        (length // step,),
        [rows] * 3 + some + [whole(vectors.shape), merge_spec(pack, width)],
        [rows, rows, kept((8, width)), kept(part), kept(part)],
        [
            jax.ShapeDtypeStruct((length, width), FULL),
            jax.ShapeDtypeStruct((length, width), LOW),
            jax.ShapeDtypeStruct((8, width), FULL),
            jax.ShapeDtypeStruct(part, LOW),
            jax.ShapeDtypeStruct(part, LOW),
        ],
        [pltpu.VMEM((width, width), LOW), pltpu.VMEM((width, width), FULL)],
        6 * length * width * width,
        (me, adapted_grad, middle, upstream, *mixed, vectors, pack),
        2 * length * width * 12,
    )


def unattend_kernel(step, head, me_ref, query, key, value, mixed, mixed_grad, logsum, cosine, sine, grads, query_sum, key_sum, value_sum):
    lane = lax.broadcasted_iota(jnp.int32, (1, LANES), 1)
    first = lane < head
    keys, values = key[...], value[...]
    zero = jnp.zeros_like(keys)
    keys_h = (jnp.where(first, keys, zero), jnp.where(first, zero, keys))
    values_h = (jnp.where(first, values, zero), jnp.where(first, zero, values))
    turned = keys.T
    scale = 1.0 / math.sqrt(head)
    for i in range(query.shape[0] // step):
        at = slice(i * step, (i + 1) * step)
        block, grad = query[at, :], mixed_grad[at, :]
        product = (grad.astype(FULL) * mixed[at, :].astype(FULL)).T
        queries, values_new, keys_new = [], [], []
        for h in range(2):
            center = jnp.sum(product[h * head : (h + 1) * head], axis=0, keepdims=True)
            probs = jnp.exp(matmul(keys_h[h], block, 1, 1) - logsum[0, h : h + 1, at])
            probs_grad = matmul(values_h[h], grad, 1, 1)
            scores_grad = (probs * (probs_grad - center)).astype(LOW)
            values_new.append(matmul(probs.astype(LOW), grad))
            keys_new.append(matmul(scores_grad, block))
            queries.append(matmul(turned[h * head : (h + 1) * head], scores_grad))
        query_sum[at, :] = jnp.concatenate(queries, axis=0).T * scale
        key_part = jnp.where(first, keys_new[0], keys_new[1])
        value_part = jnp.where(first, values_new[0], values_new[1])
        if i == 0:
            key_sum[...] = key_part
            value_sum[...] = value_part
        else:
            key_sum[...] += key_part
            value_sum[...] += value_part
    under = lower_half(head)
    cos, sin = cosine[...], sine[...]
    for which, total in enumerate((query_sum, key_sum)):
        rotated = total[...]
        swept = rotated * sin
        back = jnp.where(
            under, pltpu.roll(swept, LANES - head // 2, 1), -pltpu.roll(swept, head // 2, 1)
        )
        grads[which] = (rotated * cos + back).astype(LOW)
    grads[2] = value_sum[...].astype(LOW)


def unattend(me, query, key, value, mixed, mixed_grad, logsum, cosine, sine, head, start):
    length, width = mixed.shape
    pairs = width // LANES
    block = pl.BlockSpec((length, LANES), lambda i, _: (0, i + start))
    own = pl.BlockSpec((length, LANES), lambda i, _: (0, i))
    return call(
        partial(unattend_kernel, 256, head),
        "unattend",
        (pairs,),
        [block] * 3
        + [own, block]
        + [pl.BlockSpec((1, 2, length), lambda i, _: (i, 0, 0))]
        + [whole((length, LANES))] * 2,
        [pl.BlockSpec((3, length, LANES), lambda i, _: (0, 0, i))],
        [jax.ShapeDtypeStruct((3, length, width), LOW)],
        [pltpu.VMEM((length, LANES), FULL)] * 3,
        40 * length * length * width,
        (me, query, key, value, mixed, mixed_grad, logsum, cosine, sine),
        2 * length * width * 8,
    )[0]


def weigh_kernel(me_ref, adapted, grads, *refs):
    keep, send, turned = refs[-3:]
    i = pl.program_id(0)

    @pl.when(i == 0)
    def _():
        turned[...] = adapted[...].T

    @pl.when(i < 3)
    def _():
        split_rows(me_ref[0], matmul(turned[...], grads[0]), keep, send)

    if len(refs) > 3:

        @pl.when(i >= 3)
        def _():
            keep[...] = refs[0][...]
            send[...] = refs[1][...]


def weigh(me, adapted, grads, extra=()):
    length, width = adapted.shape
    step = grads.shape[2]
    more = extra[0].shape[2] // step if extra else 0
    part = pl.BlockSpec((2, width // 4, step), lambda i, _: (0, 0, i))
    rider = pl.BlockSpec((2, width // 4, step), lambda i, _: (0, 0, jnp.maximum(i - 3, 0)))
    shape = jax.ShapeDtypeStruct((2, width // 4, (3 + more) * step), LOW)
    return call(
        weigh_kernel,
        "weigh",
        (3 + more,),
        [whole(adapted.shape), pl.BlockSpec((1, length, step), lambda i, _: (jnp.minimum(i, 2), 0, 0))]
        + [rider] * len(extra),
        [part, part],
        [shape, shape],
        [pltpu.VMEM((width, length), LOW)],
        6 * length * width * step,
        (me, adapted, grads, *extra),
        2 * length * width * 7,
    )


def unproject_kernel(me_ref, g0, g1, hidden, middle_grad, vectors, p0, p1, p2, p3, p4, p5, o0, o1, o2, o3, sums, weight):
    i = pl.program_id(0)

    @pl.when(i == 0)
    def _():
        assemble(me_ref, weight, (p0, p1, p2, p3, p4, p5))
        sums[...] = jnp.zeros_like(sums)

    gain, grow = vectors[0:1, :], vectors[1:2, :]
    width = hidden.shape[1]
    grad, at = None, 0
    for part in (g0, g1):
        size = part.shape[2]
        for which in range(3):
            low = which * width + at
            term = matmul(part[which], weight[:, low : low + size], 1, 1)
            grad = term if grad is None else grad + term
        at += size
    unit, inverse = normalize(hidden[...].astype(FULL))
    sums[0:1, :] += column_sum(grad)
    sums[1:2, :] += column_sum(grad * (unit * gain))
    normed_grad = grad * grow
    sums[2:3, :] += column_sum(normed_grad * unit)
    low = (middle_grad[...] + unnormalize(normed_grad * gain, unit, inverse)).astype(LOW)
    for d, target in enumerate((o0, o1, o2, o3)):

        @pl.when(i == me_ref[0] ^ d)
        def _(target=target):
            target[...] = low


def unproject(me, grads, hidden, middle_grad, vectors, pieces):
    length, width = hidden.shape
    step = length // 4
    rows = pl.BlockSpec((step, width), lambda i, _: (i, 0))
    return call(
        unproject_kernel,
        "unproject",
        (length // step,),
        [pl.BlockSpec((3, step, g.shape[2]), lambda i, _: (0, i, 0)) for g in grads]
        + [rows, rows, whole(vectors.shape)]
        + [whole(p.shape) for p in pieces],
        [kept((step, width))] * 4 + [kept((8, width))],
        [jax.ShapeDtypeStruct((step, width), LOW)] * 4 + [jax.ShapeDtypeStruct((8, width), FULL)],
        [pltpu.VMEM((width, 3 * width), LOW)],
        6 * length * width * width,
        (me, *grads, hidden, middle_grad, vectors, *pieces),
        2 * length * width * 10,
    )


def lay_kernel(me_ref, *refs):
    for d, part in enumerate(refs[:-1]):
        refs[-1][pl.ds(me_ref[0] ^ d, 1)] = part[...][None]


def lay(me, parts):
    shape = (len(parts),) + parts[0].shape
    return call(
        lay_kernel, "lay", (1,), [whole(p.shape) for p in parts], [whole(shape)],
        [jax.ShapeDtypeStruct(shape, LOW)], [], 1024, (me, *parts), 1024,
    )[0]


def swap(array, axis, distance):
    size = lax.axis_size(axis)
    return lax.ppermute(array, axis, [(i, i ^ distance) for i in range(size)])


def fence(*trees):
    return lax.optimization_barrier(trees)


def bit(axis, distance):
    return (lax.axis_index(axis) // distance) % 2


def choose(parts, at):
    return lax.dynamic_index_in_dim(parts, at, 0, keepdims=False)


def choose_all(array, place):
    count = array.shape[0]
    return jnp.stack([choose(array, place ^ k) for k in range(count)])


def payload(parts):
    return jnp.concatenate([p.reshape(2, p.shape[0] // 2, p.shape[1]) for p in parts], axis=1)


def blocks_of(weight, width):
    return [weight[:, k : k + width] for k in range(0, weight.shape[1], width)]


def powers(size):
    return [1 << k for k in range(size.bit_length() - 1)]


def gather_small(array, axis, distances):
    array = array[None]
    done = []
    for distance in distances:
        other = swap(array, axis, distance)
        at = bit(axis, distance)
        place = sum(d > distance for d in done)
        lead = [2] * place
        shape = array.shape
        pair = [a.reshape(lead + [1, -1] + list(shape[1:])) for a in (array, other)]
        array = jnp.where(
            at == 0, jnp.concatenate(pair, place), jnp.concatenate(pair[::-1], place)
        ).reshape((2 * shape[0],) + shape[1:])
        done.append(distance)
    return array


def plus(*terms):
    total = terms[0].astype(FULL)
    for term in terms[1:]:
        total = total + term.astype(FULL)
    return total.astype(LOW)


def pair_kernel(at_ref, kept_term, got, mine, other):
    mine[...] = plus(kept_term[0], got[0])
    other[...] = plus(kept_term[1], got[1])


def sum_pair(kept_term, got):
    _, rows, columns = kept_term.shape
    step = rows // 4
    two = pl.BlockSpec((2, step, columns), lambda i, _: (0, i, 0))
    one = pl.BlockSpec((step, columns), lambda i, _: (i, 0))
    out = jax.ShapeDtypeStruct((rows, columns), LOW)
    return call(
        pair_kernel, "pair", (4,), [two, two], [one, one], [out, out], [], 1024,
        (jnp.zeros((1,), jnp.int32), kept_term, got), 1024,
    )


def blend_kernel(at_ref, a, b, c, d, both):
    cut = a.shape[1]
    both[:, :cut] = plus(a[...], b[...])
    both[:, cut:] = plus(c[...], d[...])


def sum_beside(first, second):
    args = (*first, *second)
    rows = args[0].shape[0]
    out = (rows, args[0].shape[1] + args[2].shape[1])
    return call(
        blend_kernel, "beside", (1,), [whole(a.shape) for a in args], [whole(out)],
        [jax.ShapeDtypeStruct(out, LOW)], [], 1024, (jnp.zeros((1,), jnp.int32), *args), 1024,
    )[0]


def deal(term):
    size = lax.axis_size("dp")
    rows, columns = term.shape
    parts = term.reshape(size, rows // size, columns)
    return lax.all_to_all(parts, "dp", 0, 0, tiled=True)


def add_kernel(at_ref, parts, total):
    total[...] = plus(*[parts[k] for k in range(parts.shape[0])])


def add_up(parts):
    shape = parts.shape[1:]
    return call(
        add_kernel, "add", (1,), [whole(parts.shape)], [whole(shape)],
        [jax.ShapeDtypeStruct(shape, LOW)], [], 1024, (jnp.zeros((1,), jnp.int32), parts), 1024,
    )[0]


def place_of(distance):
    return bit("dp", distance).astype(jnp.int32).reshape(1)


def join_kernel(at_ref, first, second, both):
    b = at_ref[0]
    both[pl.ds(b, 1)] = first[...][None]
    both[pl.ds(1 - b, 1)] = second[...][None]


def join(first, second, distance):
    rows, columns = first.shape
    shape = (2, rows, columns)
    return call(
        join_kernel, "join", (1,), [whole(first.shape)] * 2, [whole(shape)],
        [jax.ShapeDtypeStruct(shape, LOW)], [], 1024, (place_of(distance), first, second), 1024,
    )[0].reshape(2 * rows, columns)


def spread(term, got, distances):
    for k, distance in enumerate(distances[:-1]):
        term = join(term, got, distance)
        got = swap(term, "dp", distances[k + 1])
    return term, got


def settle_kernel(plan, size, at_ref, *refs):
    count = len(plan)
    outs = refs[2 * count :]
    depth = size.bit_length() - 1
    b = at_ref[0]
    for p, moves in enumerate(plan):
        rows = 2 * refs[2 * p].shape[0] // size
        for h in range(2):
            value = jnp.where(b == h, refs[2 * p][...], refs[2 * p + 1][...]).astype(FULL)
            for k in range(h, size, 2):
                at = sum(((k >> j) & 1) << (depth - 1 - j) for j in range(1, depth)) * rows
                for top, left, down, wide, out, to_row, to_column in moves:
                    low, high = max(top, k * rows), min(top + down, (k + 1) * rows)
                    if low < high:
                        start = to_row + low - top
                        source = at + low - k * rows
                        outs[out][start : start + high - low, to_column : to_column + wide] = value[
                            source : source + high - low, left : left + wide
                        ]


def settle(pairs, plan, shapes):
    args = [array for pair in pairs for array in pair]
    return call(
        partial(settle_kernel, plan, lax.axis_size("dp")),
        "settle",
        (1,),
        [whole(a.shape) for a in args],
        [whole(shape) for shape in shapes],
        [jax.ShapeDtypeStruct(shape, FULL) for shape in shapes],
        [],
        1024,
        (place_of(1), *args),
        1024,
    )


def shards(
    hidden_in,
    time_table,
    time_step,
    token_pos,
    heads_weight,
    merge_weight,
    lift_weight,
    lift_bias,
    drop_weight,
    drop_bias,
    modulate_weight,
    modulate_bias,
    first_gain,
    second_gain,
    out_grad,
):
    count = lax.axis_size("seq")
    place = lax.axis_index("seq")
    seqs, span, width = hidden_in.shape
    assert count == 4 and seqs == count
    length = span * count
    head = width // HEADS
    bits = powers(lax.axis_size("dp"))
    row_half = bit("dp", 1)
    me = jnp.stack([place, row_half]).astype(jnp.int32)

    units = drop_weight.shape[0]
    step = units // 2
    heads_pack = payload(blocks_of(heads_weight, width))
    heads_across = swap(choose(heads_pack, row_half), "seq", 2)

    parts = []
    for h in range(2):
        columns = [lift_weight[:, j * units + h * step : j * units + (h + 1) * step] for j in range(4)]
        parts.append(drop_weight[h * step : (h + 1) * step])
        parts += [jnp.concatenate(columns[k : k + 2], axis=1) for k in (0, 2)]
    pack = choose(payload(parts + [merge_weight]), row_half)
    def gather_halves(pack):
        size = 2 * count
        total = count * lax.axis_size("dp")
        groups = [list(range(k, k + size)) for k in range(0, total, size)]
        return lax.all_gather(pack, ("dp", "seq"), axis=0, axis_index_groups=groups)

    table_rows, depth = time_table.shape
    chosen_rows = (time_step[:, None] == jnp.arange(table_rows, dtype=jnp.int32)[None, :]).astype(LOW)
    conds = jnp.dot(chosen_rows, time_table, preferred_element_type=FULL)
    modulation = matmul(conds.astype(LOW), modulate_weight, 1, 1) + modulate_bias.astype(FULL)
    columns = modulation.shape[1]
    small = jnp.concatenate(
        [modulation.reshape(-1)]
        + [v.astype(FULL) for v in (lift_bias, drop_bias, first_gain, second_gain)]
        + [token_pos.astype(FULL).reshape(-1)]
    )
    small_across = swap(small, "seq", 2)
    heads_across, small, small_across, hidden_in, pack = fence(
        heads_across, small, small_across, hidden_in, pack
    )
    heads_handed = swap(heads_across, "dp", 1)
    heads_core = swap(heads_pack, "seq", 1), swap(heads_across, "seq", 1)
    hidden = lax.all_to_all(hidden_in, "seq", 0, 0, tiled=True).reshape(length, width)
    packs = gather_halves(pack)
    small = jnp.stack([small, small_across])
    small_core = swap(small, "seq", 1)
    small = jnp.stack([small[0], small_core[0], small[1], small_core[1]])
    small = choose_all(small, place)
    heads = (
        heads_pack,
        heads_core[0],
        heads_across,
        heads_handed,
        heads_core[1],
        swap(heads_handed, "seq", 1),
    )
    chosen = small[:, : seqs * columns].reshape(count, seqs, columns)
    chosen = lax.dynamic_index_in_dim(chosen, place, 1, keepdims=False).reshape(6, width)
    rest = small[:, seqs * columns :]
    sizes = (lift_bias.shape[0], drop_bias.shape[0], first_gain.shape[0], second_gain.shape[0])
    vectors, at = [], 0
    for size in sizes:
        vectors.append(rest[:, at : at + size].reshape(1, -1))
        at += size
    up_bias, down_bias, gain_one, gain_two = vectors
    positions = choose(rest[:, at:].reshape(count, seqs, span).swapaxes(0, 1), place)
    positions = positions.reshape(length)
    shift_a, scale_a, gate_a, shift_b, scale_b, gate_b = [chosen[k : k + 1] for k in range(6)]
    grow_a, grow_b = 1.0 + scale_a, 1.0 + scale_b

    def rows(*items):
        blank = jnp.zeros((8 - len(items), width), FULL)
        return jnp.concatenate(items + (blank,), axis=0)

    freqs = 10000.0 ** (-jnp.arange(0, head, 2, dtype=FULL) / head)
    freqs = jnp.tile(freqs, 2 * LANES // head)
    angles = positions[:, None] * freqs
    cosine, sine = jnp.cos(angles), jnp.sin(angles)

    hidden, heads, cosine, sine, out_grad = fence(hidden, heads, cosine, sine, out_grad)
    adapted_a, query, key, value = project(
        me, hidden, rows(gain_one, grow_a, shift_a), heads, cosine, sine, head
    )
    query, out_grad = fence(query, out_grad)
    upstream = lax.all_to_all(out_grad, "seq", 0, 0, tiled=True).reshape(length, width)
    pairs = width // LANES // 2
    mixed_0, logsum_0 = attend(me, query, key, value, head, 0, pairs)
    merge_vectors, unmerge_vectors = rows(gate_a, gain_two, grow_b, shift_b), rows(gate_a, gain_two, grow_b)
    feed_vectors = rows(gate_b, down_bias)
    bias_0, bias_1 = [up_bias.reshape(4, 2, step)[:, h].reshape(1, 4 * step) for h in range(2)]
    query, merge_vectors, unmerge_vectors, feed_vectors, bias_0, bias_1 = fence(
        query, merge_vectors, unmerge_vectors, feed_vectors, bias_0, bias_1
    )
    query, mixed_0 = fence(query, mixed_0)
    mixed_1, logsum_1 = attend(me, query, key, value, head, pairs, pairs)
    mixed_1, upstream = fence(mixed_1, upstream)
    mixed = (mixed_0, mixed_1)
    middle, adapted_b = merge(me, mixed, hidden, merge_vectors, packs)
    lowered, grad, liftbias_0, grads_0 = feed(
        me, adapted_b, upstream, feed_vectors, bias_0, packs, 0
    )

    def over_seq(grads):
        flat = grads.reshape(-1, grads.shape[-1])
        return lax.psum_scatter(flat, "seq", scatter_dimension=0, tiled=True)

    term_0 = over_seq(grads_0)
    block_out, adapted_b_grad, feed_sums, liftbias_1, grads_1 = feed(
        me, adapted_b, upstream, feed_vectors, bias_1, packs, 1, (lowered, grad, middle)
    )
    term_1 = over_seq(grads_1)
    back = bits[::-1]
    middle_grad, mixed_grad, merge_sums, merge_keep, merge_send = unmerge(
        me, adapted_b_grad, middle, upstream, mixed, unmerge_vectors, packs
    )
    block_out = lax.all_to_all(block_out.reshape(count, span, width), "seq", 0, 0, tiled=True)
    heads_0 = unattend(
        me, query, key, value, mixed_0, mixed_grad, logsum_0, cosine, sine, head, 0
    )
    heads_0, term_0, block_out = fence(heads_0, term_0, block_out)
    parts_0 = deal(term_0)
    keep_2, send_2 = weigh(me, adapted_a, heads_0, (merge_keep, merge_send))
    mixed_grad, send_2 = fence(mixed_grad, send_2)
    got_2 = swap(send_2, "seq", 1)
    heads_1 = unattend(
        me, query, key, value, mixed_1, mixed_grad, logsum_1, cosine, sine, head, pairs
    )
    heads_1, got_2, parts_0 = fence(heads_1, got_2, parts_0)
    heads_1, mine_2, other_2, term_0 = fence(heads_1, *sum_pair(keep_2, got_2), add_up(parts_0))
    got_2 = swap(other_2, "seq", 2)
    got_0 = swap(term_0, "dp", back[0])
    keep_3, send_3 = weigh(me, adapted_a, heads_1)
    heads_1, send_3, got_0, term_1 = fence(heads_1, send_3, got_0, term_1)
    got_3 = swap(send_3, "seq", 1)
    heads_1, term_0 = fence(heads_1, join(term_0, got_0, back[0]))
    got_0 = swap(term_0, "dp", back[1])
    parts_1 = deal(term_1)
    heads_1, got_3 = fence(heads_1, got_3)
    heads_1, mine_3, other_3 = fence(heads_1, *sum_pair(keep_3, got_3))
    got_3 = swap(other_3, "seq", 2)
    *input_parts, project_sums = unproject(
        me, (heads_0, heads_1), hidden, middle_grad, rows(gain_one, grow_a), heads
    )
    liftbias_grad = jnp.stack([liftbias_0.reshape(4, step), liftbias_1.reshape(4, step)], axis=1)
    modulation_grad = jnp.concatenate(
        [project_sums[0:2], merge_sums[3:4], merge_sums[0:2], feed_sums[0:1]], axis=0
    ).reshape(count, columns)
    small = jnp.concatenate(
        [
            modulation_grad,
            liftbias_grad.reshape(count, -1),
            feed_sums[1].reshape(count, -1),
            project_sums[2].reshape(count, -1),
            merge_sums[2].reshape(count, -1),
        ],
        axis=1,
    )
    parts = [choose(small, place ^ d) for d in range(4)]
    parts = [swap(part, "seq", d) if d else part for d, part in enumerate(parts)]
    input_parts, got_0, got_2, got_3, parts_1, parts = fence(
        input_parts, got_0, got_2, got_3, parts_1, parts
    )
    pack = choose_all(jnp.stack(parts), place)
    pack = jnp.concatenate(
        [
            pack[:, :columns].reshape(-1),
            jnp.sum(pack[:, columns:], axis=0),
            conds.reshape(-1),
            time_step.astype(FULL),
        ]
    )[None]

    def doubled(array, other, distance):
        pair = jnp.stack([array, other])
        return jnp.where(bit("dp", distance) == 0, pair, pair[::-1])

    last = len(back) - 1
    term_0 = join(term_0, got_0, back[1])
    term_1 = add_up(parts_1)
    term_2 = sum_beside((mine_2, got_2), (mine_3, got_3))
    input_parts, pack, term_0, term_1, term_2 = fence(input_parts, pack, term_0, term_1, term_2)
    for k in range(2, last):
        term_0 = join(term_0, swap(term_0, "dp", back[k]), back[k])
    got_0 = swap(term_0, "dp", back[-1])
    got_1 = swap(term_1, "dp", back[0])
    parts_2 = deal(term_2)
    other = swap(pack, "dp", back[0])
    input_parts = [swap(part, "seq", d) if d else part for d, part in enumerate(input_parts)]
    input_parts, got_0, got_1, parts_2, other = fence(input_parts, got_0, got_1, parts_2, other)
    term_2 = add_up(parts_2)
    got_2 = None
    for k in range(last):
        term_1 = join(term_1, got_1, back[k])
        if k:
            term_2 = join(term_2, got_2, back[k - 1])
        pack = doubled(pack, other, back[k])
        term_1, term_2, pack = fence(term_1, term_2, pack)
        got_1 = swap(term_1, "dp", back[k + 1])
        got_2 = swap(term_2, "dp", back[k])
        other = swap(pack, "dp", back[k + 1])
        if k == 0:
            input_grad = lay(me, input_parts)
        got_1, got_2, other = fence(got_1, got_2, other)
    pack = doubled(pack, other, back[-1]).reshape(lax.axis_size("dp"), -1)
    term_2 = join(term_2, got_2, back[last - 1])
    pack, term_2 = fence(pack, term_2)
    pair_0, pair_1 = (term_0, got_0), (term_1, got_1)
    pair_2 = (term_2, swap(term_2, "dp", back[-1]))
    deep = width // 4
    drop_grad, lift_grad = settle(
        [pair_0, pair_1],
        [
            [(0, 0, step, width, 0, h * step, 0)]
            + [
                (step + (j >> 1) * deep, (j & 1) * step, deep, step, 1, 0, j * units + h * step)
                for j in range(4)
            ]
            for h in range(2)
        ],
        [drop_weight.shape, lift_weight.shape],
    )
    part = width // 2
    heads_grad, merge_grad = settle(
        [pair_2],
        [
            [(0, 3 * part, deep, width, 1, 0, 0)]
            + [(0, k * part, deep, part, 0, 0, k * width) for k in range(3)]
            + [(0, (5 + k) * part, deep, part, 0, 0, k * width + part) for k in range(3)],
        ],
        [heads_weight.shape, merge_weight.shape],
    )
    row_grads = pack[:, : seqs * columns].reshape(-1, columns)
    at = seqs * columns
    ends = []
    for size in sizes:
        ends.append(jnp.sum(pack[:, at : at + size], axis=0))
        at += size
    liftbias_out, dropbias_out, firstgain_out, secondgain_out = ends
    all_conds = pack[:, at : at + seqs * depth].reshape(-1, depth)
    steps = pack[:, at + seqs * depth :].reshape(-1)
    exact = lax.Precision.HIGHEST
    modulate_grad = jnp.einsum("sm,sc->mc", row_grads, all_conds, precision=exact)
    modulatebias_grad = jnp.sum(row_grads, axis=0)
    conds_grad = jnp.einsum(
        "sm,mc->sc", row_grads, modulate_weight.astype(FULL), precision=exact
    )
    conds_grad = sum([swap(conds_grad, "seq", d) for d in (1, 2, 3)], conds_grad)
    share = table_rows // count
    own = steps[None, :] == (place * share + jnp.arange(share)).astype(FULL)[:, None]
    table_grad = jnp.dot(own.astype(FULL), conds_grad, precision=exact)
    return (
        block_out,
        input_grad,
        heads_grad,
        merge_grad,
        lift_grad,
        liftbias_out,
        drop_grad,
        dropbias_out,
        modulate_grad,
        modulatebias_grad,
        firstgain_out,
        secondgain_out,
        table_grad,
    )


def solution(mesh):
    return jax.shard_map(
        shards,
        mesh=mesh,
        in_specs=(
            P("dp", "seq", None),
            P(),
            P("dp"),
            P("dp", "seq"),
            P("seq", None),
            P("seq", None),
            P("seq", None),
            P("seq"),
            P("seq", None),
            P("seq"),
            P("seq", None),
            P("seq"),
            P("seq"),
            P("seq"),
            P("dp", "seq", None),
        ),
        out_specs=(
            P("dp", "seq", None),
            P("dp", "seq", None),
            P("seq", None),
            P("seq", None),
            P("seq", None),
            P("seq"),
            P("seq", None),
            P("seq"),
            P("seq", None),
            P("seq"),
            P("seq"),
            P("seq"),
            P("seq", None),
        ),
        check_vma=False,
    )
```

time: 604 us -> 432 us (0.72)
  waiting for transfers between devices: 241 us -> 106 us
  Pallas kernels: 159 us -> 206 us
  other arithmetic: 34.7 us -> 8.85 us
  blocking collectives: 20.6 us -> 0 us
  local copies, waits for them, and re-layouts: 39.4 us -> 20 us
  starting transfers between devices: 77.2 us -> 62.8 us
    unnamed x4 -> x3, waiting for transfers between devices: 62.6 us -> 0.05 us
    pallas_call x8 -> x27, Pallas kernels: 159 us -> 206 us  [call(): pl.pallas_call(body, name=name, grid_spec=pltpu.PrefetchScalarGridSpec(nu...]
    all_to_all x1, waiting for transfers between devices: 50.9 us -> 20.2 us  [shards(): lax.all_to_all(hidden_in, 'seq', 0, 0, tiled=True).reshape(length, width)]
    all_to_all x7 -> x3, waiting for transfers between devices: 27.3 us -> 0.01 us  [deal(): return lax.all_to_all(parts, 'dp', 0, 0, tiled=True)]
    ppermute x40 -> x32, waiting for transfers between devices: 93.3 us -> 69.8 us  [swap(): return lax.ppermute(array, axis, [(i, i ^ distance) for i in range(size)])]
    add x9 -> x0, other arithmetic: 13.1 us -> none  [the longest x4 8.02 us: reduce_over_rows(): term = keep.astype(FULL) + swap(send, 'seq', 1).astype(FULL)]
    convert_element_type x9 -> x2, other arithmetic: 11.6 us -> 0.01 us  [the longest x1 0.01 us: shards(): (place * share + jnp.arange(share)).astype(FULL)[:, None]]
    all_to_all x7 -> x3, starting transfers between devices: 30.2 us -> 19.6 us  [deal(): return lax.all_to_all(parts, 'dp', 0, 0, tiled=True)]
  transfers between devices with their start and end apart: 52 -> 41, of which waited for: 24 -> 16; matrix products, arithmetic and copies ran while one was open for 11% -> 4% of each run, Pallas kernels for 16% -> 37%
where the time goes in v2:
time: 432 us; the launch traced here: 423 us
  Pallas kernels  206 us (48%)
  waiting for transfers between devices  106 us (25%)
  starting transfers between devices  62.8 us (15%)
  local copies, waits for them, and re-layouts  20 us (5%)
  between operations  14.8 us (3%)
  other arithmetic  8.85 us (2%)
  matrix products  4.44 us (1%)
    pallas_call x27, Pallas kernels, call(): pl.pallas_call(body, name=name, grid_spec=pltpu.PrefetchScalarGridSpec(nu...  206 us
    ppermute x32, waiting for transfers between devices, swap(): return lax.ppermute(array, axis, [(i, i ^ distance) for i in range(size)])  69.8 us
    ppermute x32, starting transfers between devices, swap(): return lax.ppermute(array, axis, [(i, i ^ distance) for i in range(size)])  32.1 us
    all_to_all x1, waiting for transfers between devices, shards(): lax.all_to_all(hidden_in, 'seq', 0, 0, tiled=True).reshape(length, width)  20.2 us
    all_to_all x3, starting transfers between devices, deal(): return lax.all_to_all(parts, 'dp', 0, 0, tiled=True)  19.6 us
    all_to_all x1, waiting for transfers between devices, shards(): lax.all_to_all(out_grad, 'seq', 0, 0, tiled=True).reshape(length, width)  10.2 us
  transfers between devices with their start and end apart: 41, of which 16 were waited for; matrix products, arithmetic and copies ran while one was open for 4% of the time, Pallas kernels for 37%

profile of v2, /device:TPU:8, one launch (start us, length us, event | category | flops | bytes accessed | tf_op | source)
XLA Modules:
  0.0 423.4 jit_solution(9525326659341965260)
XLA Ops:
  10.1 2.8 concatenate.46
  20.0 8.2 %collective-permute-done.p2 = bf16[288,768]{1,0:T(8,128)(2,1)S(1)} collective-permute-done((bf16[288,768]{1,0:T(8,128)(2,1)}, bf16[288,768]{1,0:T(8,128)(2,1)S(1)}, u32[]{:S(2)}, u32[]{:S(2)}) %collective-permute-start) | collective-permute-done | bytes 442400 | tf_op jit(solution)/shard_map/ppermute | solution.py:600
  31.5 3.6 all-to-all-start
  36.1 9.3 %collective-permute-done.3.p3 = bf16[288,768]{1,0:T(8,128)(2,1)} collective-permute-done((bf16[288,768]{1,0:T(8,128)(2,1)S(1)}, bf16[288,768]{1,0:T(8,128)(2,1)}, u32[]{:S(2)}, u32[]{:S(2)}) %collective-permute-start.3) | collective-permute-done | bytes 442400 | tf_op jit(solution)/shard_map/ppermute | solution.py:600
  46.1 3.1 multiply_sine_fusion
  49.2 20.2 %all-to-all-done = bf16[4,256,768]{2,1,0:T(8,128)(2,1)S(1)} async-done(((bf16[4,256,768]{2,1,0:T(8,128)(2,1)}), bf16[4,256,768]{2,1,0:T(8,128)(2,1)S(1)}, u32[]{:S(2)}, u32[]{:S(2)}) %all-to-all-start) | async-done | bytes 1572896 | tf_op jit(solution)/shard_map/all_to_all | solution.py:831
  70.5 9.7 %project.1 = (bf16[1024,768]{1,0:T(8,128)(2,1)}, bf16[1024,768]{1,0:T(8,128)(2,1)}, bf16[1024,768]{1,0:T(8,128)(2,1)}, bf16[1024,768]{1,0:T(8,128)(2,1)}) custom-call(s32[2]{0:T(128)} %pad_add_fusion.me_ref.at_ref, bf16[1024,768]{1,0:T(8,128)(2,1)} %bitcast.77, f32[8,768]{1,0:T(8,128)} %get-tuple-element.325.vectors, bf16[2,288,768]{2,1,0:T(8,128)(2,1)} %copy-done.3, ...), custom_call_target="tpu_custom_call" | custom-call | flops 1024 | bytes 1024 | tf_op jit(solution)/shard_map/project/pallas_call | solution.py:25
  80.2 3.6 all-to-all-start.1
  86.0 12.4 %attend.2 = (bf16[1024,384]{1,0:T(8,128)(2,1)}, f32[3,2,1024]{2,1,0:T(2,128)}) custom-call(s32[2]{0:T(128)} %pad_add_fusion.me_ref.at_ref, bf16[1024,768]{1,0:T(8,128)(2,1)} %get-tuple-element.166.query, bf16[1024,768]{1,0:T(8,128)(2,1)} %get-tuple-element.163.key, bf16[1024,768]{1,0:T(8,128)(2,1)} %get-tuple-element.164.value), custom_call_target="tpu_custom_call" | custom-call | flops 1024 | bytes 1024 | tf_op jit(solution)/shard_map/attend/pallas_call | solution.py:25
  98.3 12.4 %attend.3 = (bf16[1024,384]{1,0:T(8,128)(2,1)}, f32[3,2,1024]{2,1,0:T(2,128)}) custom-call(s32[2]{0:T(128)} %pad_add_fusion.me_ref.at_ref, bf16[1024,768]{1,0:T(8,128)(2,1)} %get-tuple-element.166.query, bf16[1024,768]{1,0:T(8,128)(2,1)} %get-tuple-element.163.key, bf16[1024,768]{1,0:T(8,128)(2,1)} %get-tuple-element.164.value), custom_call_target="tpu_custom_call" | custom-call | flops 1024 | bytes 1024 | tf_op jit(solution)/shard_map/attend/pallas_call | solution.py:25
  110.7 10.2 %all-to-all-done.1 = bf16[4,256,768]{2,1,0:T(8,128)(2,1)S(1)} async-done(((bf16[4,256,768]{2,1,0:T(8,128)(2,1)}), bf16[4,256,768]{2,1,0:T(8,128)(2,1)S(1)}, u32[]{:S(2)}, u32[]{:S(2)}) %all-to-all-start.1) | async-done | bytes 1572896 | tf_op jit(solution)/shard_map/all_to_all | solution.py:873
  120.9 1.9 all-gather.3.cloned.1.call-done
  122.8 7.5 %merge.1 = (f32[1024,768]{1,0:T(8,128)}, bf16[1024,768]{1,0:T(8,128)(2,1)}) custom-call(s32[2]{0:T(128)} %pad_add_fusion.me_ref.at_ref, bf16[1024,384]{1,0:T(8,128)(2,1)} %get-tuple-element.167.m0.mixed, bf16[1024,384]{1,0:T(8,128)(2,1)} %get-tuple-element.170.m1.mixed, bf16[1024,768]{1,0:T(8,128)(2,1)} %bitcast.78, f32[8,768]{1,0:T(8,128)} %concatenate.53.vectors, ...), custom_call_target="tpu_custom_call" | custom-call | flops 1024 | bytes 1024 | tf_op jit(solution)/shard_map/merge/pallas_call | solution.py:25
  130.3 22.3 %feed.2 = (f32[1024,768]{1,0:T(8,128)}, f32[1024,768]{1,0:T(8,128)}, f32[1,1536]{1,0:T(1,128)}, bf16[4,768,768]{2,1,0:T(8,128)(2,1)}) custom-call(s32[2]{0:T(128)} %pad_add_fusion.me_ref.at_ref, bf16[1024,768]{1,0:T(8,128)(2,1)} %get-tuple-element.173.adapted, bf16[1024,768]{1,0:T(8,128)(2,1)} %bitcast.74, f32[8,768]{1,0:T(8,128)} %get-tuple-element.175.vectors, ...), custom_call_target="tpu_custom_call" | custom-call | flops 1024 | bytes 1024 | tf_op jit(solution)/shard_map/feed/pallas_call | solution.py:25
  152.6 24.3 %feed.3 = (bf16[1024,768]{1,0:T(8,128)(2,1)}, f32[1024,768]{1,0:T(8,128)}, f32[8,768]{1,0:T(8,128)}, f32[1,1536]{1,0:T(1,128)}, bf16[4,768,768]{2,1,0:T(8,128)(2,1)}) custom-call(s32[2]{0:T(128)} %pad_add_fusion.me_ref.at_ref, bf16[1024,768]{1,0:T(8,128)(2,1)} %get-tuple-element.173.adapted, bf16[1024,768]{1,0:T(8,128)(2,1)} %bitcast.75, ...), custom_call_target="tpu_custom_call" | custom-call | flops 1024 | bytes 1024 | tf_op jit(solution)/shard_map/feed/pallas_call | solution.py:25
  176.9 3.6 all-to-all-start.2
  180.5 11.7 %unmerge.1 = (f32[1024,768]{1,0:T(8,128)}, bf16[1024,768]{1,0:T(8,128)(2,1)}, f32[8,768]{1,0:T(8,128)}, bf16[2,192,768]{2,1,0:T(8,128)(2,1)}, bf16[2,192,768]{2,1,0:T(8,128)(2,1)}) custom-call(s32[2]{0:T(128)} %pad_add_fusion.me_ref.at_ref, f32[1024,768]{1,0:T(8,128)} %get-tuple-element.181.adapted_grad, f32[1024,768]{1,0:T(8,128)} %get-tuple-element.180.refs_2_.middle, ...), custom_call_target="tpu_custom_call" | custom-call | flops 1024 | bytes 1024 | tf_op jit(solution)/shard_map/unmerge/pallas_call | solution.py:25
  192.2 19.9 %unattend.2.grads.g0 = bf16[3,1024,384]{2,1,0:T(8,128)(2,1)} custom-call(s32[2]{0:T(128)} %pad_add_fusion.me_ref.at_ref, bf16[1024,768]{1,0:T(8,128)(2,1)} %get-tuple-element.166.query, bf16[1024,768]{1,0:T(8,128)(2,1)} %get-tuple-element.163.key, bf16[1024,768]{1,0:T(8,128)(2,1)} %get-tuple-element.164.value, ...), custom_call_target="tpu_custom_call" | custom-call | flops 1024 | bytes 1024 | tf_op jit(solution)/shard_map/unattend/pallas_call | solution.py:25
  212.2 3.8 all-to-all-done.2
  216.0 6.5 %all-to-all-start.3 = ((bf16[8,96,768]{2,1,0:T(8,128)(2,1)}), bf16[8,96,768]{2,1,0:T(8,128)(2,1)S(1)}, u32[]{:S(2)}, u32[]{:S(2)}) async-start(bf16[8,96,768]{2,1,0:T(8,128)(2,1)} %bitcast.95), calls=%async_computation.4 | async-start | bytes 2359296 | tf_op jit(solution)/shard_map/all_to_all | solution.py:693
  222.5 9.4 %weigh.2 = (bf16[2,192,1920]{2,1,0:T(8,128)(2,1)}, bf16[2,192,1920]{2,1,0:T(8,128)(2,1)}) custom-call(s32[2]{0:T(128)} %pad_add_fusion.me_ref.at_ref, bf16[1024,768]{1,0:T(8,128)(2,1)} %get-tuple-element.189.adapted, bf16[3,1024,384]{2,1,0:T(8,128)(2,1)} %unattend.2.grads.g0, bf16[2,192,768]{2,1,0:T(8,128)(2,1)} %get-tuple-element.190.refs_0_, ...), custom_call_target="tpu_custom_call" | custom-call | flops 1024 | bytes 1024 | tf_op jit(solution)/shard_map/weigh/pallas_call | solution.py:25
  231.9 20.0 %unattend.3.grads.g1 = bf16[3,1024,384]{2,1,0:T(8,128)(2,1)} custom-call(s32[2]{0:T(128)} %pad_add_fusion.me_ref.at_ref, bf16[1024,768]{1,0:T(8,128)(2,1)} %get-tuple-element.166.query, bf16[1024,768]{1,0:T(8,128)(2,1)} %get-tuple-element.163.key, bf16[1024,768]{1,0:T(8,128)(2,1)} %get-tuple-element.164.value, ...), custom_call_target="tpu_custom_call" | custom-call | flops 1024 | bytes 1024 | tf_op jit(solution)/shard_map/unattend/pallas_call | solution.py:25
  252.9 2.1 add.140.first
  255.0 3.9 pair.2
  258.9 2.4 collective-permute-start.8
  261.2 7.2 %weigh.3 = (bf16[2,192,1152]{2,1,0:T(8,128)(2,1)}, bf16[2,192,1152]{2,1,0:T(8,128)(2,1)}) custom-call(s32[2]{0:T(128)} %pad_add_fusion.me_ref.at_ref, bf16[1024,768]{1,0:T(8,128)(2,1)} %get-tuple-element.189.adapted, bf16[3,1024,384]{2,1,0:T(8,128)(2,1)} %unattend.3.grads.g1), custom_call_target="tpu_custom_call" | custom-call | flops 1024 | bytes 1024 | tf_op jit(solution)/shard_map/weigh/pallas_call | solution.py:25
  268.4 7.0 %all-to-all-start.4 = ((bf16[8,96,768]{2,1,0:T(8,128)(2,1)}), bf16[8,96,768]{2,1,0:T(8,128)(2,1)S(1)}, u32[]{:S(2)}, u32[]{:S(2)}) async-start(bf16[8,96,768]{2,1,0:T(8,128)(2,1)} %bitcast.94), calls=%async_computation.6 | async-start | bytes 2359296 | tf_op jit(solution)/shard_map/all_to_all | solution.py:693
  278.3 3.5 pair.3
  284.2 12.3 %unproject.1 = (bf16[256,768]{1,0:T(8,128)(2,1)}, bf16[256,768]{1,0:T(8,128)(2,1)}, bf16[256,768]{1,0:T(8,128)(2,1)}, bf16[256,768]{1,0:T(8,128)(2,1)}, f32[8,768]{1,0:T(8,128)}) custom-call(s32[2]{0:T(128)} %pad_add_fusion.me_ref.at_ref, bf16[3,1024,384]{2,1,0:T(8,128)(2,1)} %unattend.2.grads.g0, bf16[3,1024,384]{2,1,0:T(8,128)(2,1)} %unattend.3.grads.g1, ...), custom_call_target="tpu_custom_call" | custom-call | flops 1024 | bytes 1024 | tf_op jit(solution)/shard_map/unproject/pallas_call | solution.py:25
  300.0 2.3 collective-permute-done.10.second
  305.7 2.1 add.141.first
  307.8 1.9 join.7
  309.7 2.9 beside.1
  312.6 6.1 %all-to-all-start.5 = ((bf16[8,24,3072]{2,1,0:T(8,128)(2,1)}), bf16[8,24,3072]{2,1,0:T(8,128)(2,1)S(1)}, u32[]{:S(2)}, u32[]{:S(2)}) async-start(bf16[8,24,3072]{2,1,0:T(8,128)(2,1)} %bitcast.82), calls=%async_computation.7 | async-start | bytes 2359296 | tf_op jit(solution)/shard_map/all_to_all | solution.py:693
  322.0 2.4 collective-permute-start.21
  324.4 20.9 %collective-permute-done.21 = f32[1,6468]{1,0:T(1,128)S(1)} collective-permute-done((f32[1,6468]{1,0:T(1,128)S(1)}, f32[1,6468]{1,0:T(1,128)S(1)}, u32[]{:S(2)}, u32[]{:S(2)}) %collective-permute-start.21) | collective-permute-done | bytes 25904 | tf_op jit(solution)/shard_map/ppermute | solution.py:600
  345.3 3.4 collective-permute-start.20
  348.8 4.8 %collective-permute-done.20.second = bf16[96,768]{1,0:T(8,128)(2,1)S(1)} collective-permute-done((bf16[96,768]{1,0:T(8,128)(2,1)S(1)}, bf16[96,768]{1,0:T(8,128)(2,1)S(1)}, u32[]{:S(2)}, u32[]{:S(2)}) %collective-permute-start.20) | collective-permute-done | bytes 147488 | tf_op jit(solution)/shard_map/ppermute | solution.py:600
  356.7 2.1 add.142.first
  358.8 3.7 collective-permute-start.22
  364.3 9.7 %collective-permute-done.24 = f32[2,1,6468]{2,0,1:T(2,128)S(1)} collective-permute-done((f32[2,1,6468]{2,0,1:T(2,128)S(1)}, f32[2,1,6468]{2,0,1:T(2,128)S(1)}, u32[]{:S(2)}, u32[]{:S(2)}) %collective-permute-start.24) | collective-permute-done | bytes 51776 | tf_op jit(solution)/shard_map/ppermute | solution.py:600
  374.8 1.9 join.9
  382.3 3.3 lay.1
  385.6 10.1 %collective-permute-done.27 = f32[2,2,1,6468]{3,1,0,2:T(2,128)S(1)} collective-permute-done((f32[2,2,1,6468]{3,1,0,2:T(2,128)S(1)}, f32[2,2,1,6468]{3,1,0,2:T(2,128)S(1)}, u32[]{:S(2)}, u32[]{:S(2)}) %collective-permute-start.27) | collective-permute-done | bytes 103520 | tf_op jit(solution)/shard_map/ppermute | solution.py:600
  396.4 1.9 join.11
  402.9 1.9 fusion.17
  405.5 4.0 settle.3
  412.7 2.8 settle.2
  (219 shorter events, 56.0 us)
Async XLA Ops:
  7.2 115.6 %all-gather.3.cloned.1.call-start = ((), (), s32[]{:S(2)}) async-start(), calls=%async_computation.10 | async-start | bytes 11943936 | tf_op jit(solution)/shard_map/all_gather | solution.py:813
  12.8 7.2 %collective-permute-start.1 = (f32[6976]{0:T(1024)S(1)}, f32[6976]{0:T(1024)S(1)}, u32[]{:S(2)}, u32[]{:S(2)}) collective-permute-start(f32[6976]{0:T(1024)S(1)} %concatenate.46), channel_id=1, source_target_pairs={{0,2},{1,3},{2,0},{3,1},{4,6},{5,7},{6,4},{7,5},{8,10},{9,11},{10,... | collective-permute-start | bytes 83720 | tf_op jit(solution)/shard_map/ppermute | solution.py:600
  15.6 12.7 %copy-start.3 = (bf16[2,288,768]{2,1,0:T(8,128)(2,1)}, bf16[2,288,768]{2,1,0:T(8,128)(2,1)S(1)}, u32[]{:S(2)}) copy-start(bf16[2,288,768]{2,1,0:T(8,128)(2,1)S(1)} %pad_maximum_fusion.p0) | copy-start | bytes 2654212
  16.4 11.8 %collective-permute-start = (bf16[288,768]{1,0:T(8,128)(2,1)}, bf16[288,768]{1,0:T(8,128)(2,1)S(1)}, u32[]{:S(2)}, u32[]{:S(2)}) collective-permute-start(bf16[288,768]{1,0:T(8,128)(2,1)} %dynamic-slice_bitcast_fusion.1), channel_id=1, source_target_pairs={{0,2},{1,3},{2,0},{3,1},{4,6},{5,7},{6,4},{7,5},{8,10},{9,11},{10,... | collective-permute-start | bytes 1327112 | tf_op jit(solution)/shard_map/ppermute | solution.py:600
  28.3 20.9 %collective-permute-start.2 = (bf16[2,288,768]{2,1,0:T(8,128)(2,1)S(1)}, bf16[2,288,768]{2,1,0:T(8,128)(2,1)}, u32[]{:S(2)}, u32[]{:S(2)}) collective-permute-start(bf16[2,288,768]{2,1,0:T(8,128)(2,1)S(1)} %pad_maximum_fusion.p0), channel_id=1, source_target_pairs={{0,1},{1,0},{2,3},{3,2},{4,5},{5,4},{6,7},{7,6},{8,9},{9,8},{10,11... | collective-permute-start | bytes 2654216 | tf_op jit(solution)/shard_map/ppermute | solution.py:600
  28.5 6.6 %collective-permute-start.6 = (f32[2,6976]{1,0:T(2,128)S(1)}, f32[2,6976]{1,0:T(2,128)S(1)}, u32[]{:S(2)}, u32[]{:S(2)}) collective-permute-start(f32[2,6976]{1,0:T(2,128)S(1)} %pad_maximum_fusion.9), channel_id=1, source_target_pairs={{0,1},{1,0},{2,3},{3,2},{4,5},{5,4},{6,7},{7,6},{8,9},{9,8},{10,11... | collective-permute-start | bytes 167432 | tf_op jit(solution)/shard_map/ppermute | solution.py:600
  29.9 19.3 %collective-permute-start.4 = (bf16[288,768]{1,0:T(8,128)(2,1)S(1)}, bf16[288,768]{1,0:T(8,128)(2,1)}, u32[]{:S(2)}, u32[]{:S(2)}) collective-permute-start(bf16[288,768]{1,0:T(8,128)(2,1)S(1)} %collective-permute-done.p2), channel_id=1, source_target_pairs={{0,1},{1,0},{2,3},{3,2},{4,5},{5,4},{6,7},{7,6},{8,9},{9,8},{10,11... | collective-permute-start | bytes 1327112 | tf_op jit(solution)/shard_map/ppermute | solution.py:600
  29.9 15.5 %collective-permute-start.3 = (bf16[288,768]{1,0:T(8,128)(2,1)S(1)}, bf16[288,768]{1,0:T(8,128)(2,1)}, u32[]{:S(2)}, u32[]{:S(2)}) collective-permute-start(bf16[288,768]{1,0:T(8,128)(2,1)S(1)} %collective-permute-done.p2), channel_id=1, source_target_pairs={{0,4},{4,0},{8,12},{12,8},{16,20},{20,16},{24,28},{28,24},{1,5},{5... | collective-permute-start | bytes 1327112 | tf_op jit(solution)/shard_map/ppermute | solution.py:600
  31.5 37.8 %all-to-all-start = ((bf16[4,256,768]{2,1,0:T(8,128)(2,1)}), bf16[4,256,768]{2,1,0:T(8,128)(2,1)S(1)}, u32[]{:S(2)}, u32[]{:S(2)}) async-start(bf16[4,256,768]{2,1,0:T(8,128)(2,1)} %param.15), calls=%async_computation | async-start | bytes 3145728 | tf_op jit(solution)/shard_map/all_to_all | solution.py:831
  45.4 3.8 collective-permute-start.5
  80.2 40.7 %all-to-all-start.1 = ((bf16[4,256,768]{2,1,0:T(8,128)(2,1)}), bf16[4,256,768]{2,1,0:T(8,128)(2,1)S(1)}, u32[]{:S(2)}, u32[]{:S(2)}) async-start(bf16[4,256,768]{2,1,0:T(8,128)(2,1)} %param.29), calls=%async_computation.1 | async-start | bytes 3145728 | tf_op jit(solution)/shard_map/all_to_all | solution.py:873
  83.8 132.3 %reduce-scatter.3.cloned.1.call-start = ((), (), s32[]{:S(2)}) async-start(), calls=%async_computation.8 | async-start | bytes 5898240 | tf_op jit(solution)/shard_map/reduce_scatter | solution.py:893
  120.9 9.4 %copy-start.1 = (bf16[4,256,768]{2,1,0:T(8,128)(2,1)}, bf16[4,256,768]{2,1,0:T(8,128)(2,1)S(1)}, u32[]{:S(2)}) copy-start(bf16[4,256,768]{2,1,0:T(8,128)(2,1)S(1)} %all-to-all-done.1) | copy-start | bytes 4718596
  152.6 115.9 %reduce-scatter.5.cloned.1.call-start = ((), (), s32[]{:S(2)}) async-start(), calls=%async_computation.9 | async-start | bytes 5898240 | tf_op jit(solution)/shard_map/reduce_scatter | solution.py:893
  176.9 39.0 %all-to-all-start.2 = ((bf16[4,256,768]{2,1,0:T(8,128)(2,1)}), bf16[4,256,768]{2,1,0:T(8,128)(2,1)S(1)}, u32[]{:S(2)}, u32[]{:S(2)}) async-start(bf16[4,256,768]{2,1,0:T(8,128)(2,1)} %bitcast.22), calls=%async_computation.3 | async-start | bytes 3145728 | tf_op jit(solution)/shard_map/all_to_all | solution.py:904
  216.0 35.9 %all-to-all-start.3 = ((bf16[8,96,768]{2,1,0:T(8,128)(2,1)}), bf16[8,96,768]{2,1,0:T(8,128)(2,1)S(1)}, u32[]{:S(2)}, u32[]{:S(2)}) async-start(bf16[8,96,768]{2,1,0:T(8,128)(2,1)} %bitcast.95), calls=%async_computation.4 | async-start | bytes 2359296 | tf_op jit(solution)/shard_map/all_to_all | solution.py:693
  231.9 20.0 %collective-permute-start.7 = (bf16[2,192,1920]{2,1,0:T(8,128)(2,1)}, bf16[2,192,1920]{2,1,0:T(8,128)(2,1)}, u32[]{:S(2)}, u32[]{:S(2)}) collective-permute-start(bf16[2,192,1920]{2,1,0:T(8,128)(2,1)} %get-tuple-element.195), channel_id=1, source_target_pairs={{0,1},{1,0},{2,3},{3,2},{4,5},{5,4},{6,7},{7,6},{8,9},{9,8},{10,11... | collective-permute-start | bytes 4423688 | tf_op jit(solution)/shard_map/ppermute | solution.py:600
  258.9 9.5 %collective-permute-start.8 = (bf16[96,768]{1,0:T(8,128)(2,1)S(1)}, bf16[96,768]{1,0:T(8,128)(2,1)S(1)}, u32[]{:S(2)}, u32[]{:S(2)}) collective-permute-start(bf16[96,768]{1,0:T(8,128)(2,1)S(1)} %copy-done.12), channel_id=1, source_target_pairs={{0,16},{4,20},{8,24},{12,28},{16,0},{20,4},{24,8},{28,12},{1,17},{... | collective-permute-start | bytes 442376 | tf_op jit(solution)/shard_map/ppermute | solution.py:600
  268.4 7.7 %copy-start.17 = (bf16[96,768]{1,0:T(8,128)(2,1)}, bf16[96,768]{1,0:T(8,128)(2,1)S(1)}, u32[]{:S(2)}) copy-start(bf16[96,768]{1,0:T(8,128)(2,1)S(1)} %collective-permute-done.8.second) | copy-start | bytes 442372
  268.4 36.3 %all-to-all-start.4 = ((bf16[8,96,768]{2,1,0:T(8,128)(2,1)}), bf16[8,96,768]{2,1,0:T(8,128)(2,1)S(1)}, u32[]{:S(2)}, u32[]{:S(2)}) async-start(bf16[8,96,768]{2,1,0:T(8,128)(2,1)} %bitcast.94), calls=%async_computation.6 | async-start | bytes 2359296 | tf_op jit(solution)/shard_map/all_to_all | solution.py:693
  275.5 8.4 %copy-start.21 = (f32[1,1536]{1,0:T(1,128)S(1)}, f32[1,1536]{1,0:T(1,128)}, u32[]{:S(2)}) copy-start(f32[1,1536]{1,0:T(1,128)} %get-tuple-element.229) | copy-start | bytes 18436
  275.5 8.6 %copy-start.22 = (f32[1,1536]{1,0:T(1,128)S(1)}, f32[1,1536]{1,0:T(1,128)}, u32[]{:S(2)}) copy-start(f32[1,1536]{1,0:T(1,128)} %get-tuple-element.230) | copy-start | bytes 18436
  275.5 2.8 collective-permute-start.9
  275.6 26.7 %collective-permute-start.11 = (bf16[192,1920]{1,0:T(8,128)(2,1)}, bf16[192,1920]{1,0:T(8,128)(2,1)}, u32[]{:S(2)}, u32[]{:S(2)}) collective-permute-start(bf16[192,1920]{1,0:T(8,128)(2,1)} %get-tuple-element.223), channel_id=1, source_target_pairs={{0,2},{1,3},{2,0},{3,1},{4,6},{5,7},{6,4},{7,5},{8,10},{9,11},{10,... | collective-permute-start | bytes 2211848 | tf_op jit(solution)/shard_map/ppermute | solution.py:600
  281.9 22.8 %collective-permute-start.12 = (bf16[192,1152]{1,0:T(8,128)(2,1)}, bf16[192,1152]{1,0:T(8,128)(2,1)}, u32[]{:S(2)}, u32[]{:S(2)}) collective-permute-start(bf16[192,1152]{1,0:T(8,128)(2,1)} %get-tuple-element.224), channel_id=1, source_target_pairs={{0,2},{1,3},{2,0},{3,1},{4,6},{5,7},{6,4},{7,5},{8,10},{9,11},{10,... | collective-permute-start | bytes 1327112 | tf_op jit(solution)/shard_map/ppermute | solution.py:600
  284.1 18.1 %collective-permute-start.10 = (bf16[192,768]{1,0:T(8,128)(2,1)S(1)}, bf16[192,768]{1,0:T(8,128)(2,1)}, u32[]{:S(2)}, u32[]{:S(2)}) collective-permute-start(bf16[192,768]{1,0:T(8,128)(2,1)S(1)} %bitcast.101), channel_id=1, source_target_pairs={{0,8},{4,12},{8,0},{12,4},{16,24},{20,28},{24,16},{28,20},{1,9},{5... | collective-permute-start | bytes 884744 | tf_op jit(solution)/shard_map/ppermute | solution.py:600
  284.2 18.0 %copy-start.23 = (s32[4]{0:T(128)S(1)}, s32[4]{0:T(128)}, u32[]{:S(2)}) copy-start(s32[4]{0:T(128)} %param.17) | copy-start | bytes 52
  298.4 5.6 %collective-permute-start.15 = (f32[2496]{0:T(1024)S(1)}, f32[2496]{0:T(1024)S(1)}, u32[]{:S(2)}, u32[]{:S(2)}) collective-permute-start(f32[2496]{0:T(1024)S(1)} %get-tuple-element.282), channel_id=1, source_target_pairs={{0,3},{1,2},{2,1},{3,0},{4,7},{5,6},{6,5},{7,4},{8,11},{9,10},{10,... | collective-permute-start | bytes 29960 | tf_op jit(solution)/shard_map/ppermute | solution.py:600
  298.8 5.9 %collective-permute-start.14 = (f32[2496]{0:T(1024)S(1)}, f32[2496]{0:T(1024)S(1)}, u32[]{:S(2)}, u32[]{:S(2)}) collective-permute-start(f32[2496]{0:T(1024)S(1)} %get-tuple-element.283), channel_id=1, source_target_pairs={{0,2},{1,3},{2,0},{3,1},{4,6},{5,7},{6,4},{7,5},{8,10},{9,11},{10,... | collective-permute-start | bytes 29960 | tf_op jit(solution)/shard_map/ppermute | solution.py:600
  302.2 2.5 collective-permute-start.13
  312.6 32.8 %copy-start.13 = (bf16[96,768]{1,0:T(8,128)(2,1)S(1)}, bf16[96,768]{1,0:T(8,128)(2,1)}, u32[]{:S(2)}) copy-start(bf16[96,768]{1,0:T(8,128)(2,1)} %add.141.first) | copy-start | bytes 442372
  312.6 41.0 %all-to-all-start.5 = ((bf16[8,24,3072]{2,1,0:T(8,128)(2,1)}), bf16[8,24,3072]{2,1,0:T(8,128)(2,1)S(1)}, u32[]{:S(2)}, u32[]{:S(2)}) async-start(bf16[8,24,3072]{2,1,0:T(8,128)(2,1)} %bitcast.82), calls=%async_computation.7 | async-start | bytes 2359296 | tf_op jit(solution)/shard_map/all_to_all | solution.py:693
  318.7 34.9 %collective-permute-start.19 = (bf16[384,768]{1,0:T(8,128)(2,1)}, bf16[384,768]{1,0:T(8,128)(2,1)}, u32[]{:S(2)}, u32[]{:S(2)}) collective-permute-start(bf16[384,768]{1,0:T(8,128)(2,1)} %bitcast.83), channel_id=1, source_target_pairs={{0,4},{4,0},{8,12},{12,8},{16,20},{20,16},{24,28},{28,24},{1,5},{5... | collective-permute-start | bytes 1769480 | tf_op jit(solution)/shard_map/ppermute | solution.py:600
  320.2 33.4 %collective-permute-start.16 = (bf16[256,768]{1,0:T(8,128)(2,1)}, bf16[256,768]{1,0:T(8,128)(2,1)}, u32[]{:S(2)}, u32[]{:S(2)}) collective-permute-start(bf16[256,768]{1,0:T(8,128)(2,1)} %get-tuple-element.246), channel_id=1, source_target_pairs={{0,1},{1,0},{2,3},{3,2},{4,5},{5,4},{6,7},{7,6},{8,9},{9,8},{10,11... | collective-permute-start | bytes 1179656 | tf_op jit(solution)/shard_map/ppermute | solution.py:600
  320.2 33.4 %collective-permute-start.17 = (bf16[256,768]{1,0:T(8,128)(2,1)}, bf16[256,768]{1,0:T(8,128)(2,1)}, u32[]{:S(2)}, u32[]{:S(2)}) collective-permute-start(bf16[256,768]{1,0:T(8,128)(2,1)} %get-tuple-element.247), channel_id=1, source_target_pairs={{0,2},{1,3},{2,0},{3,1},{4,6},{5,7},{6,4},{7,5},{8,10},{9,11},{10,... | collective-permute-start | bytes 1179656 | tf_op jit(solution)/shard_map/ppermute | solution.py:600
  320.6 33.0 %collective-permute-start.18 = (bf16[256,768]{1,0:T(8,128)(2,1)}, bf16[256,768]{1,0:T(8,128)(2,1)}, u32[]{:S(2)}, u32[]{:S(2)}) collective-permute-start(bf16[256,768]{1,0:T(8,128)(2,1)} %get-tuple-element.248), channel_id=1, source_target_pairs={{0,3},{1,2},{2,1},{3,0},{4,7},{5,6},{6,5},{7,4},{8,11},{9,10},{10,... | collective-permute-start | bytes 1179656 | tf_op jit(solution)/shard_map/ppermute | solution.py:600
  322.0 23.3 %collective-permute-start.21 = (f32[1,6468]{1,0:T(1,128)S(1)}, f32[1,6468]{1,0:T(1,128)S(1)}, u32[]{:S(2)}, u32[]{:S(2)}) collective-permute-start(f32[1,6468]{1,0:T(1,128)S(1)} %broadcast_in_dim.5), channel_id=1, source_target_pairs={{0,16},{4,20},{8,24},{12,28},{16,0},{20,4},{24,8},{28,12},{1,17},{... | collective-permute-start | bytes 77624 | tf_op jit(solution)/shard_map/ppermute | solution.py:600
  345.3 8.2 %collective-permute-start.20 = (bf16[96,768]{1,0:T(8,128)(2,1)S(1)}, bf16[96,768]{1,0:T(8,128)(2,1)S(1)}, u32[]{:S(2)}, u32[]{:S(2)}) collective-permute-start(bf16[96,768]{1,0:T(8,128)(2,1)S(1)} %copy-done.13), channel_id=1, source_target_pairs={{0,16},{4,20},{8,24},{12,28},{16,0},{20,4},{24,8},{28,12},{1,17},{... | collective-permute-start | bytes 442376 | tf_op jit(solution)/shard_map/ppermute | solution.py:600
  358.8 15.2 %collective-permute-start.22 = (bf16[192,768]{1,0:T(8,128)(2,1)}, bf16[192,768]{1,0:T(8,128)(2,1)S(1)}, u32[]{:S(2)}, u32[]{:S(2)}) collective-permute-start(bf16[192,768]{1,0:T(8,128)(2,1)} %bitcast.104), channel_id=1, source_target_pairs={{0,8},{4,12},{8,0},{12,4},{16,24},{20,28},{24,16},{28,20},{1,9},{5... | collective-permute-start | bytes 884744 | tf_op jit(solution)/shard_map/ppermute | solution.py:600
  362.5 11.5 %collective-permute-start.23 = (bf16[24,3072]{1,0:T(8,128)(2,1)}, bf16[24,3072]{1,0:T(8,128)(2,1)S(1)}, u32[]{:S(2)}, u32[]{:S(2)}) collective-permute-start(bf16[24,3072]{1,0:T(8,128)(2,1)} %add.142.first), channel_id=1, source_target_pairs={{0,16},{4,20},{8,24},{12,28},{16,0},{20,4},{24,8},{28,12},{1,17},{... | collective-permute-start | bytes 442376 | tf_op jit(solution)/shard_map/ppermute | solution.py:600
  362.5 11.5 %collective-permute-start.24 = (f32[2,1,6468]{2,0,1:T(2,128)S(1)}, f32[2,1,6468]{2,0,1:T(2,128)S(1)}, u32[]{:S(2)}, u32[]{:S(2)}) collective-permute-start(f32[2,1,6468]{2,0,1:T(2,128)S(1)} %broadcast_select_fusion), channel_id=1, source_target_pairs={{0,8},{4,12},{8,0},{12,4},{16,24},{20,28},{24,16},{28,20},{1,9},{5... | collective-permute-start | bytes 155240 | tf_op jit(solution)/shard_map/ppermute | solution.py:600
  378.5 17.2 %collective-permute-start.25 = (bf16[384,768]{1,0:T(8,128)(2,1)}, bf16[384,768]{1,0:T(8,128)(2,1)S(1)}, u32[]{:S(2)}, u32[]{:S(2)}) collective-permute-start(bf16[384,768]{1,0:T(8,128)(2,1)} %bitcast.85), channel_id=1, source_target_pairs={{0,4},{4,0},{8,12},{12,8},{16,20},{20,16},{24,28},{28,24},{1,5},{5... | collective-permute-start | bytes 1769480 | tf_op jit(solution)/shard_map/ppermute | solution.py:600
  380.3 15.4 %collective-permute-start.26 = (bf16[48,3072]{1,0:T(8,128)(2,1)}, bf16[48,3072]{1,0:T(8,128)(2,1)S(1)}, u32[]{:S(2)}, u32[]{:S(2)}) collective-permute-start(bf16[48,3072]{1,0:T(8,128)(2,1)} %bitcast.102), channel_id=1, source_target_pairs={{0,8},{4,12},{8,0},{12,4},{16,24},{20,28},{24,16},{28,20},{1,9},{5... | collective-permute-start | bytes 884744 | tf_op jit(solution)/shard_map/ppermute | solution.py:600
  382.0 13.6 %collective-permute-start.27 = (f32[2,2,1,6468]{3,1,0,2:T(2,128)S(1)}, f32[2,2,1,6468]{3,1,0,2:T(2,128)S(1)}, u32[]{:S(2)}, u32[]{:S(2)}) collective-permute-start(f32[2,2,1,6468]{3,1,0,2:T(2,128)S(1)} %reverse_select_fusion.1), channel_id=1, source_target_pairs={{0,4},{4,0},{8,12},{12,8},{16,20},{20,16},{24,28},{28,24},{1,5},{5... | collective-permute-start | bytes 310472 | tf_op jit(solution)/shard_map/ppermute | solution.py:600
  398.6 14.1 %collective-permute-start.28 = (bf16[96,3072]{1,0:T(8,128)(2,1)}, bf16[96,3072]{1,0:T(8,128)(2,1)}, u32[]{:S(2)}, u32[]{:S(2)}) collective-permute-start(bf16[96,3072]{1,0:T(8,128)(2,1)} %bitcast.87), channel_id=1, source_target_pairs={{0,4},{4,0},{8,12},{12,8},{16,20},{20,16},{24,28},{28,24},{1,5},{5... | collective-permute-start | bytes 1769480 | tf_op jit(solution)/shard_map/ppermute | solution.py:600
  401.1 9.3 %collective-permute-start.31 = (f32[32,128]{1,0:T(8,128)S(1)}, f32[32,128]{1,0:T(8,128)S(1)}, u32[]{:S(2)}, u32[]{:S(2)}) collective-permute-start(f32[32,128]{1,0:T(8,128)S(1)} %fusion.18), channel_id=1, source_target_pairs={{0,3},{1,2},{2,1},{3,0},{4,7},{5,6},{6,5},{7,4},{8,11},{9,10},{10,... | collective-permute-start | bytes 49160 | tf_op jit(solution)/shard_map/ppermute | solution.py:600
  401.1 9.2 %collective-permute-start.30 = (f32[32,128]{1,0:T(8,128)S(1)}, f32[32,128]{1,0:T(8,128)S(1)}, u32[]{:S(2)}, u32[]{:S(2)}) collective-permute-start(f32[32,128]{1,0:T(8,128)S(1)} %fusion.18), channel_id=1, source_target_pairs={{0,2},{1,3},{2,0},{3,1},{4,6},{5,7},{6,4},{7,5},{8,10},{9,11},{10,... | collective-permute-start | bytes 49160 | tf_op jit(solution)/shard_map/ppermute | solution.py:600
  401.6 8.8 %collective-permute-start.29 = (f32[32,128]{1,0:T(8,128)S(1)}, f32[32,128]{1,0:T(8,128)S(1)}, u32[]{:S(2)}, u32[]{:S(2)}) collective-permute-start(f32[32,128]{1,0:T(8,128)S(1)} %fusion.18), channel_id=1, source_target_pairs={{0,1},{1,0},{2,3},{3,2},{4,5},{5,4},{6,7},{7,6},{8,9},{9,8},{10,11... | collective-permute-start | bytes 49160 | tf_op jit(solution)/shard_map/ppermute | solution.py:600
  (17 other events, 45.6 us)
Sparse Core Ops, SparseCore 0:
  28.4 94.3 all-gather.2
  152.7 63.2 reduce-scatter.2
  218.7 48.1 reduce-scatter.4
